TPU v7x, 32 devices: a whole 2x2x4 slice. The times are simulated.
32 devices in a mesh: dp: 8 (over y, x, core), tensor: 4 (over z).
Axes of the slice: x: 2, y: 2, z: 4, core: 2. Of those that a mesh axis runs over, the one named last changes fastest.
Arguments:
- tokens: bfloat16 [16384, 768], P(('dp', 'tensor')), may hold values from -6 to 6
- cotangent: bfloat16 [16384, 768], P(('dp', 'tensor')), may hold values from -6 to 6
- labels: int32 [8], P('dp'), may hold values from 0 to 13
- piece_start: int32 [8, 2], P('dp'), may hold values from 0 to 8, as said below
- piece_len: int32 [8, 2], P('dp'), may hold values from 0 to 4, as said below
- w_qkv: bfloat16 [768, 3, 768], P('dp', None, 'tensor'), may hold values from -0.21875 to 0.21875
- w_out: bfloat16 [768, 768], P('tensor', 'dp'), may hold values from -6 to 6
- w_up: bfloat16 [768, 3072], P('dp', 'tensor'), may hold values from -0.21875 to 0.21875
- w_down: bfloat16 [3072, 768], P('tensor', 'dp'), may hold values from -0.109375 to 0.109375
- vec_table: float32 [8, 768], replicated, may hold values from -1.2 to 1.4, as said below
- ff_bias: float32 [3072], replicated, may hold values from -1.8 to 1.8
- cls_proj: bfloat16 [768, 128], replicated, may hold values from -0.21875 to 0.21875
- cls_vec: float32 [3, 128], replicated, may hold values from -4 to 4
- cls_hidden: bfloat16 [128, 128], replicated, may hold values from -6 to 6
- cls_out: bfloat16 [128, 14], replicated, may hold values from -1.796875 to 1.796875
- cls_bias: float32 [14], replicated, may hold values from -3 to 3
Outputs:
- layer_out: bfloat16 [16384, 768], P(('dp', 'tensor'))
- logits: float32 [8, 14], P('dp')
- grad_tokens: float32 [16384, 768], P(('dp', 'tensor'))
- grad_w_qkv: float32 [768, 3, 768], P('dp', None, 'tensor')
- grad_w_out: float32 [768, 768], P('tensor', 'dp')
- grad_w_up: float32 [768, 3072], P('dp', 'tensor')
- grad_w_down: float32 [3072, 768], P('tensor', 'dp')
- grad_vec_table: float32 [8, 768], replicated
- grad_ff_bias: float32 [3072], replicated
- grad_cls_proj: float32 [768, 128], replicated
- grad_cls_vec: float32 [3, 128], replicated
- grad_cls_hidden: float32 [128, 128], replicated
- grad_cls_out: float32 [128, 14], replicated
- grad_cls_bias: float32 [14], replicated
Inputs may be any that keep to these rules, and one draw needn't show every extreme that they name: Blocks are counted in units of 256 tokens; piece_start[s, p] lies from p * 4 to (p + 1) * 4, and a piece with piece_len above 0 ends within that region. A picture piece covers piece_len whole blocks; 0 leaves the slot empty. `vec_table`: rows 3 and 6 are near 1, the others near 0.
All inputs are finite; a program needn't handle non-finite values.
Results may differ from a plain program's by a relative error of at most 0.017.
Values may be sent and summed in bfloat16 or wider, within the bound.
No kernel may reach another device: no remote copies, remote signals or barrier semaphores. Data moves between devices by JAX's collectives and lax.ppermute only.
A program may use at most 128 MiB of HBM per device.

v0:
```python
import jax
import jax.numpy as jnp
from jax import lax
from jax.sharding import PartitionSpec as P

HEAD_DIM = 64
FF = 3072
CH = 128
POOL_HEADS = 2
CLASSES = 14
PIECE_BLOCK = 256


NORM_EPS = 1e-05
MASK_FILL = -1e30
PRECISE = lax.Precision.HIGHEST


def joined_2(value, axis, join):
    pieces = jax.tree.map(lambda part: lax.all_gather(part, axis), value)
    head = jax.tree.map(lambda part: part[0], pieces)
    tail = jax.tree.map(lambda part: part[1:], pieces)
    subtotal, _ = lax.scan(lambda subtotal, share: (join(subtotal, share), None), head, tail)
    return subtotal


def layer_norm(values, gain_vec, shift_vec):
    centered = values - jnp.mean(values, axis=-1, keepdims=True)
    spread = jnp.mean(centered * centered, axis=-1, keepdims=True)
    return centered * lax.rsqrt(spread + NORM_EPS) * gain_vec + shift_vec


def gelu_exact(values):
    return jax.nn.gelu(values, approximate=False)


def piece_ids(starts, counts, length, block_tokens):
    blocks = jnp.arange(length, dtype=jnp.int32) // block_tokens
    inside = (blocks[:, None] >= starts[None, :]) & (
        blocks[:, None] < starts[None, :] + counts[None, :]
    )
    numbers = jnp.arange(1, starts.shape[0] + 1, dtype=jnp.int32)
    return jnp.sum(jnp.where(inside, numbers[None, :], 0), axis=1)


def allowed_mask(query_pos, query_ids, key_pos, key_ids):
    causal = key_pos[None, :] <= query_pos[:, None]
    same_piece = (key_ids[None, :] == query_ids[:, None]) & (query_ids[:, None] > 0)
    return causal | same_piece


def contract_rows(left_mat, right_mat):
    return lax.dot_general(
        left_mat, right_mat, (((0,), (0,)), ((), ())), preferred_element_type=jnp.float32
    )


def contract_cols(left_mat, right_mat):
    return lax.dot_general(
        left_mat, right_mat, (((1,), (1,)), ((), ())), preferred_element_type=jnp.float32
    )


def merge_pool(first_part, second_part):
    max_one, total_one, acc_one = first_part
    max_two, total_two, acc_two = second_part
    joint_max = jnp.maximum(max_one, max_two)
    scale_one = jnp.exp(max_one - joint_max)
    scale_two = jnp.exp(max_two - joint_max)
    return (
        joint_max,
        total_one * scale_one + total_two * scale_two,
        acc_one * scale_one[:, None] + acc_two * scale_two[:, None],
    )


def classifier_head(pooled, hidden_w, hidden_b, out_w, out_b):
    hidden_cls = jnp.tanh(jnp.dot(pooled[None, :], hidden_w, precision=PRECISE)[0] + hidden_b)
    return jnp.dot(hidden_cls[None, :], out_w, precision=PRECISE)[0] + out_b


def attend_forward(query_heads, key_heads, value_heads, seq_ids, block_size):
    length, heads_here, head_dim = query_heads.shape
    head_scale = head_dim ** (-0.5)
    positions = jnp.arange(length, dtype=jnp.int32)

    def one_block(block_index):
        begin_at = block_index * block_size
        q_block = lax.dynamic_slice_in_dim(query_heads, begin_at, block_size, 0)
        pos_block = lax.dynamic_slice_in_dim(positions, begin_at, block_size, 0)
        id_block = lax.dynamic_slice_in_dim(seq_ids, begin_at, block_size, 0)
        scores = (
            jnp.einsum("qhd,khd->hqk", q_block, key_heads, preferred_element_type=jnp.float32)
            * head_scale
        )
        allowed = allowed_mask(pos_block, id_block, positions, seq_ids)
        scores = jnp.where(allowed[None], scores, MASK_FILL)
        row_max = jnp.max(scores, axis=-1, keepdims=True)
        powers = jnp.exp(scores - row_max)
        row_total = jnp.sum(powers, axis=-1, keepdims=True)
        prob_block = (powers / row_total).astype(jnp.bfloat16)
        mixed_block = jnp.einsum(
            "hqk,khd->qhd", prob_block, value_heads, preferred_element_type=jnp.float32
        )
        log_total = (row_max + jnp.log(row_total))[:, :, 0]
        return (mixed_block, log_total)

    mixed_blocks, log_totals = lax.map(one_block, jnp.arange(length // block_size, dtype=jnp.int32))
    return (mixed_blocks.reshape(length, heads_here * head_dim), log_totals)


def attend_backward(
    query_heads, key_heads, value_heads, seq_ids, log_totals, grad_mixed, block_size
):
    length, heads_here, head_dim = query_heads.shape
    head_scale = head_dim ** (-0.5)
    positions = jnp.arange(length, dtype=jnp.int32)

    def one_block(carried, block_index):
        grad_keys, grad_values = carried
        begin_at = block_index * block_size
        q_block = lax.dynamic_slice_in_dim(query_heads, begin_at, block_size, 0)
        pos_block = lax.dynamic_slice_in_dim(positions, begin_at, block_size, 0)
        id_block = lax.dynamic_slice_in_dim(seq_ids, begin_at, block_size, 0)
        grad_block = lax.dynamic_slice_in_dim(grad_mixed, begin_at, block_size, 0)
        log_block = log_totals[block_index]
        scores = (
            jnp.einsum("qhd,khd->hqk", q_block, key_heads, preferred_element_type=jnp.float32)
            * head_scale
        )
        allowed = allowed_mask(pos_block, id_block, positions, seq_ids)
        prob_block = jnp.where(allowed[None], jnp.exp(scores - log_block[:, :, None]), 0.0)
        prob_low = prob_block.astype(jnp.bfloat16)
        grad_values = grad_values + jnp.einsum(
            "hqk,qhd->khd", prob_low, grad_block, preferred_element_type=jnp.float32
        )
        grad_probs = jnp.einsum(
            "qhd,khd->hqk", grad_block, value_heads, preferred_element_type=jnp.float32
        )
        row_dot = jnp.sum(prob_block * grad_probs, axis=-1, keepdims=True)
        grad_scores = (prob_block * (grad_probs - row_dot)).astype(jnp.bfloat16)
        grad_query = (
            jnp.einsum("hqk,khd->qhd", grad_scores, key_heads, preferred_element_type=jnp.float32)
            * head_scale
        )
        grad_keys = (
            grad_keys
            + jnp.einsum("hqk,qhd->khd", grad_scores, q_block, preferred_element_type=jnp.float32)
            * head_scale
        )
        return ((grad_keys, grad_values), grad_query)

    zero_heads = jnp.zeros((length, heads_here, head_dim), jnp.float32)
    (grad_keys, grad_values), grad_query = lax.scan(
        one_block, (zero_heads, zero_heads), jnp.arange(length // block_size, dtype=jnp.int32)
    )
    local_width = heads_here * head_dim
    return (
        grad_query.reshape(length, local_width),
        grad_keys.reshape(length, local_width),
        grad_values.reshape(length, local_width),
    )


def placed(piece_vec, full_len, begin_at):
    return lax.dynamic_update_slice_in_dim(
        jnp.zeros((full_len,), jnp.float32), piece_vec, begin_at, 0
    )


def per_device(
    tokens,
    cotangent,
    labels,
    piece_start,
    piece_len,
    w_qkv,
    w_out,
    w_up,
    w_down,
    vec_table,
    ff_bias,
    cls_proj,
    cls_vec,
    cls_hidden,
    cls_out,
    cls_bias,
):
    row_count, model_width = tokens.shape
    tensor_size = lax.axis_size("tensor")
    tensor_index = lax.axis_index("tensor")
    seq_len = row_count * tensor_size
    local_width = w_qkv.shape[2]
    local_ff = w_up.shape[1]
    heads_here = local_width // HEAD_DIM
    block_size = min(512, seq_len)
    pool_width = CH // POOL_HEADS
    pool_scale = pool_width ** (-0.5)
    qkv_full, out_full, up_full, down_full = (
        lax.all_gather(w_qkv, "dp", axis=0, tiled=True),
        lax.all_gather(w_out, "dp", axis=1, tiled=True),
        lax.all_gather(w_up, "dp", axis=0, tiled=True),
        lax.all_gather(w_down, "dp", axis=1, tiled=True),
    )
    joined = qkv_full.reshape(model_width, 3 * local_width)
    query_bias = lax.dynamic_slice_in_dim(vec_table[0], tensor_index * local_width, local_width, 0)
    value_bias = lax.dynamic_slice_in_dim(vec_table[1], tensor_index * local_width, local_width, 0)
    inner_bias = lax.dynamic_slice_in_dim(ff_bias, tensor_index * local_ff, local_ff, 0)
    seq_ids = piece_ids(piece_start[0], piece_len[0], seq_len, PIECE_BLOCK)
    gathered = lax.all_gather(tokens, "tensor", axis=0, tiled=True)
    proj_bias = jnp.concatenate([query_bias, jnp.zeros((local_width,), jnp.float32), value_bias])
    qkv_low = (jnp.dot(gathered, joined, preferred_element_type=jnp.float32) + proj_bias).astype(
        jnp.bfloat16
    )
    query_heads = qkv_low[:, :local_width].reshape(seq_len, heads_here, HEAD_DIM)
    key_heads = qkv_low[:, local_width : 2 * local_width].reshape(seq_len, heads_here, HEAD_DIM)
    value_heads = qkv_low[:, 2 * local_width :].reshape(seq_len, heads_here, HEAD_DIM)
    attn_mixed, log_totals = attend_forward(
        query_heads, key_heads, value_heads, seq_ids, block_size
    )
    mixed_low = attn_mixed.astype(jnp.bfloat16)
    attn_branch = lax.psum_scatter(
        jnp.dot(mixed_low, out_full, preferred_element_type=jnp.float32),
        "tensor",
        scatter_dimension=0,
        tiled=True,
    )
    h_one = tokens.astype(jnp.float32) + attn_branch + vec_table[2]
    x_one, norm_one_pull = jax.vjp(layer_norm, h_one, vec_table[3], vec_table[4])
    x_low = x_one.astype(jnp.bfloat16)
    x_gathered = lax.all_gather(x_low, "tensor", axis=0, tiled=True)
    ff_upper = jnp.dot(x_gathered, up_full, preferred_element_type=jnp.float32) + inner_bias
    act_value, gelu_pull = jax.vjp(gelu_exact, ff_upper)
    act_low = act_value.astype(jnp.bfloat16)
    ff_branch = lax.psum_scatter(
        jnp.dot(act_low, down_full, preferred_element_type=jnp.float32).astype(jnp.bfloat16),
        "tensor",
        scatter_dimension=0,
        tiled=True,
    ).astype(jnp.float32)
    h_two = x_one + ff_branch + vec_table[5]
    normed, norm_two_pull = jax.vjp(layer_norm, h_two, vec_table[6], vec_table[7])
    out_low = normed.astype(jnp.bfloat16)
    student = jnp.dot(out_low, cls_proj, preferred_element_type=jnp.float32) + cls_vec[0]
    split_heads = student.reshape(row_count, POOL_HEADS, pool_width)
    pool_query = cls_vec[1].reshape(POOL_HEADS, pool_width)
    pool_logit = jnp.einsum("rhd,hd->rh", split_heads, pool_query, precision=PRECISE) * pool_scale
    local_max = jnp.max(pool_logit, axis=0)
    local_weights = jnp.exp(pool_logit - local_max[None, :])
    local_total = jnp.sum(local_weights, axis=0)
    local_acc = jnp.einsum("rh,rhd->hd", local_weights, split_heads, precision=PRECISE)
    pool_max, pool_total, pool_acc = joined_2(
        (local_max, local_total, local_acc), "tensor", merge_pool
    )
    pooled_heads = pool_acc / pool_total[:, None]
    pooled = pooled_heads.reshape(CH)
    weight_rows = local_weights * jnp.exp(local_max - pool_max)[None, :] / pool_total[None, :]
    hidden_w = cls_hidden.astype(jnp.float32)
    out_w = cls_out.astype(jnp.float32)
    logit_row, head_pull = jax.vjp(classifier_head, pooled, hidden_w, cls_vec[2], out_w, cls_bias)
    class_powers = jnp.exp(logit_row - jnp.max(logit_row))
    class_probs = class_powers / jnp.sum(class_powers)
    label_hot = (jnp.arange(CLASSES, dtype=jnp.int32) == labels[0]).astype(jnp.float32)
    grad_pooled, grad_hidden_w, grad_hidden_b, grad_out_w, grad_out_b = head_pull(
        class_probs - label_hot
    )
    grad_heads = grad_pooled.reshape(POOL_HEADS, pool_width)
    grad_weight_rows = jnp.einsum("rhd,hd->rh", split_heads, grad_heads, precision=PRECISE)
    baseline = jnp.sum(grad_heads * pooled_heads, axis=1)
    grad_logit = weight_rows * (grad_weight_rows - baseline[None, :])
    grad_split = (
        weight_rows[:, :, None] * grad_heads[None]
        + grad_logit[:, :, None] * pool_query[None] * pool_scale
    )
    grad_query_pool = (
        jnp.einsum("rh,rhd->hd", grad_logit, split_heads, precision=PRECISE).reshape(CH)
        * pool_scale
    )
    grad_student = grad_split.reshape(row_count, CH)
    grad_student_bias = jnp.sum(grad_student, axis=0)
    grad_student_low = grad_student.astype(jnp.bfloat16)
    grad_cls_proj_part = contract_rows(out_low, grad_student_low)
    grad_normed = cotangent.astype(jnp.float32) + contract_cols(grad_student_low, cls_proj)
    grad_h_two, grad_gain_two, grad_shift_two = norm_two_pull(grad_normed)
    grad_ff_out_bias = jnp.sum(grad_h_two, axis=0)
    grad_two_low = grad_h_two.astype(jnp.bfloat16)
    ff_grad_gathered = lax.all_gather(grad_two_low, "tensor", axis=0, tiled=True)
    grad_down = contract_rows(act_low, ff_grad_gathered)
    grad_act = contract_cols(ff_grad_gathered, down_full)
    grad_upper = gelu_pull(grad_act)[0]
    grad_inner_bias = jnp.sum(grad_upper, axis=0)
    grad_upper_low = grad_upper.astype(jnp.bfloat16)
    grad_up = contract_rows(x_gathered, grad_upper_low)
    grad_x_one = grad_h_two + lax.psum_scatter(
        contract_cols(grad_upper_low, up_full), "tensor", scatter_dimension=0, tiled=True
    )
    grad_h_one, grad_gain_one, grad_shift_one = norm_one_pull(grad_x_one)
    grad_attn_bias = jnp.sum(grad_h_one, axis=0)
    grad_one_low = grad_h_one.astype(jnp.bfloat16)
    attn_grad_gathered = lax.all_gather(grad_one_low, "tensor", axis=0, tiled=True)
    grad_out = contract_rows(mixed_low, attn_grad_gathered)
    grad_mixed = (
        contract_cols(attn_grad_gathered, out_full)
        .astype(jnp.bfloat16)
        .reshape(seq_len, heads_here, HEAD_DIM)
    )
    grad_query, grad_keys, grad_values = attend_backward(
        query_heads, key_heads, value_heads, seq_ids, log_totals, grad_mixed, block_size
    )
    grad_qkv_low = jnp.concatenate([grad_query, grad_keys, grad_values], axis=1).astype(
        jnp.bfloat16
    )
    grad_qkv = contract_rows(gathered, grad_qkv_low).reshape(model_width, 3, local_width)
    grad_tokens = grad_h_one + lax.psum_scatter(
        contract_cols(grad_qkv_low, joined).astype(jnp.bfloat16),
        "tensor",
        scatter_dimension=0,
        tiled=True,
    ).astype(jnp.float32)
    grad_w_qkv, grad_w_out, grad_w_up, grad_w_down = (
        lax.psum_scatter(grad_qkv, "dp", scatter_dimension=0, tiled=True),
        lax.psum_scatter(grad_out, "dp", scatter_dimension=1, tiled=True),
        lax.psum_scatter(grad_up, "dp", scatter_dimension=0, tiled=True),
        lax.psum_scatter(grad_down, "dp", scatter_dimension=1, tiled=True),
    )
    offset_here = tensor_index * local_width
    grad_vec = jnp.stack(
        [
            placed(jnp.sum(grad_query, axis=0), model_width, offset_here),
            placed(jnp.sum(grad_values, axis=0), model_width, offset_here),
            grad_attn_bias,
            grad_gain_one,
            grad_shift_one,
            grad_ff_out_bias,
            grad_gain_two,
            grad_shift_two,
        ]
    )
    grad_inner = placed(grad_inner_bias, FF, tensor_index * local_ff)
    first_only = (tensor_index == 0).astype(jnp.float32)
    grad_cls_vec_part = jnp.stack([grad_student_bias, grad_query_pool, grad_hidden_b * first_only])
    small_sums = lax.psum(
        (
            grad_vec,
            grad_inner,
            grad_cls_proj_part,
            grad_cls_vec_part,
            grad_hidden_w * first_only,
            grad_out_w * first_only,
            grad_out_b * first_only,
        ),
        ("dp", "tensor"),
    )
    return (
        out_low,
        logit_row[None, :],
        grad_tokens,
        grad_w_qkv,
        grad_w_out,
        grad_w_up,
        grad_w_down,
        small_sums[0],
        small_sums[1],
        small_sums[2],
        small_sums[3],
        small_sums[4],
        small_sums[5],
        small_sums[6],
    )


def solution(mesh):
    return jax.shard_map(
        per_device,
        mesh=mesh,
        in_specs=(
            P(("dp", "tensor"), None),
            P(("dp", "tensor"), None),
            P("dp"),
            P("dp", None),
            P("dp", None),
            P("dp", None, "tensor"),
            P("tensor", "dp"),
            P("dp", "tensor"),
            P("tensor", "dp"),
            P(),
            P(),
            P(),
            P(),
            P(),
            P(),
            P(),
        ),
        out_specs=(
            P(("dp", "tensor"), None),
            P("dp", None),
            P(("dp", "tensor"), None),
            P("dp", None, "tensor"),
            P("tensor", "dp"),
            P("dp", "tensor"),
            P("tensor", "dp"),
            P(),
            P(),
            P(),
            P(),
            P(),
            P(),
            P(),
        ),
        check_vma=False,
    )
```

profile of v0, /device:TPU:0, one launch (start us, length us, event | category | flops | bytes accessed | tf_op | source)
XLA Modules:
  0.0 1135.1 jit_solution(3709606041264841756)
XLA Ops:
  10.8 14.6 %all_gather.43 = bf16[768,3,192]{2,1,0:T(4,128)(2,1)S(1)} all-gather(bf16[96,3,192]{2,1,0:T(4,128)(2,1)S(1)} %copy.43), channel_id=1, replica_groups=mesh['dp'=8,'tensor'=4] {'dp'}, dimensions={0}, use_global_device_ids=true | all-gather | bytes 995328 | tf_op jit(solution)/shard_map/all_gather | solution.py:200
  27.5 9.6 all_gather.44
  38.2 38.5 %all-gather.11.cloned.1.call-done = bf16[2048,768]{1,0:T(8,128)(2,1)} async-done(((bf16[512,768]{1,0:T(8,128)(2,1)}), bf16[2048,768]{1,0:T(8,128)(2,1)}) %all-gather.11.cloned.1.call-update) | async-done | bytes 3145744 | tf_op jit(solution)/shard_map/all_gather | solution.py:210
  81.0 89.0 %while.47 = (s32[]{:T(128)}, bf16[4,512,3,64]{1,3,2,0:T(8,128)(2,1)S(1)}, f32[4,3,512]{2,1,0:T(4,128)S(1)}, s32[2048]{0:T(1024)S(1)}, s32[4]{0:T(128)S(1)}, /*in...) while((s32[]{:T(128)}, ...), condition=%wide.region_4.5_spmd.clone.clone, body=%wide.region_1.4_spmd.clone.sunk.clone | while | flops 847248384 | bytes 44195004 | solution.py:108
  89.8 6.8 fusion.196
  112.0 6.8 fusion.196
  156.5 6.8 fusion.196
  175.9 108.7 %reduce-scatter.11.cloned.1.call-done = f32[512,768]{1,0:T(8,128)} async-done(((f32[2048,768]{1,0:T(8,128)}), f32[512,768]{1,0:T(8,128)}) %reduce-scatter.11.cloned.1.call-update) | async-done | bytes 1572880 | tf_op jit(solution)/shard_map/reduce_scatter | solution.py:222
  289.5 62.6 %all-gather.13.cloned.1.call-done = bf16[2048,768]{1,0:T(8,128)(2,1)} async-done(((bf16[512,768]{1,0:T(8,128)(2,1)}), bf16[2048,768]{1,0:T(8,128)(2,1)}) %all-gather.13.cloned.1.call-update) | async-done | bytes 3145744 | tf_op jit(solution)/shard_map/all_gather | solution.py:231
  352.0 18.9 %multiply_convert_fusion.1 = (bf16[2048,768]{1,0:T(8,128)(2,1)}, f32[2048,768]{1,0:T(8,128)}, f32[2048,768]{1,0:T(8,128)}) fusion(f32[768]{0:T(1024)S(1)} %dynamic_slice.59, bf16[2048,768]{1,0:T(8,128)(2,1)} %all-gather.13.cloned.1.call-done, bf16[768,768]{1,0:T(8,128)(2,1)} %all-gather.15.cloned.1.call-done), kind=kOutput, calls=%fused_computation.59 | convolution fusion | flops 2519728128 | bytes 20057088 | tf_op jit(solution)/shard_map/dot_general | solution.py:232
  385.0 58.3 %reduce-scatter.13.cloned.1.call-done = bf16[512,768]{1,0:T(8,128)(2,1)} async-done(((bf16[2048,768]{1,0:T(8,128)(2,1)}), bf16[512,768]{1,0:T(8,128)(2,1)}) %reduce-scatter.13.cloned.1.call-update) | async-done | bytes 786448 | tf_op jit(solution)/shard_map/reduce_scatter | solution.py:235
  448.9 9.6 all-gather.3
  458.8 8.8 all-reduce.4
  482.9 63.2 %all-gather.19.cloned.1.call-done = bf16[2048,768]{1,0:T(8,128)(2,1)} async-done(((bf16[512,768]{1,0:T(8,128)(2,1)}), bf16[2048,768]{1,0:T(8,128)(2,1)}) %all-gather.19.cloned.1.call-update) | async-done | bytes 3145744 | tf_op jit(solution)/shard_map/all_gather | solution.py:287
  546.0 11.2 fusion.87
  563.5 109.5 %reduce-scatter.15.cloned.1.call-done = f32[512,768]{1,0:T(8,128)} async-done(((f32[2048,768]{1,0:T(8,128)}), f32[512,768]{1,0:T(8,128)}) %reduce-scatter.15.cloned.1.call-update) | async-done | bytes 1572880 | tf_op jit(solution)/shard_map/reduce_scatter | solution.py:294
  680.0 63.9 %all-gather.21.cloned.1.call-done = bf16[2048,768]{1,0:T(8,128)(2,1)} async-done(((bf16[512,768]{1,0:T(8,128)(2,1)}), bf16[2048,768]{1,0:T(8,128)(2,1)}) %all-gather.21.cloned.1.call-update) | async-done | bytes 3145744 | tf_op jit(solution)/shard_map/all_gather | solution.py:300
  747.0 135.7 %while.48 = (s32[]{:T(128)}, f32[2048,3,64]{0,2,1:T(8,128)}, f32[2048,3,64]{0,2,1:T(8,128)}, f32[4,512,3,64]{1,3,2,0:T(8,128)}, s32[4]{0:T(128)S(1)}, /*index=5*...) while((s32[]{:T(128)}, f32[2048,3,64]{0,2,1:T(8,128)}, ...), condition=%wide.region_25.26_spmd.clone.clone.clone, body=%wide.region_23.25_spmd.clone.clone.sunk.clone | while | flops 2066709504 | bytes 169289264 | solution.py:154
  897.9 6.9 fusion.48
  904.9 7.2 fusion.103
  922.7 45.0 %all-reduce.2 = (f32[8,768]{1,0:T(8,128)}, f32[3072]{0:T(1024)}, f32[3,128]{1,0:T(4,128)}, f32[128,14]{0,1:T(8,128)}, f32[14]{0:T(128)}) all-reduce(f32[8,768]{1,0:T(8,128)S(1)} %stack.34, f32[3072]{0:T(1024)S(1)} %dynamic_update_slice.24, f32[3,128]{1,0:T(4,128)S(1)} %pad_maximum_fusion.4, ...), channel_id=1, replica_groups=mesh['dp'=8,'tensor'=4] {'dp','tensor'}, use_global_device_ids=true, to_apply=%region_39.40 | all-reduce | flops 11406 | bytes 91248 | tf_op jit(solution)/shard_map/psum | solution.py:342
  969.3 15.5 %reduce-scatter.17.cloned.1.call-done = bf16[512,768]{1,0:T(8,128)(2,1)} async-done(((bf16[2048,768]{1,0:T(8,128)(2,1)}), bf16[512,768]{1,0:T(8,128)(2,1)}) %reduce-scatter.17.cloned.1.call-update) | async-done | bytes 786448 | tf_op jit(solution)/shard_map/reduce_scatter | solution.py:314
  987.4 85.1 %all-reduce.7.cloned.1.call-done = (f32[768,128]{1,0:T(8,128)}, f32[128,128]{1,0:T(8,128)}) async-done(((f32[768,128]{1,0:T(8,128)}, f32[128,128]{1,0:T(8,128)}), (f32[768,128]{1,0:T(8,128)}, f32[128,128]{1,0:T(8,128)})) %all-reduce.7.cloned.1.call-update) | async-done | bytes 458768 | tf_op jit(solution)/shard_map/psum | solution.py:342
  1077.9 46.1 %reduce-scatter.19.cloned.1.call-done = f32[96,3,192]{2,0,1:T(8,128)} async-done(((f32[768,3,192]{2,0,1:T(8,128)}), f32[96,3,192]{2,0,1:T(8,128)}) %reduce-scatter.19.cloned.1.call-update) | async-done | bytes 221200 | tf_op jit(solution)/shard_map/reduce_scatter | solution.py:321
  (445 shorter events, 299.3 us)
Async XLA Ops:
  8.0 439.4 %copy-start = (bf16[768,128]{1,0:T(8,128)(2,1)S(1)}, bf16[768,128]{1,0:T(8,128)(2,1)}, u32[]{:S(2)}) copy-start(bf16[768,128]{1,0:T(8,128)(2,1)} %param.33) | copy-start | bytes 589828
  8.1 68.6 %all-gather.11.cloned.1.call-start = ((), (), s32[]{:S(2)}) async-start(), calls=%async_computation.8 | async-start | bytes 3932160 | tf_op jit(solution)/shard_map/all_gather | solution.py:210
  8.8 275.8 %reduce-scatter.11.cloned.1.call-start = ((), (), s32[]{:S(2)}) async-start(), calls=%async_computation.9 | async-start | bytes 7864320 | tf_op jit(solution)/shard_map/reduce_scatter | solution.py:222
  175.0 111.8 %copy-start.32 = (f32[768]{0:T(1024)S(1)}, f32[768]{0:T(1024)}, u32[]{:S(2)}) copy-start(f32[768]{0:T(1024)} %get-tuple-element.391) | copy-start | bytes 9220
  175.1 111.8 %copy-start.36 = (f32[768]{0:T(1024)S(1)}, f32[768]{0:T(1024)}, u32[]{:S(2)}) copy-start(f32[768]{0:T(1024)} %get-tuple-element.392) | copy-start | bytes 9220
  175.1 114.4 %all-gather.15.cloned.1.call-start = ((), (), s32[]{:S(2)}) async-start(), calls=%async_computation.11 | async-start | bytes 1327104 | tf_op jit(solution)/shard_map/all_gather | solution.py:202
  175.6 176.4 %all-gather.13.cloned.1.call-start = ((), (), s32[]{:S(2)}) async-start(), calls=%async_computation.10 | async-start | bytes 3932160 | tf_op jit(solution)/shard_map/all_gather | solution.py:231
  288.0 88.3 %all-gather.17.cloned.1.call-start = ((), (), s32[]{:S(2)}) async-start(), calls=%async_computation.12 | async-start | bytes 1327104 | tf_op jit(solution)/shard_map/all_gather | solution.py:203
  288.6 154.7 %reduce-scatter.13.cloned.1.call-start = ((), (), s32[]{:S(2)}) async-start(), calls=%async_computation.13 | async-start | bytes 3932160 | tf_op jit(solution)/shard_map/reduce_scatter | solution.py:235
  383.0 163.1 %all-gather.19.cloned.1.call-start = ((), (), s32[]{:S(2)}) async-start(), calls=%async_computation.14 | async-start | bytes 3932160 | tf_op jit(solution)/shard_map/all_gather | solution.py:287
  383.7 91.8 %copy-start.57 = (f32[128]{0:T(128)}, f32[128]{0:T(128)S(1)}, u32[]{:S(2)}) copy-start(f32[128]{0:T(128)S(1)} %get-tuple-element.395) | copy-start | bytes 1540
  482.8 190.2 %reduce-scatter.15.cloned.1.call-start = ((), (), s32[]{:S(2)}) async-start(), calls=%async_computation.15 | async-start | bytes 7864320 | tf_op jit(solution)/shard_map/reduce_scatter | solution.py:294
  563.5 180.4 %all-gather.21.cloned.1.call-start = ((), (), s32[]{:S(2)}) async-start(), calls=%async_computation.16 | async-start | bytes 3932160 | tf_op jit(solution)/shard_map/all_gather | solution.py:300
  677.0 66.9 %copy-start.25 = (bf16[192,768]{0,1:T(8,128)(2,1)S(1)}, bf16[192,768]{0,1:T(8,128)(2,1)}, u32[]{:S(2)}) copy-start(bf16[192,768]{0,1:T(8,128)(2,1)} %all_gather.44) | copy-start | bytes 884740
  677.0 69.9 %copy-start.41 = (f32[512]{0:T(512)}, f32[512]{0:T(512)S(1)}, u32[]{:S(2)}) copy-start(f32[512]{0:T(512)S(1)} %negate_multiply_fusion.1) | copy-start | bytes 6148
  679.9 287.8 %reduce-scatter.25.cloned.1.call-start = ((), (), s32[]{:S(2)}) async-start(), calls=%async_computation.21 | async-start | bytes 884736
  887.2 97.6 %reduce-scatter.17.cloned.1.call-start = ((), (), s32[]{:S(2)}) async-start(), calls=%async_computation.17 | async-start | bytes 3932160 | tf_op jit(solution)/shard_map/reduce_scatter | solution.py:314
  895.2 177.2 %all-reduce.7.cloned.1.call-start = ((), (), s32[]{:S(2)}) async-start(), calls=%async_computation.22 | async-start | bytes 917504 | tf_op jit(solution)/shard_map/psum | solution.py:342
  897.8 174.6 %reduce-scatter.21.cloned.1.call-start = ((), (), s32[]{:S(2)}) async-start(), calls=%async_computation.19 | async-start | bytes 2654208 | tf_op jit(solution)/shard_map/reduce_scatter | solution.py:323
  904.9 173.1 %reduce-scatter.23.cloned.1.call-start = ((), (), s32[]{:S(2)}) async-start(), calls=%async_computation.20 | async-start | bytes 2654208 | tf_op jit(solution)/shard_map/reduce_scatter | solution.py:324
  912.1 212.0 %reduce-scatter.19.cloned.1.call-start = ((), (), s32[]{:S(2)}) async-start(), calls=%async_computation.18 | async-start | bytes 2654208 | tf_op jit(solution)/shard_map/reduce_scatter | solution.py:321
  917.4 67.5 %copy-start.13 = (f32[512,768]{1,0:T(8,128)S(1)}, f32[512,768]{1,0:T(8,128)}, u32[]{:S(2)}) copy-start(f32[512,768]{1,0:T(8,128)} %copy-done.12) | copy-start | bytes 4718596
  917.4 67.4 %copy-start.42 = (f32[512]{0:T(512)S(1)}, f32[512]{0:T(512)}, u32[]{:S(2)}) copy-start(f32[512]{0:T(512)} %copy-done.41) | copy-start | bytes 6148
  920.9 206.4 %copy-start.1 = (bf16[768,128]{1,0:T(8,128)(2,1)S(1)}, bf16[768,128]{1,0:T(8,128)(2,1)}, u32[]{:S(2)}) copy-start(bf16[768,128]{1,0:T(8,128)(2,1)} %param.33) | copy-start | bytes 589828
  (95 other events, 712.4 us)
Sparse Core Ops, SparseCore 0:
  10.5 66.1 all-gather.10
  175.2 109.3 reduce-scatter.10
  563.6 109.3 reduce-scatter.14
  902.5 169.8 all-reduce.6
Sparse Core Ops, SparseCore 1:
  177.4 22.5 all-gather.14
  288.1 63.9 all-gather.12
  353.8 22.5 all-gather.16
  383.0 60.3 reduce-scatter.12
  482.9 63.1 all-gather.18
  680.0 63.8 all-gather.20
  887.3 33.7 reduce-scatter.24
  923.3 61.5 reduce-scatter.16
  988.7 42.3 reduce-scatter.20
  1035.4 42.5 reduce-scatter.22
  1081.7 42.3 reduce-scatter.18
where the time goes:
time: 1140 us
  waiting for transfers between devices  664 us (58%)
  matrix products  224 us (20%)
  blocking collectives  87.6 us (8%)
  other arithmetic  82.1 us (7%)
  local copies, waits for them, and re-layouts  44 us (4%)
  between operations  18.3 us (2%)
  loops' own time  14.4 us (1%)
    reduce_scatter x1, waiting for transfers between devices, per_device(): lax.psum_scatter(contract_cols(grad_upper_low, up_full), 'tensor', scatte...  110 us
    reduce_scatter x1, waiting for transfers between devices, per_device(): lax.psum_scatter(jnp.dot(mixed_low, out_full, preferred_element_type=jnp....  109 us
    psum x1, waiting for transfers between devices, per_device(): lax.psum((grad_vec, grad_inner, grad_cls_proj_part, grad_cls_vec_part, gr...  85.1 us
    all_gather x1, waiting for transfers between devices, per_device(): lax.all_gather(grad_one_low, 'tensor', axis=0, tiled=True)  63.9 us
    all_gather x1, waiting for transfers between devices, per_device(): lax.all_gather(grad_two_low, 'tensor', axis=0, tiled=True)  63.2 us
    all_gather x1, waiting for transfers between devices, per_device(): x_gathered = lax.all_gather(x_low, 'tensor', axis=0, tiled=True)  62.6 us
    reduce_scatter x1, waiting for transfers between devices, per_device(): lax.psum_scatter(jnp.dot(act_low, down_full, preferred_element_type=jnp.f...  58.3 us
    reduce_scatter x1, waiting for transfers between devices, per_device(): lax.psum_scatter(grad_qkv, 'dp', scatter_dimension=0, tiled=True)  46.1 us
  transfers between devices with their start and end apart: 15, of which 12 were waited for; matrix products, arithmetic and copies ran while one was open for 6% of the time, Pallas kernels for 0%

commit v1 on v0

v1 whole, which is shorter than its diff:
```python
import functools

import jax
import jax.numpy as jnp
from jax import lax
from jax.experimental import pallas as pl
from jax.experimental.pallas import tpu as pltpu
from jax.sharding import PartitionSpec as P

HEAD_DIM = 64
CLASSES = 14
PIECE_BLOCK = 256
POOL_HEADS = 2
LANES = 128
NORM_EPS = 1e-05
MASK_FILL = -1e30
PRECISE = lax.Precision.HIGHEST
F32 = jnp.float32
BF16 = jnp.bfloat16
VMEM_LIMIT = 48 * 1024 * 1024


def dot_nn(a, b, precision=None):
    return lax.dot_general(
        a, b, (((1,), (0,)), ((), ())), preferred_element_type=F32, precision=precision
    )


def dot_nt(a, b, precision=None):
    return lax.dot_general(
        a, b, (((1,), (1,)), ((), ())), preferred_element_type=F32, precision=precision
    )


def dot_tn(a, b, precision=None):
    return lax.dot_general(
        a, b, (((0,), (0,)), ((), ())), preferred_element_type=F32, precision=precision
    )


def shifted(value, axis, size, by):
    return lax.ppermute(value, axis, [(i, (i + by) % size) for i in range(size)])


def swapped(value, axis, size, bit):
    return lax.ppermute(value, axis, [(i, i ^ bit) for i in range(size)])


def bits_of(size):
    return [1 << n for n in range(size.bit_length() - 1)]


def summed(value, dp, tensor, axes=("dp", "tensor")):
    for axis, size in (("dp", dp), ("tensor", tensor)):
        if axis in axes:
            for bit in bits_of(size):
                value = value + swapped(value, axis, size, bit)
    return value


def summed_to_owner(parts, axis, size):
    index = lax.axis_index(axis)
    for bit in bits_of(size):
        mine = (index // bit) % 2
        pairs = parts.reshape(parts.shape[0] // 2, 2, *parts.shape[1:])
        keep = lax.dynamic_index_in_dim(pairs, mine, 1, keepdims=False)
        give = lax.dynamic_index_in_dim(pairs, 1 - mine, 1, keepdims=False)
        parts = keep + swapped(give.astype(BF16), axis, size, bit).astype(F32)
    return parts[0]


def gathered(value, axis, size):
    index = lax.axis_index(axis)
    for bit in bits_of(size):
        other = swapped(value, axis, size, bit)
        low = (index // bit) % 2 == 0
        value = jnp.where(
            low, jnp.concatenate([value, other], 0), jnp.concatenate([other, value], 0)
        )
    return value


def block_range(start_ref, len_ref, block):
    first, stop, inside_any = block, block + 1, jnp.int32(0)
    for piece in range(start_ref.shape[1]):
        begin, count = start_ref[0, piece], len_ref[0, piece]
        inside = jnp.logical_and(block >= begin, block < begin + count)
        first = jnp.where(inside, begin, first)
        stop = jnp.where(inside, begin + count, stop)
        inside_any = jnp.where(inside, jnp.int32(1), inside_any)
    return first, stop, inside_any


def head_lanes(shape, head):
    lane = lax.broadcasted_iota(jnp.int32, shape, len(shape) - 1)
    return (lane >= head * HEAD_DIM) & (lane < (head + 1) * HEAD_DIM)


def attend_forward_kernel(heads, z_ref, start_ref, len_ref, *refs):
    tensor = len(refs) - 2 - 3
    chunks = refs[:tensor]
    o_ref, lse_ref = refs[tensor : tensor + 2]
    q_s, k_s, vt_s = refs[tensor + 2 :]
    rows, padded = chunks[0].shape[0], chunks[0].shape[1] // 3
    blk = PIECE_BLOCK
    blocks = tensor * rows // blk
    per_chunk = rows // blk
    z = z_ref[0]
    scale = HEAD_DIM ** (-0.5)
    for t in range(tensor):
        quarter = lax.rem(z - t + tensor, tensor)
        for part in range(per_chunk):
            b = quarter * per_chunk + part
            here = pl.ds(part * blk, blk)
            q = chunks[t][here, 0:padded]
            for h in range(heads):
                q_s[h, b] = jnp.where(head_lanes(q.shape, h), q * scale, 0.0).astype(BF16)
            pair, at = b // 2, lax.rem(b, 2) * blk
            k_s[pair, pl.ds(at, blk), :] = chunks[t][here, padded : 2 * padded]
            vt = chunks[t][here, 2 * padded : 3 * padded].T
            for side in range(2):

                @pl.when(lax.rem(b, 2) == side)
                def _():
                    vt_s[pair, :, side * blk : (side + 1) * blk] = vt


    def one_query(i, carry):
        _, stop, inside = block_range(start_ref, len_ref, i)
        q_h = [q_s[h, i] for h in range(heads)]
        query = i * blk + lax.broadcasted_iota(jnp.int32, (1, blk), 1)
        limit = jnp.maximum(query, jnp.where(inside > 0, stop * blk - 1, 0))

        def step(j, state, masked):
            tops, totals, mixed = state
            out = ([], [], [])
            keys = 2 * blk
            if masked:
                key = j * keys + lax.broadcasted_iota(jnp.int32, (keys, blk), 0)
                seen = key <= limit
            for h in range(heads):
                s = dot_nt(k_s[j], q_h[h])
                if masked:
                    s = jnp.where(seen, s, MASK_FILL)
                top = jnp.maximum(tops[h], jnp.max(s, axis=0, keepdims=True))
                p = jnp.exp(s - top)
                fade = jnp.exp(tops[h] - top)
                vt = vt_s[j, h * HEAD_DIM : (h + 1) * HEAD_DIM, :]
                out[0].append(top)
                out[1].append(totals[h] * fade + jnp.sum(p, axis=0, keepdims=True))
                out[2].append(mixed[h] * fade + dot_nn(vt, p.astype(BF16)))
            return tuple(tuple(v) for v in out)

        state = (
            tuple(jnp.full((1, blk), MASK_FILL, F32) for _ in range(heads)),
            tuple(jnp.zeros((1, blk), F32) for _ in range(heads)),
            tuple(jnp.zeros((HEAD_DIM, blk), F32) for _ in range(heads)),
        )
        own = i // 2
        state = lax.fori_loop(0, own, lambda j, c: step(j, c, False), state)
        state = step(own, state, True)
        tops, totals, mixed = lax.fori_loop(
            own + 1, (stop + 1) // 2, lambda j, c: step(j, c, True), state
        )
        outs = [mixed[h] * (1.0 / totals[h]) for h in range(heads)]
        lses = [tops[h] + jnp.log(totals[h]) for h in range(heads)]
        t = lax.rem(z - i // per_chunk + tensor, tensor)
        here = pl.ds(lax.rem(i, per_chunk) * blk, blk)
        o_ref[t, here, :] = jnp.concatenate(outs, axis=0).T.astype(BF16)
        lse_ref[i] = jnp.concatenate(lses + [jnp.zeros((8 - heads, blk), F32)], axis=0)
        return carry

    lax.fori_loop(0, blocks, one_query, 0)


def attend_forward(z, starts, lens, chunks, heads):
    tensor = len(chunks)
    rows, width = chunks[0].shape
    padded = width // 3
    seq, blk = tensor * rows, PIECE_BLOCK
    blocks = seq // blk
    smem = pl.BlockSpec(memory_space=pltpu.SMEM)
    vmem = pl.BlockSpec(memory_space=pltpu.VMEM)
    pairs = blocks * (blocks + 1) // 2
    return pl.pallas_call(
        functools.partial(attend_forward_kernel, heads),
        out_shape=(
            jax.ShapeDtypeStruct((tensor, rows, heads * HEAD_DIM), BF16),
            jax.ShapeDtypeStruct((blocks, 8, blk), F32),
        ),
        in_specs=[smem] * 3 + [vmem] * tensor,
        out_specs=(vmem, vmem),
        scratch_shapes=[
            pltpu.VMEM((heads, blocks, blk, padded), BF16),
            pltpu.VMEM((blocks // 2, 2 * blk, padded), BF16),
            pltpu.VMEM((blocks // 2, padded, 2 * blk), BF16),
        ],
        compiler_params=pltpu.CompilerParams(vmem_limit_bytes=VMEM_LIMIT),
        cost_estimate=pl.CostEstimate(
            flops=pairs * heads * blk * blk * 4 * 256,
            bytes_accessed=4 * seq * width,
            transcendentals=pairs * heads * blk * blk,
        ),
        name="attend_forward",
    )(z, starts, lens, *chunks)


def attend_backward_kernel(heads, z_ref, start_ref, len_ref, *refs):
    tensor = (len(refs) - 2 - 2 - 9) // 2
    chunks, grads = refs[:tensor], refs[tensor : 2 * tensor]
    o_ref, lse_ref, dqkv_ref, bias_ref = refs[2 * tensor : 2 * tensor + 4]
    q_s, k_s, kt_s, v_s, g_s, delta_s, dqt_s, dk_s, dv_s = refs[2 * tensor + 4 :]
    rows, padded = chunks[0].shape[0], chunks[0].shape[1] // 3
    width = heads * HEAD_DIM
    blk = PIECE_BLOCK
    blocks = tensor * rows // blk
    per_chunk = rows // blk
    z = z_ref[0]
    scale = HEAD_DIM ** (-0.5)
    for t in range(tensor):
        quarter = lax.rem(z - t + tensor, tensor)
        for part in range(per_chunk):
            b = quarter * per_chunk + part
            here = pl.ds(part * blk, blk)
            q = chunks[t][here, 0:padded]
            g = grads[t][here, :]
            for h in range(heads):
                q_s[h, b] = jnp.where(head_lanes(q.shape, h), q * scale, 0.0).astype(BF16)
                g_s[h, b, :, 0:width] = jnp.where(head_lanes(g.shape, h), g, 0.0).astype(BF16)
                if padded > width:
                    g_s[h, b, :, width:padded] = jnp.zeros((blk, padded - width), BF16)
            k = chunks[t][here, padded : 2 * padded]
            pair, at = b // 2, lax.rem(b, 2) * blk
            k_s[pair, pl.ds(at, blk), :] = k
            v_s[pair, pl.ds(at, blk), :] = chunks[t][here, 2 * padded : 3 * padded]
            kt = k.T
            for side in range(2):

                @pl.when(lax.rem(b, 2) == side)
                def _():
                    kt_s[pair, :, side * blk : (side + 1) * blk] = kt

            prod = (g.astype(F32) * o_ref[t, here, :].astype(F32)).T
            sums = [
                jnp.sum(prod[h * HEAD_DIM : (h + 1) * HEAD_DIM, :], axis=0, keepdims=True)
                for h in range(heads)
            ]
            delta_s[b] = jnp.concatenate(sums + [jnp.zeros((8 - heads, blk), F32)], axis=0)
            dqt_s[b] = jnp.zeros((padded, blk), F32)
    bias_ref[...] = jnp.zeros_like(bias_ref)

    keys = 2 * blk

    def one_pair(j, carry):
        first, _, _ = block_range(start_ref, len_ref, 2 * j)
        also, _, _ = block_range(start_ref, len_ref, 2 * j + 1)
        dk_s[...] = jnp.zeros_like(dk_s)
        dv_s[...] = jnp.zeros_like(dv_s)

        def step(i, masked):
            lse, delta = lse_ref[i], delta_s[i]
            if masked:
                _, stop, inside = block_range(start_ref, len_ref, i)
                query = i * blk + lax.broadcasted_iota(jnp.int32, (1, blk), 1)
                limit = jnp.maximum(query, jnp.where(inside > 0, stop * blk - 1, 0))
                key = j * keys + lax.broadcasted_iota(jnp.int32, (keys, blk), 0)
                seen = key <= limit
            dv, dk = dv_s[...], dk_s[...]
            for h in range(heads):
                q_h, g_h = q_s[h, i], g_s[h, i]
                p = jnp.exp(dot_nt(k_s[j], q_h) - lse[h : h + 1, :])
                if masked:
                    p = jnp.where(seen, p, 0.0)
                ds = (p * (dot_nt(v_s[j], g_h) - delta[h : h + 1, :])).astype(BF16)
                dv = dv + dot_nn(p.astype(BF16), g_h)
                dk = dk + dot_nn(ds, q_h)
                lo, hi = h * HEAD_DIM, (h + 1) * HEAD_DIM
                dqt_s[i, lo:hi, :] = dqt_s[i, lo:hi, :] + dot_nn(kt_s[j, lo:hi, :], ds)
            dv_s[...] = dv
            dk_s[...] = dk

        def masked_step(i, c):
            step(i, True)
            return c

        def open_step(i, c):
            step(i, False)
            return c

        lax.fori_loop(jnp.minimum(first, also), 2 * j + 2, masked_step, 0)
        lax.fori_loop(2 * j + 2, blocks, open_step, 0)
        for part in range(2):
            b = 2 * j + part
            t = lax.rem(z - b // per_chunk + tensor, tensor)
            here = pl.ds(lax.rem(b, per_chunk) * blk, blk)
            own = slice(part * blk, (part + 1) * blk)
            dqkv_ref[t, here, padded : 2 * padded] = dk_s[own, :].astype(BF16)
            dqkv_ref[t, here, 2 * padded : 3 * padded] = dv_s[own, :].astype(BF16)
        bias_ref[1:2, :] = bias_ref[1:2, :] + jnp.sum(dv_s[...], axis=0, keepdims=True)
        return carry

    lax.fori_loop(0, blocks // 2, one_pair, 0)

    def one_query(i, carry):
        dq = dqt_s[i].T * scale
        quarter = i // per_chunk
        t = lax.rem(z - quarter + tensor, tensor)
        here = pl.ds(lax.rem(i, per_chunk) * blk, blk)
        dqkv_ref[t, here, 0:padded] = dq.astype(BF16)
        bias_ref[0:1, :] = bias_ref[0:1, :] + jnp.sum(dq, axis=0, keepdims=True)
        return carry

    lax.fori_loop(0, blocks, one_query, 0)


def attend_backward(z, starts, lens, chunks, grads, mixed, lse, heads):
    tensor = len(chunks)
    rows, width = chunks[0].shape
    padded = width // 3
    seq, blk = tensor * rows, PIECE_BLOCK
    blocks = seq // blk
    smem = pl.BlockSpec(memory_space=pltpu.SMEM)
    vmem = pl.BlockSpec(memory_space=pltpu.VMEM)
    pairs = blocks * (blocks + 1) // 2
    return pl.pallas_call(
        functools.partial(attend_backward_kernel, heads),
        out_shape=(
            jax.ShapeDtypeStruct((tensor, rows, width), BF16),
            jax.ShapeDtypeStruct((8, padded), F32),
        ),
        in_specs=[smem] * 3 + [vmem] * (2 * tensor + 2),
        out_specs=(vmem, vmem),
        scratch_shapes=[
            pltpu.VMEM((heads, blocks, blk, padded), BF16),
            pltpu.VMEM((blocks // 2, 2 * blk, padded), BF16),
            pltpu.VMEM((blocks // 2, padded, 2 * blk), BF16),
            pltpu.VMEM((blocks // 2, 2 * blk, padded), BF16),
            pltpu.VMEM((heads, blocks, blk, padded), BF16),
            pltpu.VMEM((blocks, 8, blk), F32),
            pltpu.VMEM((blocks, padded, blk), F32),
            pltpu.VMEM((2 * blk, padded), F32),
            pltpu.VMEM((2 * blk, padded), F32),
        ],
        compiler_params=pltpu.CompilerParams(vmem_limit_bytes=VMEM_LIMIT),
        cost_estimate=pl.CostEstimate(
            flops=pairs * heads * blk * blk * 10 * 256,
            bytes_accessed=6 * seq * width,
            transcendentals=pairs * heads * blk * blk,
        ),
        name="attend_backward",
    )(z, starts, lens, *chunks, *grads, mixed, lse)


def weight_slots(tensor, dp, shard):
    if shard % 16:
        return [(0, t, t, None) for t in range(tensor)]
    bits = bits_of(dp)
    slots = []
    for side, order in enumerate((bits[1:], bits[1:][::-1])):
        offsets = [0]
        for bit in order:
            offsets = offsets + [o ^ bit for o in offsets]
        half = tensor // 2
        for n, offset in enumerate(offsets):
            for t in range(half):
                slots.append((2 * side, n * half + t, side * half + t, offset))
                slots.append((2 * side + 1, n * half + t, side * half + t, offset ^ bits[0]))
    return slots


def gathered_weights(part, dp, tensor, z):
    shard, columns = part.shape
    if shard % 16:
        whole = lax.all_gather(part, ("tensor", "dp"), axis=0, tiled=True)
        whole = whole.reshape(tensor, dp * shard, columns)
        order = (z - jnp.arange(tensor)) % tensor
        return [jnp.take(whole, order, axis=0)]
    ring = [part]
    for _ in range(tensor - 1):
        ring.append(shifted(ring[-1], "tensor", tensor, 1))
    bits = bits_of(dp)
    half = tensor // 2
    out = []
    for side, order in enumerate((bits[1:], bits[1:][::-1])):
        value = jnp.stack(ring[side * half : (side + 1) * half])
        for bit in order:
            value = jnp.concatenate([value, swapped(value, "dp", dp, bit)], axis=0)
        out += [value, swapped(value, "dp", dp, bits[0])]
    return out


def start_weights(slots, shard, place_ref, pieces, w_s, wo_s, sems, o_sem):
    wide = w_s.shape[2]
    for which, slot, t, offset in slots:
        if offset is None:
            here = slice(None)
        else:
            here = pl.ds(jnp.bitwise_xor(place_ref[1], offset) * shard, shard)
        pltpu.make_async_copy(
            pieces[which].at[slot, :, wide:], wo_s.at[t, here, :], o_sem
        ).start()
    for which, slot, t, offset in slots:
        if offset is None:
            here = slice(None)
        else:
            here = pl.ds(jnp.bitwise_xor(place_ref[1], offset) * shard, shard)
        pltpu.make_async_copy(
            pieces[which].at[slot, :, :wide], w_s.at[t, here, :], sems.at[t]
        ).start()


def center(values):
    mean = jnp.mean(values, axis=-1, keepdims=True)
    centered = values - mean
    spread = jnp.mean(centered * centered, axis=-1, keepdims=True)
    return centered, lax.rsqrt(spread + NORM_EPS)


def same_head(value):
    row = lax.broadcasted_iota(jnp.int32, (value, value), 0) // (value // POOL_HEADS)
    col = lax.broadcasted_iota(jnp.int32, (value, value), 1) // (value // POOL_HEADS)
    return (row == col).astype(F32)


def rows_forward_kernel(tensor, slots, shard, arrays, place_ref, *refs):
    mixed = refs[:tensor]
    tok_ref, vec_ref, bias_ref, proj_ref, cvec_ref = refs[tensor : tensor + 5]
    pieces = refs[tensor + 5 : tensor + 5 + arrays]
    (
        low_ref, xlow_ref, act_ref, slope_ref, xh1_ref, xh2_ref, rs_ref, stud_ref, mall_ref,
        e_ref, stats_ref, acc_s, w_s, wo_s, sems, o_sem,
    ) = refs[tensor + 5 + arrays :]
    j = pl.program_id(0)
    hidden = act_ref.shape[2]

    @pl.when(j == 0)
    def _():
        start_weights(slots, shard, place_ref, pieces, w_s, wo_s, sems, o_sem)
        total = tok_ref[...].astype(F32) + vec_ref[2:3, :]
        pltpu.make_async_copy(wo_s, wo_s, o_sem).wait()
        for s in range(tensor):
            piece = mixed[s][...]
            mall_ref[s] = piece
            total = total + dot_nt(piece, wo_s[s])
        centered, rstd = center(total)
        xhat = centered * rstd
        xh1_ref[...] = xhat
        rs_ref[:, 0:1] = rstd
        x_one = xhat * vec_ref[3:4, :] + vec_ref[4:5, :]
        xlow_ref[...] = x_one.astype(BF16)
        acc_s[...] = x_one + vec_ref[5:6, :]

    pltpu.make_async_copy(w_s.at[j], w_s.at[j], sems.at[j]).wait()
    upper = dot_nn(xlow_ref[...], w_s[j, :, 0:hidden]) + bias_ref[0]
    phi = 0.5 * (1.0 + lax.erf(upper * (0.5**0.5)))
    act = (upper * phi).astype(BF16)
    slope = phi + upper * (jnp.exp(-0.5 * upper * upper) * 0.3989422804014327)
    act_ref[0] = act
    slope_ref[0] = slope.astype(BF16)
    acc_s[...] = acc_s[...] + dot_nt(act, w_s[j, :, hidden:])

    @pl.when(j == pl.num_programs(0) - 1)
    def _():
        centered, rstd = center(acc_s[...])
        xhat = centered * rstd
        xh2_ref[...] = xhat
        rs_ref[:, 1:2] = rstd
        low = (xhat * vec_ref[6:7, :] + vec_ref[7:8, :]).astype(BF16)
        low_ref[...] = low
        student = dot_nn(low, proj_ref[...]) + cvec_ref[0:1, :]
        stud_ref[...] = student
        width = student.shape[1]
        scale = (width // POOL_HEADS) ** (-0.5)
        e = dot_nn(student * (cvec_ref[1:2, :] * scale), same_head(width), PRECISE)
        e_ref[...] = e
        top = jnp.max(e, axis=0, keepdims=True)
        w = jnp.exp(e - top)
        stats_ref[...] = jnp.concatenate(
            [
                top,
                jnp.sum(w, axis=0, keepdims=True),
                jnp.sum(w * student, axis=0, keepdims=True),
                jnp.zeros((5, width), F32),
            ],
            axis=0,
        )


def whole(*shape):
    return pl.BlockSpec(shape, lambda j, *_: (0,) * len(shape))


def block(*shape):
    return pl.BlockSpec((1,) + shape, lambda j, *_: (j,) + (0,) * len(shape))


def rows_forward(place, slots, pieces, mixed, tokens, vec_table, ff_bias, cls_proj, cls_vec):
    tensor = len(mixed)
    rows, width = tokens.shape
    head_width = mixed[0].shape[1]
    shard = pieces[0].shape[1]
    hidden = ff_bias.shape[2]
    ch = cls_proj.shape[1]
    far = pl.BlockSpec(memory_space=pl.ANY)

    def of_block(j, place_ref):
        return (lax.rem(place_ref[0] - j + tensor, tensor), 0, 0)

    return pl.pallas_call(
        functools.partial(rows_forward_kernel, tensor, slots, shard, len(pieces)),
        grid_spec=pltpu.PrefetchScalarGridSpec(
            num_scalar_prefetch=1,
            grid=(tensor,),
            in_specs=[whole(rows, head_width)] * tensor
            + [
                whole(rows, width),
                whole(8, width),
                pl.BlockSpec((1, 1, hidden), of_block),
                whole(width, ch),
                whole(3, ch),
            ]
            + [far] * len(pieces),
            out_specs=(
                whole(rows, width),
                whole(rows, width),
                block(rows, hidden),
                block(rows, hidden),
                whole(rows, width),
                whole(rows, width),
                whole(rows, 2),
                whole(rows, ch),
                whole(tensor, rows, head_width),
                whole(rows, ch),
                whole(8, ch),
            ),
            scratch_shapes=[
                pltpu.VMEM((rows, width), F32),
                pltpu.VMEM((tensor, width, 2 * hidden), BF16),
                pltpu.VMEM((tensor, width, head_width), BF16),
                pltpu.SemaphoreType.DMA((tensor,)),
                pltpu.SemaphoreType.DMA,
            ],
        ),
        out_shape=(
            jax.ShapeDtypeStruct((rows, width), BF16),
            jax.ShapeDtypeStruct((rows, width), BF16),
            jax.ShapeDtypeStruct((tensor, rows, hidden), BF16),
            jax.ShapeDtypeStruct((tensor, rows, hidden), BF16),
            jax.ShapeDtypeStruct((rows, width), F32),
            jax.ShapeDtypeStruct((rows, width), F32),
            jax.ShapeDtypeStruct((rows, 2), F32),
            jax.ShapeDtypeStruct((rows, ch), F32),
            jax.ShapeDtypeStruct((tensor, rows, head_width), BF16),
            jax.ShapeDtypeStruct((rows, ch), F32),
            jax.ShapeDtypeStruct((8, ch), F32),
        ),
        compiler_params=pltpu.CompilerParams(vmem_limit_bytes=VMEM_LIMIT),
        cost_estimate=pl.CostEstimate(
            flops=4 * rows * width * hidden * tensor + 2 * rows * width * width,
            bytes_accessed=4 * width * hidden * tensor + 20 * rows * width,
            transcendentals=2 * rows * hidden * tensor,
        ),
        name="rows_forward",
    )(place, *mixed, tokens, vec_table, ff_bias, cls_proj, cls_vec, *pieces)


def norm_back(grad, xhat, rstd, gain):
    g = grad * gain
    return (
        g - jnp.mean(g, axis=-1, keepdims=True) - xhat * jnp.mean(g * xhat, axis=-1, keepdims=True)
    ) * rstd


def rows_backward_kernel(tensor, slots, shard, arrays, place_ref, *refs):
    stats_refs = refs[:tensor]
    (
        stud_ref, e_ref, cot_ref, xh1_ref, xh2_ref, rs_ref, slope_ref, vec_ref, proj_ref,
        cvec_ref, chid_ref, cout_ref, cbias_ref,
    ) = refs[tensor : tensor + 13]
    pieces = refs[tensor + 13 : tensor + 13 + arrays]
    (
        logit_ref, two_ref, gu_ref, one_ref, gh1_ref, gm_ref, sums_ref, ffb_ref, gsl_ref,
        small_ref, ghid_ref, gout_ref, acc_s, w_s, wo_s, sems, o_sem,
    ) = refs[tensor + 13 + arrays :]
    j = pl.program_id(0)
    ch = stud_ref.shape[1]
    hidden = gu_ref.shape[2]
    scale = (ch // POOL_HEADS) ** (-0.5)

    @pl.when(j == 0)
    def _():
        start_weights(slots, shard, place_ref, pieces, w_s, wo_s, sems, o_sem)
        head_of = same_head(ch)
        first = (place_ref[0] == 0).astype(F32)
        stats = [r[...] for r in stats_refs]
        top = functools.reduce(jnp.maximum, [v[0:1, :] for v in stats])
        weights = [jnp.exp(v[0:1, :] - top) for v in stats]
        total = sum(v[1:2, :] * w for v, w in zip(stats, weights))
        pooled = sum(v[2:3, :] * w for v, w in zip(stats, weights)) / total

        first_row = lax.broadcasted_iota(jnp.int32, (8, ch), 0) == 0
        lane = lax.broadcasted_iota(jnp.int32, (8, ch), 1)
        pooled8 = jnp.broadcast_to(pooled, (8, ch))
        chid = chid_ref[...].astype(F32)
        cout = cout_ref[...].astype(F32)
        hid = jnp.tanh(dot_nn(pooled8, chid, PRECISE) + cvec_ref[2:3, :])
        logits = dot_nn(hid, cout, PRECISE) + cbias_ref[...]
        logit_ref[...] = logits
        real = lane < CLASSES
        masked = jnp.where(real, logits, MASK_FILL)
        powers = jnp.where(real, jnp.exp(masked - jnp.max(masked, axis=1, keepdims=True)), 0.0)
        probs = powers / jnp.sum(powers, axis=1, keepdims=True)
        grad_logits = probs - (lane == place_ref[2]).astype(F32)
        grad_pre = (1.0 - hid * hid) * dot_nt(grad_logits, cout, PRECISE)
        grad_pooled = dot_nt(grad_pre, chid, PRECISE)
        gl_row = jnp.where(first_row, grad_logits, 0.0) * first
        gp_row = jnp.where(first_row, grad_pre, 0.0) * first
        gout_ref[...] = dot_tn(hid, gl_row, PRECISE)
        ghid_ref[...] = dot_tn(pooled8, gp_row, PRECISE)
        base = dot_nn(grad_pooled * pooled8, head_of, PRECISE)[0:1, :]
        gp = grad_pooled[0:1, :]
        query = cvec_ref[1:2, :] * scale
        student = stud_ref[...]
        w = jnp.exp(e_ref[...] - top) / total
        grad_w = dot_nn(student * gp, head_of, PRECISE)
        grad_e = w * (grad_w - base)
        grad_student = w * gp + grad_e * query
        gsl = grad_student.astype(BF16)
        gsl_ref[...] = gsl
        small_ref[...] = jnp.concatenate(
            [
                jnp.sum(grad_student, axis=0, keepdims=True),
                jnp.sum(grad_e * student, axis=0, keepdims=True) * scale,
                gp_row[0:1, :],
                gl_row[0:1, :],
                jnp.zeros((4, ch), F32),
            ],
            axis=0,
        )
        grad = cot_ref[...].astype(F32) + dot_nt(gsl, proj_ref[...])
        xhat = xh2_ref[...]
        sums_ref[...] = jnp.zeros_like(sums_ref)
        sums_ref[6:7, :] = jnp.sum(grad * xhat, axis=0, keepdims=True)
        sums_ref[7:8, :] = jnp.sum(grad, axis=0, keepdims=True)
        two = norm_back(grad, xhat, rs_ref[:, 1:2], vec_ref[6:7, :])
        sums_ref[5:6, :] = jnp.sum(two, axis=0, keepdims=True)
        acc_s[...] = two
        two_ref[...] = two.astype(BF16)

    pltpu.make_async_copy(w_s.at[j], w_s.at[j], sems.at[j]).wait()
    upper = dot_nn(two_ref[...], w_s[j, :, hidden:]) * slope_ref[0].astype(F32)
    ffb_ref[0] = jnp.sum(upper, axis=0, keepdims=True)
    low = upper.astype(BF16)
    gu_ref[0] = low
    acc_s[...] = acc_s[...] + dot_nt(low, w_s[j, :, 0:hidden])

    @pl.when(j == pl.num_programs(0) - 1)
    def _():
        grad = acc_s[...]
        xhat = xh1_ref[...]
        sums_ref[3:4, :] = jnp.sum(grad * xhat, axis=0, keepdims=True)
        sums_ref[4:5, :] = jnp.sum(grad, axis=0, keepdims=True)
        one = norm_back(grad, xhat, rs_ref[:, 0:1], vec_ref[3:4, :])
        sums_ref[2:3, :] = jnp.sum(one, axis=0, keepdims=True)
        gh1_ref[...] = one
        low = one.astype(BF16)
        one_ref[...] = low
        pltpu.make_async_copy(wo_s, wo_s, o_sem).wait()
        for s in range(tensor):
            gm_ref[s] = dot_nn(low, wo_s[s]).astype(BF16)


def rows_backward(
    place, slots, pieces, stats, kept, cotangent, vec_table, cls_proj, cls_vec, cls_hidden,
    cls_out, cls_bias,
):
    _, _, _, slope, xh1, xh2, rs, student, mixed, pool_logit, _ = kept
    tensor, rows, hidden = slope.shape
    width = xh1.shape[1]
    head_width = mixed.shape[2]
    shard = pieces[0].shape[1]
    ch = student.shape[1]
    far = pl.BlockSpec(memory_space=pl.ANY)

    def of_block(j, place_ref):
        return (lax.rem(place_ref[0] - j + tensor, tensor), 0, 0)

    return pl.pallas_call(
        functools.partial(rows_backward_kernel, tensor, slots, shard, len(pieces)),
        grid_spec=pltpu.PrefetchScalarGridSpec(
            num_scalar_prefetch=1,
            grid=(tensor,),
            in_specs=[whole(8, ch)] * tensor
            + [
                whole(rows, ch),
                whole(rows, ch),
                whole(rows, width),
                whole(rows, width),
                whole(rows, width),
                whole(rows, 2),
                block(rows, hidden),
                whole(8, width),
                whole(width, ch),
                whole(3, ch),
                whole(ch, ch),
                whole(ch, ch),
                whole(1, ch),
            ]
            + [far] * len(pieces),
            out_specs=(
                whole(8, ch),
                whole(rows, width),
                block(rows, hidden),
                whole(rows, width),
                whole(rows, width),
                whole(tensor, rows, head_width),
                whole(8, width),
                pl.BlockSpec((1, 1, hidden), of_block),
                whole(rows, ch),
                whole(8, ch),
                whole(ch, ch),
                whole(ch, ch),
            ),
            scratch_shapes=[
                pltpu.VMEM((rows, width), F32),
                pltpu.VMEM((tensor, width, 2 * hidden), BF16),
                pltpu.VMEM((tensor, width, head_width), BF16),
                pltpu.SemaphoreType.DMA((tensor,)),
                pltpu.SemaphoreType.DMA,
            ],
        ),
        out_shape=(
            jax.ShapeDtypeStruct((8, ch), F32),
            jax.ShapeDtypeStruct((rows, width), BF16),
            jax.ShapeDtypeStruct((tensor, rows, hidden), BF16),
            jax.ShapeDtypeStruct((rows, width), BF16),
            jax.ShapeDtypeStruct((rows, width), F32),
            jax.ShapeDtypeStruct((tensor, rows, head_width), BF16),
            jax.ShapeDtypeStruct((8, width), F32),
            jax.ShapeDtypeStruct((tensor, 1, hidden), F32),
            jax.ShapeDtypeStruct((rows, ch), BF16),
            jax.ShapeDtypeStruct((8, ch), F32),
            jax.ShapeDtypeStruct((ch, ch), F32),
            jax.ShapeDtypeStruct((ch, ch), F32),
        ),
        compiler_params=pltpu.CompilerParams(vmem_limit_bytes=VMEM_LIMIT),
        cost_estimate=pl.CostEstimate(
            flops=4 * rows * width * hidden * tensor + 2 * rows * width * width,
            bytes_accessed=4 * width * hidden * tensor + 20 * rows * width,
            transcendentals=rows * ch,
        ),
        name="rows_backward",
    )(
        place, *stats, student, pool_logit, cotangent, xh1, xh2, rs, slope, vec_table, cls_proj,
        cls_vec, cls_hidden, cls_out, cls_bias, *pieces,
    )


def weight_grads_kernel(
    dp, shard, place_ref, x_ref, two_ref, one_ref, gu_ref, act_ref, mix_ref, low_ref, gsl_ref,
    *refs,
):
    outs, proj_ref = refs[:-4], refs[-4]
    lefts = refs[-3:]
    j = pl.program_id(0)
    hidden = gu_ref.shape[2]
    width = x_ref.shape[1]
    apart = len(outs) == 2

    @pl.when(j == 0)
    def _():
        for source, left in zip((x_ref, two_ref, one_ref), lefts):
            turned = source[...].T
            if not apart:
                left[...] = turned
                continue
            for b in range(dp):
                offset = jnp.bitwise_xor(place_ref[1], b)
                at = lax.rem(offset, 2) * (dp // 2) + offset // 2
                left[pl.ds(at * shard, shard), :] = turned[b * shard : (b + 1) * shard, :]
        proj_ref[...] = dot_tn(low_ref[...], gsl_ref[...])

    count = width // len(outs)
    rights = (gu_ref[0], act_ref[0], mix_ref[0])
    ends = (0, hidden, 2 * hidden, 2 * hidden + mix_ref.shape[2])
    for n, out in enumerate(outs):
        here = slice(n * count, (n + 1) * count)
        for m in range(3):
            part = dot_nn(lefts[m][here, :], rights[m]).astype(BF16)
            out[0, :, :, ends[m] : ends[m + 1]] = part.reshape(
                out.shape[1], out.shape[2], ends[m + 1] - ends[m]
            )


def weight_grads(
    place, dp, shard, x_low, two_low, one_low, upper_low, act, mixed, out_low, student_low
):
    tensor, rows, hidden = upper_low.shape
    width = x_low.shape[1]
    head_width = mixed.shape[2]
    ch = student_low.shape[1]
    total = 2 * hidden + head_width
    if shard % 16:
        parts = [(1, width)]
    else:
        parts = [(dp // 2, shard)] * 2
    return pl.pallas_call(
        functools.partial(weight_grads_kernel, dp, shard),
        grid_spec=pltpu.PrefetchScalarGridSpec(
            num_scalar_prefetch=1,
            grid=(tensor,),
            in_specs=[
                whole(rows, width),
                whole(rows, width),
                whole(rows, width),
                block(rows, hidden),
                block(rows, hidden),
                block(rows, head_width),
                whole(rows, width),
                whole(rows, ch),
            ],
            out_specs=tuple(block(*part, total) for part in parts) + (whole(width, ch),),
            scratch_shapes=[pltpu.VMEM((width, rows), BF16)] * 3,
        ),
        out_shape=tuple(jax.ShapeDtypeStruct((tensor, *part, total), BF16) for part in parts)
        + (jax.ShapeDtypeStruct((width, ch), F32),),
        compiler_params=pltpu.CompilerParams(vmem_limit_bytes=VMEM_LIMIT),
        cost_estimate=pl.CostEstimate(
            flops=2 * rows * width * total * tensor,
            bytes_accessed=2 * width * total * tensor + 4 * rows * hidden * tensor,
            transcendentals=0,
        ),
        name="weight_grads",
    )(place, x_low, two_low, one_low, upper_low, act, mixed, out_low, student_low)


def weights_to_owner(parts, dp, tensor, shard, z):
    if len(parts) == 1:
        order = (z - jnp.arange(tensor)) % tensor
        whole_parts = jnp.take(parts[0], order, axis=0)
        columns = whole_parts.shape[-1]
        return lax.psum_scatter(
            whole_parts.reshape(-1, columns), ("tensor", "dp"), scatter_dimension=0, tiled=True
        ).astype(F32)
    keep, give = parts
    bits = bits_of(dp)
    got = swapped(give, "dp", dp, bits[0])
    half = tensor // 2
    own = []
    for side, order in enumerate((bits[1:], bits[1:][::-1])):
        here = slice(side * half, (side + 1) * half)
        value = keep[here].astype(F32) + got[here].astype(F32)
        left = list(bits[1:])
        for bit in order:
            place = left.index(bit)
            low, high = 1 << place, 1 << (len(left) - 1 - place)
            shape = value.shape
            pairs = value.reshape(half, high, 2, low, *shape[2:])
            sent = swapped(pairs[:, :, 1].astype(BF16), "dp", dp, bit)
            value = (pairs[:, :, 0] + sent.astype(F32)).reshape(half, high * low, *shape[2:])
            left.remove(bit)
        own += [value[t, 0] for t in range(half)]
    total = own[1]
    for t in list(range(2, tensor)) + [0]:
        total = own[t] + shifted(total.astype(BF16), "tensor", tensor, 1).astype(F32)
    return total


def per_device(
    dp, tensor, tokens, cotangent, labels, piece_start, piece_len, w_qkv, w_out, w_up, w_down,
    vec_table, ff_bias, cls_proj, cls_vec, cls_hidden, cls_out, cls_bias,
):
    rows, width = tokens.shape
    local = w_qkv.shape[2]
    heads = local // HEAD_DIM
    padded = -(-local // LANES) * LANES
    shard = w_qkv.shape[0]
    hidden = w_up.shape[1]
    ch = cls_proj.shape[1]
    z = lax.axis_index("tensor")
    z_one = z.reshape(1).astype(jnp.int32)
    place = jnp.stack([z, lax.axis_index("dp"), labels[0]]).astype(jnp.int32)

    extra = padded - local
    qkv_shard = jnp.pad(w_qkv, ((0, 0), (0, 0), (0, extra))).reshape(shard, 3 * padded)
    w_in = gathered(qkv_shard, "dp", dp)
    pieces = gathered_weights(
        jnp.concatenate([w_up, w_down.T, w_out.T], axis=1), dp, tensor, z
    )
    slots = weight_slots(tensor, dp, shard)

    q_bias = lax.dynamic_slice_in_dim(vec_table[0], z * local, local, 0)
    v_bias = lax.dynamic_slice_in_dim(vec_table[1], z * local, local, 0)
    in_bias = jnp.pad(
        jnp.stack([q_bias, jnp.zeros_like(q_bias), v_bias]), ((0, 0), (0, extra))
    ).reshape(1, 3 * padded)

    seq_rows = [tokens]
    for _ in range(tensor - 1):
        seq_rows.append(shifted(seq_rows[-1], "tensor", tensor, 1))
    chunks = [
        (jnp.dot(part, w_in, preferred_element_type=F32) + in_bias).astype(BF16)
        for part in seq_rows
    ]
    mixed, lse = attend_forward(z_one, piece_start, piece_len, chunks, heads)

    def to_rows(parts):
        return [parts[0]] + [
            shifted(parts[tensor - s], "tensor", tensor, s) for s in range(1, tensor)
        ]

    kept = rows_forward(
        place, slots, pieces, to_rows(mixed), tokens, vec_table,
        ff_bias.reshape(tensor, 1, hidden), cls_proj, cls_vec,
    )
    out_low, x_low, act, _, _, _, _, _, mixed_all, _, stats = kept
    all_stats = [stats] + [shifted(stats, "tensor", tensor, s) for s in range(1, tensor)]
    (
        logits, two_low, upper_low, one_low, grad_h_one, grad_mixed, sums, ff_sums, student_low,
        small, grad_hid, grad_out_w,
    ) = rows_backward(
        place, slots, pieces, all_stats, kept, cotangent, vec_table, cls_proj, cls_vec,
        cls_hidden, jnp.pad(cls_out, ((0, 0), (0, ch - CLASSES))),
        jnp.pad(cls_bias, (0, ch - CLASSES)).reshape(1, ch),
    )
    grad_rows = to_rows(grad_mixed)
    *ff_parts, grad_proj = weight_grads(
        place, dp, shard, x_low, two_low, one_low, upper_low, act, mixed_all, out_low, student_low
    )
    ff_own = weights_to_owner(ff_parts, dp, tensor, shard, z)

    proj_sum, hid_sum, out_w_sum, small_sum, vec_sum, ff_bias_sum = lax.psum(
        (grad_proj, grad_hid, grad_out_w, small, sums, ff_sums.reshape(tensor, hidden)),
        ("dp", "tensor"),
    )

    d_chunks, bias_sums = attend_backward(
        z_one, piece_start, piece_len, chunks, grad_rows, mixed, lse, heads
    )
    total = None
    for t in list(range(1, tensor)) + [0]:
        part = lax.dot_general(
            d_chunks[t], w_in, (((1,), (1,)), ((), ())), preferred_element_type=F32
        )
        if total is not None:
            part = part + total.astype(F32)
        total = shifted(part.astype(BF16), "tensor", tensor, 1) if t else part
    grad_tokens = grad_h_one + total

    grad_in = None
    for t in range(tensor):
        part = lax.dot_general(
            seq_rows[t], d_chunks[t], (((0,), (0,)), ((), ())), preferred_element_type=F32
        )
        grad_in = part if grad_in is None else grad_in + part
    grad_in = summed_to_owner(grad_in.reshape(dp, shard, 3 * padded), "dp", dp)
    grad_w_qkv = grad_in.reshape(shard, 3, padded)[:, :, :local]

    bias_rows = lax.dynamic_update_slice(
        jnp.zeros((2, width), F32), bias_sums[:2, :local], (0, z * local)
    )
    bias_sum = summed(bias_rows, dp, tensor)
    grad_vec = jnp.concatenate([bias_sum, vec_sum[2:]], axis=0)
    return (
        out_low,
        logits[0:1, :CLASSES],
        grad_tokens,
        grad_w_qkv,
        ff_own[:, 2 * hidden :].T,
        ff_own[:, :hidden],
        ff_own[:, hidden : 2 * hidden].T,
        grad_vec,
        ff_bias_sum.reshape(-1),
        proj_sum,
        small_sum[:3],
        hid_sum,
        out_w_sum[:, :CLASSES],
        small_sum[3, :CLASSES],
    )


def solution(mesh):
    dp, tensor = mesh.shape["dp"], mesh.shape["tensor"]
    return jax.shard_map(
        functools.partial(per_device, dp, tensor),
        mesh=mesh,
        in_specs=(
            P(("dp", "tensor"), None),
            P(("dp", "tensor"), None),
            P("dp"),
            P("dp", None),
            P("dp", None),
            P("dp", None, "tensor"),
            P("tensor", "dp"),
            P("dp", "tensor"),
            P("tensor", "dp"),
            P(),
            P(),
            P(),
            P(),
            P(),
            P(),
            P(),
        ),
        out_specs=(
            P(("dp", "tensor"), None),
            P("dp", None),
            P(("dp", "tensor"), None),
            P("dp", None, "tensor"),
            P("tensor", "dp"),
            P("dp", "tensor"),
            P("tensor", "dp"),
            P(),
            P(),
            P(),
            P(),
            P(),
            P(),
            P(),
        ),
        check_vma=False,
    )
```

time: 1140 us -> 475 us (0.42)
  waiting for transfers between devices: 664 us -> 177 us
  matrix products: 224 us -> 35.2 us
  Pallas kernels: 0 us -> 108 us
  other arithmetic: 82.1 us -> 21.3 us
  blocking collectives: 87.6 us -> 42.7 us
  starting transfers between devices: 0.85 us -> 43.7 us
  local copies, waits for them, and re-layouts: 44 us -> 24.3 us
  loops' own time: 14.4 us -> 0 us
    reduce_scatter x7 -> x0, waiting for transfers between devices: 344 us -> none  [the longest x1 110 us: per_device(): lax.psum_scatter(contract_cols(grad_upper_low, up_full), 'tensor', scatte...]
    all_gather x6 -> x0, waiting for transfers between devices: 234 us -> none  [the longest x1 63.9 us: per_device(): lax.all_gather(grad_one_low, 'tensor', axis=0, tiled=True)]
    dot_general x50 -> x12, matrix products: 219 us -> 35.2 us  [the longest x4 14.4 us: per_device(): lax.dot_general(seq_rows[t], d_chunks[t], (((0,), (0,)), ((), ())), prefe...]
    ppermute x0 -> x43, waiting for transfers between devices: none -> 177 us  [the longest x21 92.7 us: shifted(): lax.ppermute(value, axis, [(i, (i + by) % size) for i in range(size)])]
    pallas_call x0 -> x5, Pallas kernels: none -> 108 us  [the longest x1 33.9 us: attend_backward(): pl.pallas_call(functools.partial(attend_backward_kernel, heads), out_shap...]
    psum x1, waiting for transfers between devices: 85.1 us -> 0.01 us  [per_device(): lax.psum((grad_proj, grad_hid, grad_out_w, small, sums, ff_sums.reshape(t...]
    reduce_sum x20 -> x0, other arithmetic: 43.7 us -> none  [the longest x4 27.1 us: one_block(): row_total = jnp.sum(powers, axis=-1, keepdims=True)]
    ppermute x0 -> x43, starting transfers between devices: none -> 43.7 us  [the longest x21 26.5 us: shifted(): lax.ppermute(value, axis, [(i, (i + by) % size) for i in range(size)])]
  transfers between devices with their start and end apart: 15 -> 44, of which waited for: 12 -> 21; matrix products, arithmetic and copies ran while one was open for 6% -> 14% of each run, Pallas kernels for 0% -> 13%
where the time goes in v1:
time: 475 us; the launch traced here: 468 us
  waiting for transfers between devices  177 us (37%)
  Pallas kernels  108 us (23%)
  starting transfers between devices  43.7 us (9%)
  blocking collectives  42.7 us (9%)
  matrix products  35.2 us (7%)
  local copies, waits for them, and re-layouts  24.3 us (5%)
  other arithmetic  21.3 us (4%)
  between operations  15.9 us (3%)
    ppermute x21, waiting for transfers between devices, shifted(): lax.ppermute(value, axis, [(i, (i + by) % size) for i in range(size)])  92.7 us
    ppermute x22, waiting for transfers between devices, swapped(): return lax.ppermute(value, axis, [(i, i ^ bit) for i in range(size)])  84 us
    psum x1, blocking collectives, per_device(): lax.psum((grad_proj, grad_hid, grad_out_w, small, sums, ff_sums.reshape(t...  42.7 us
    pallas_call x1, Pallas kernels, attend_backward(): pl.pallas_call(functools.partial(attend_backward_kernel, heads), out_shap...  33.9 us
    pallas_call x1, Pallas kernels, attend_forward(): pl.pallas_call(functools.partial(attend_forward_kernel, heads), out_shape...  28.4 us
    ppermute x21, starting transfers between devices, shifted(): lax.ppermute(value, axis, [(i, (i + by) % size) for i in range(size)])  26.5 us
    unnamed x97, local copies, waits for them, and re-layouts  17.4 us
    pallas_call x1, Pallas kernels, rows_forward(): pl.pallas_call(functools.partial(rows_forward_kernel, tensor, slots, shar...  17.3 us
  transfers between devices with their start and end apart: 44, of which 21 were waited for; matrix products, arithmetic and copies ran while one was open for 14% of the time, Pallas kernels for 13%

profile of v1, /device:TPU:0, one launch (start us, length us, event | category | flops | bytes accessed | tf_op | source)
XLA Modules:
  0.0 467.9 jit_solution(7052648017982697715)
XLA Ops:
  12.2 10.1 %collective-permute-done.9 = bf16[96,1728]{1,0:T(8,128)(2,1)S(1)} collective-permute-done((bf16[96,1728]{1,0:T(8,128)(2,1)S(1)}, bf16[96,1728]{1,0:T(8,128)(2,1)S(1)}, u32[]{:S(2)}, u32[]{:S(2)}) %collective-permute-start.9) | collective-permute-done | bytes 331808 | tf_op jit(solution)/shard_map/ppermute | solution.py:42
  22.3 11.0 %collective-permute-done.13 = bf16[96,1728]{1,0:T(8,128)(2,1)S(1)} collective-permute-done((bf16[96,1728]{1,0:T(8,128)(2,1)S(1)}, bf16[96,1728]{1,0:T(8,128)(2,1)S(1)}, u32[]{:S(2)}, u32[]{:S(2)}) %collective-permute-start.13) | collective-permute-done | bytes 331808 | tf_op jit(solution)/shard_map/ppermute | solution.py:42
  34.7 8.7 %collective-permute-done.14 = bf16[96,1728]{1,0:T(8,128)(2,1)S(1)} collective-permute-done((bf16[96,1728]{1,0:T(8,128)(2,1)S(1)}, bf16[96,1728]{1,0:T(8,128)(2,1)S(1)}, u32[]{:S(2)}, u32[]{:S(2)}) %collective-permute-start.14) | collective-permute-done | bytes 331808 | tf_op jit(solution)/shard_map/ppermute | solution.py:42
  52.3 9.7 %collective-permute-done.15 = bf16[2,96,1728]{2,1,0:T(8,128)(2,1)S(1)} collective-permute-done((bf16[2,96,1728]{2,1,0:T(8,128)(2,1)S(1)}, bf16[2,96,1728]{2,1,0:T(8,128)(2,1)S(1)}, u32[]{:S(2)}, u32[]{:S(2)}) %collective-permute-start.15) | collective-permute-done | bytes 663584 | tf_op jit(solution)/shard_map/ppermute | solution.py:46
  67.1 27.7 %collective-permute-done.1 = bf16[192,768]{1,0:T(8,128)(2,1)S(1)} collective-permute-done((bf16[192,768]{1,0:T(8,128)(2,1)S(1)}, bf16[192,768]{1,0:T(8,128)(2,1)S(1)}, u32[]{:S(2)}, u32[]{:S(2)}) %collective-permute-start.1) | collective-permute-done | bytes 294944 | tf_op jit(solution)/shard_map/ppermute | solution.py:46
  102.7 10.3 %collective-permute-done.4 = bf16[512,768]{1,0:T(8,128)(2,1)} collective-permute-done((bf16[512,768]{1,0:T(8,128)(2,1)}, bf16[512,768]{1,0:T(8,128)(2,1)}, u32[]{:S(2)}, u32[]{:S(2)}) %collective-permute-start.4) | collective-permute-done | bytes 786464 | tf_op jit(solution)/shard_map/ppermute | solution.py:42
  120.6 6.5 %collective-permute-done.5 = bf16[512,768]{1,0:T(8,128)(2,1)S(1)} collective-permute-done((bf16[512,768]{1,0:T(8,128)(2,1)}, bf16[512,768]{1,0:T(8,128)(2,1)S(1)}, u32[]{:S(2)}, u32[]{:S(2)}) %collective-permute-start.5) | collective-permute-done | bytes 786464 | tf_op jit(solution)/shard_map/ppermute | solution.py:42
  129.6 28.4 %attend_forward.1 = (bf16[4,512,192]{2,1,0:T(8,128)(2,1)S(1)}, f32[8,8,256]{2,1,0:T(8,128)S(1)}) custom-call(s32[1]{0:T(128)} %bitcast.z_ref, s32[1,2]{1,0:T(1,128)S(1)} %copy-done.7, s32[1,2]{1,0:T(1,128)S(1)} %copy-done.8, bf16[512,768]{1,0:T(8,128)(2,1)S(1)} %fusion.8.refs_0_, bf16[512,768]{1,0:T(8,128)(2,1)S(1)} %fusion.9.refs_1_, ...), custom_call_target="tpu_custom_call" | custom-call | flops 7247757312 | bytes 6291456 | tf_op jit(solution)/shard_map/attend_forward/pallas_call | solution.py:185
  162.9 5.2 %collective-permute-done.6.refs_1_ = bf16[512,192]{1,0:T(8,128)(2,1)S(1)} collective-permute-done((bf16[512,192]{1,0:T(8,128)(2,1)S(1)}, bf16[512,192]{1,0:T(8,128)(2,1)S(1)}, u32[]{:S(2)}, u32[]{:S(2)}) %collective-permute-start.6) | collective-permute-done | bytes 196640 | tf_op jit(solution)/shard_map/ppermute | solution.py:42
  168.2 6.0 %collective-permute-done.7.refs_2_ = bf16[512,192]{1,0:T(8,128)(2,1)S(1)} collective-permute-done((bf16[512,192]{1,0:T(8,128)(2,1)S(1)}, bf16[512,192]{1,0:T(8,128)(2,1)S(1)}, u32[]{:S(2)}, u32[]{:S(2)}) %collective-permute-start.7) | collective-permute-done | bytes 196640 | tf_op jit(solution)/shard_map/ppermute | solution.py:42
  174.2 17.3 %rows_forward.1 = (bf16[512,768]{1,0:T(8,128)(2,1)}, bf16[512,768]{1,0:T(8,128)(2,1)S(1)}, bf16[4,512,768]{2,1,0:T(8,128)(2,1)}, bf16[4,512,768]{2,1,0:T(8,128)(...) custom-call(s32[3]{0:T(128)S(1)} %pad_add_fusion.place_ref, ...), custom_call_target="tpu_custom_call" | custom-call | flops 5435817984 | bytes 17301504 | tf_op jit(solution)/shard_map/rows_forward/pallas_call | solution.py:509
  194.8 4.9 %collective-permute-start.18 = (f32[8,128]{1,0:T(8,128)S(1)}, f32[8,128]{1,0:T(8,128)S(1)}, u32[]{:S(2)}, u32[]{:S(2)}) collective-permute-start(f32[8,128]{1,0:T(8,128)S(1)} %get-tuple-element.46.refs_0_), channel_id=1, source_target_pairs={{0,1},{1,2},{2,3},{3,0},{4,5},{5,6},{6,7},{7,4},{8,9},{9,10},{10,1... | collective-permute-start | bytes 12296 | tf_op jit(solution)/shard_map/ppermute | solution.py:42
  207.3 17.3 %rows_backward.1 = (f32[8,128]{1,0:T(8,128)S(1)}, bf16[512,768]{1,0:T(8,128)(2,1)S(1)}, bf16[4,512,768]{2,1,0:T(8,128)(2,1)}, bf16[512,768]{1,0:T(8,128)(2,1)S(1...) custom-call(s32[3]{0:T(128)S(1)} %pad_add_fusion.place_ref, ...), custom_call_target="tpu_custom_call" | custom-call | flops 5435817984 | bytes 17301504 | tf_op jit(solution)/shard_map/rows_backward/pallas_call | solution.py:688
  224.7 11.2 %weight_grads.1 = (bf16[4,4,96,1728]{3,2,1,0:T(8,128)(2,1)}, bf16[4,4,96,1728]{3,2,1,0:T(8,128)(2,1)}, f32[768,128]{1,0:T(8,128)}) custom-call(s32[3]{0:T(128)S(1)} %pad_add_fusion.place_ref, bf16[512,768]{1,0:T(8,128)(2,1)S(1)} %copy-done.25, bf16[512,768]{1,0:T(8,128)(2,1)S(1)} %get-tuple-element.59.two_ref, ...), custom_call_target="tpu_custom_call" | custom-call | flops 5435817984 | bytes 16908288 | tf_op jit(solution)/shard_map/weight_grads/pallas_call | solution.py:807
  241.8 42.7 %all-reduce.4 = (f32[8,768]{1,0:T(8,128)S(1)}, f32[3072]{0:T(1024)}, f32[8,128]{1,0:T(8,128)S(1)}) all-reduce(f32[8,768]{1,0:T(8,128)S(1)} %get-tuple-element.68, f32[3072]{0:T(1024)S(1)} %bitcast.148, f32[8,128]{1,0:T(8,128)S(1)} %get-tuple-element.71), channel_id=1, replica_groups=mesh['dp'=8,'tensor'=4] {'dp','tensor'}, use_global_device_ids=true, to_apply=%region_0.1 | all-reduce | flops 10240 | bytes 81920 | tf_op jit(solution)/shard_map/psum | solution.py:932
  291.3 33.9 %attend_backward.1 = (bf16[4,512,768]{2,1,0:T(8,128)(2,1)}, f32[8,256]{1,0:T(8,128)S(1)}) custom-call(s32[1]{0:T(128)} %bitcast.z_ref, s32[1,2]{1,0:T(1,128)S(1)} %copy-done.7, s32[1,2]{1,0:T(1,128)S(1)} %copy-done.8, bf16[512,768]{1,0:T(8,128)(2,1)S(1)} %copy-done.17, bf16[512,768]{1,0:T(8,128)(2,1)S(1)} %copy-done.15, bf16[512,768]{1,0:T(8,128)(2,1)S(1)} %copy-done.19, ...), custom_call_target="tpu_custom_call" | custom-call | flops 18119393280 | bytes 9437184 | tf_op jit(solution)/shard_map/attend_backward/pallas_call | solution.py:325
  355.4 11.3 %collective-permute-done.42 = f32[2,768]{1,0:T(2,128)S(1)} collective-permute-done((f32[2,768]{1,0:T(2,128)S(1)}, f32[2,768]{1,0:T(2,128)S(1)}, u32[]{:S(2)}, u32[]{:S(2)}) %collective-permute-start.42) | collective-permute-done | bytes 6176 | tf_op jit(solution)/shard_map/ppermute | solution.py:46
  381.0 13.5 %collective-permute-done.25 = bf16[512,768]{1,0:T(8,128)(2,1)S(1)} collective-permute-done((bf16[512,768]{1,0:T(8,128)(2,1)S(1)}, bf16[512,768]{1,0:T(8,128)(2,1)S(1)}, u32[]{:S(2)}, u32[]{:S(2)}) %collective-permute-start.25) | collective-permute-done | bytes 786464 | tf_op jit(solution)/shard_map/ppermute | solution.py:42
  398.4 5.8 %collective-permute-done.31 = bf16[2,2,1,96,1728]{4,3,0,1,2:T(8,128)(2,1)S(1)} collective-permute-done((bf16[2,2,1,96,1728]{4,3,0,1,2:T(8,128)(2,1)S(1)}, bf16[2,2,1,96,1728]{4,3,0,1,2:T(8,128)(2,1)S(1)}, u32[]{:S(2)}, u32[]{:S(2)}) %collective-permute-start.31) | collective-permute-done | bytes 1327136 | tf_op jit(solution)/shard_map/ppermute | solution.py:46
  405.9 10.8 %collective-permute-done.33 = bf16[2,1,2,96,1728]{4,3,0,2,1:T(8,128)(2,1)S(1)} collective-permute-done((bf16[2,1,2,96,1728]{4,3,0,2,1:T(8,128)(2,1)S(1)}, bf16[2,1,2,96,1728]{4,3,0,2,1:T(8,128)(2,1)S(1)}, u32[]{:S(2)}, u32[]{:S(2)}) %collective-permute-start.33) | collective-permute-done | bytes 1327136 | tf_op jit(solution)/shard_map/ppermute | solution.py:46
  418.2 9.5 %collective-permute-done.32 = bf16[2,1,1,96,1728]{4,3,2,1,0:T(8,128)(2,1)S(1)} collective-permute-done((bf16[2,1,1,96,1728]{4,3,2,1,0:T(8,128)(2,1)S(1)}, bf16[2,1,1,96,1728]{4,3,2,1,0:T(8,128)(2,1)S(1)}, u32[]{:S(2)}, u32[]{:S(2)}) %collective-permute-start.32) | collective-permute-done | bytes 663584 | tf_op jit(solution)/shard_map/ppermute | solution.py:46
  428.4 8.6 %collective-permute-done.35 = bf16[96,1728]{1,0:T(8,128)(2,1)S(1)} collective-permute-done((bf16[96,1728]{1,0:T(8,128)(2,1)S(1)}, bf16[96,1728]{1,0:T(8,128)(2,1)S(1)}, u32[]{:S(2)}, u32[]{:S(2)}) %collective-permute-start.35) | collective-permute-done | bytes 331808 | tf_op jit(solution)/shard_map/ppermute | solution.py:42
  442.6 4.8 %collective-permute-done.36 = bf16[96,1728]{1,0:T(8,128)(2,1)} collective-permute-done((bf16[96,1728]{1,0:T(8,128)(2,1)}, bf16[96,1728]{1,0:T(8,128)(2,1)}, u32[]{:S(2)}, u32[]{:S(2)}) %collective-permute-start.36) | collective-permute-done | bytes 331808 | tf_op jit(solution)/shard_map/ppermute | solution.py:42
  451.6 5.9 %collective-permute-done.37 = bf16[96,1728]{1,0:T(8,128)(2,1)S(1)} collective-permute-done((bf16[96,1728]{1,0:T(8,128)(2,1)S(1)}, bf16[96,1728]{1,0:T(8,128)(2,1)S(1)}, u32[]{:S(2)}, u32[]{:S(2)}) %collective-permute-start.37) | collective-permute-done | bytes 331808 | tf_op jit(solution)/shard_map/ppermute | solution.py:42
  (239 shorter events, 130.8 us)
Async XLA Ops:
  7.2 431.3 %all-reduce.8.cloned.1.call-start = ((), (), s32[]{:S(2)}) async-start(), calls=%async_computation | async-start | bytes 1048576 | tf_op jit(solution)/shard_map/psum | solution.py:932
  43.6 18.4 %collective-permute-start.15 = (bf16[2,96,1728]{2,1,0:T(8,128)(2,1)S(1)}, bf16[2,96,1728]{2,1,0:T(8,128)(2,1)S(1)}, u32[]{:S(2)}, u32[]{:S(2)}) collective-permute-start(bf16[2,96,1728]{2,1,0:T(8,128)(2,1)S(1)} %pad_maximum_fusion.5), channel_id=1, source_target_pairs={{0,16},{4,20},{8,24},{12,28},{16,0},{20,4},{24,8},{28,12},{1,17},{... | collective-permute-start | bytes 1990664 | tf_op jit(solution)/shard_map/ppermute | solution.py:46
  51.3 45.1 %collective-permute-start.11 = (bf16[4,96,1728]{2,1,0:T(8,128)(2,1)}, bf16[4,96,1728]{2,1,0:T(8,128)(2,1)}, u32[]{:S(2)}, u32[]{:S(2)}) collective-permute-start(bf16[4,96,1728]{2,1,0:T(8,128)(2,1)} %pad_maximum_fusion.2), channel_id=1, source_target_pairs={{0,16},{4,20},{8,24},{12,28},{16,0},{20,4},{24,8},{28,12},{1,17},{... | collective-permute-start | bytes 3981320 | tf_op jit(solution)/shard_map/ppermute | solution.py:46
  63.3 35.9 %collective-permute-start.16 = (bf16[4,96,1728]{2,1,0:T(8,128)(2,1)}, bf16[4,96,1728]{2,1,0:T(8,128)(2,1)}, u32[]{:S(2)}, u32[]{:S(2)}) collective-permute-start(bf16[4,96,1728]{2,1,0:T(8,128)(2,1)} %pad_maximum_fusion.3), channel_id=1, source_target_pairs={{0,8},{4,12},{8,0},{12,4},{16,24},{20,28},{24,16},{28,20},{1,9},{5... | collective-permute-start | bytes 3981320 | tf_op jit(solution)/shard_map/ppermute | solution.py:46
  64.3 32.1 %collective-permute-start.3 = (bf16[512,768]{1,0:T(8,128)(2,1)S(1)}, bf16[512,768]{1,0:T(8,128)(2,1)}, u32[]{:S(2)}, u32[]{:S(2)}) collective-permute-start(bf16[512,768]{1,0:T(8,128)(2,1)S(1)} %copy-done), channel_id=1, source_target_pairs={{0,1},{1,2},{2,3},{3,0},{4,5},{5,6},{6,7},{7,4},{8,9},{9,10},{10,1... | collective-permute-start | bytes 2359304 | tf_op jit(solution)/shard_map/ppermute | solution.py:42
  66.0 28.8 %collective-permute-start.1 = (bf16[192,768]{1,0:T(8,128)(2,1)S(1)}, bf16[192,768]{1,0:T(8,128)(2,1)S(1)}, u32[]{:S(2)}, u32[]{:S(2)}) collective-permute-start(bf16[192,768]{1,0:T(8,128)(2,1)S(1)} %maximum_select_fusion.2), channel_id=1, source_target_pairs={{0,8},{4,12},{8,0},{12,4},{16,24},{20,28},{24,16},{28,20},{1,9},{5... | collective-permute-start | bytes 884744 | tf_op jit(solution)/shard_map/ppermute | solution.py:46
  95.8 17.3 %collective-permute-start.2 = (bf16[384,768]{1,0:T(8,128)(2,1)}, bf16[384,768]{1,0:T(8,128)(2,1)S(1)}, u32[]{:S(2)}, u32[]{:S(2)}) collective-permute-start(bf16[384,768]{1,0:T(8,128)(2,1)} %maximum_select_fusion.1), channel_id=1, source_target_pairs={{0,16},{4,20},{8,24},{12,28},{16,0},{20,4},{24,8},{28,12},{1,17},{... | collective-permute-start | bytes 1769480 | tf_op jit(solution)/shard_map/ppermute | solution.py:46
  96.3 16.7 %collective-permute-start.4 = (bf16[512,768]{1,0:T(8,128)(2,1)}, bf16[512,768]{1,0:T(8,128)(2,1)}, u32[]{:S(2)}, u32[]{:S(2)}) collective-permute-start(bf16[512,768]{1,0:T(8,128)(2,1)} %collective-permute-done.3), channel_id=1, source_target_pairs={{0,1},{1,2},{2,3},{3,0},{4,5},{5,6},{6,7},{7,4},{8,9},{9,10},{10,1... | collective-permute-start | bytes 2359304 | tf_op jit(solution)/shard_map/ppermute | solution.py:42
  99.2 74.9 %collective-permute-start.12 = (bf16[8,96,1728]{2,1,0:T(8,128)(2,1)}, bf16[8,96,1728]{2,1,0:T(8,128)(2,1)}, u32[]{:S(2)}, u32[]{:S(2)}) collective-permute-start(bf16[8,96,1728]{2,1,0:T(8,128)(2,1)} %pad_maximum_fusion.refs_9_.refs_17_), channel_id=1, source_target_pairs={{0,4},{4,0},{8,12},{12,8},{16,20},{20,16},{24,28},{28,24},{1,5},{5... | collective-permute-start | bytes 7962632 | tf_op jit(solution)/shard_map/ppermute | solution.py:46
  102.0 72.1 %collective-permute-start.17 = (bf16[8,96,1728]{2,1,0:T(8,128)(2,1)}, bf16[8,96,1728]{2,1,0:T(8,128)(2,1)}, u32[]{:S(2)}, u32[]{:S(2)}) collective-permute-start(bf16[8,96,1728]{2,1,0:T(8,128)(2,1)} %pad_maximum_fusion.1.refs_11_.refs_19_), channel_id=1, source_target_pairs={{0,4},{4,0},{8,12},{12,8},{16,20},{20,16},{24,28},{28,24},{1,5},{5... | collective-permute-start | bytes 7962632 | tf_op jit(solution)/shard_map/ppermute | solution.py:46
  158.2 15.9 %collective-permute-start.7 = (bf16[512,192]{1,0:T(8,128)(2,1)S(1)}, bf16[512,192]{1,0:T(8,128)(2,1)S(1)}, u32[]{:S(2)}, u32[]{:S(2)}) collective-permute-start(bf16[512,192]{1,0:T(8,128)(2,1)S(1)} %get-tuple-element.129), channel_id=1, source_target_pairs={{0,2},{1,3},{2,0},{3,1},{4,6},{5,7},{6,4},{7,5},{8,10},{9,11},{10,... | collective-permute-start | bytes 589832 | tf_op jit(solution)/shard_map/ppermute | solution.py:42
  235.8 132.1 %collective-permute-start.30 = (bf16[4,4,96,1728]{3,2,1,0:T(8,128)(2,1)}, bf16[4,4,96,1728]{3,2,1,0:T(8,128)(2,1)}, u32[]{:S(2)}, u32[]{:S(2)}) collective-permute-start(bf16[4,4,96,1728]{3,2,1,0:T(8,128)(2,1)} %get-tuple-element.66), channel_id=1, source_target_pairs={{0,4},{4,0},{8,12},{12,8},{16,20},{20,16},{24,28},{28,24},{1,5},{5... | collective-permute-start | bytes 15925256 | tf_op jit(solution)/shard_map/ppermute | solution.py:46
  236.7 50.1 %collective-permute-start.21 = (bf16[512,192]{1,0:T(8,128)(2,1)}, bf16[512,192]{1,0:T(8,128)(2,1)S(1)}, u32[]{:S(2)}, u32[]{:S(2)}) collective-permute-start(bf16[512,192]{1,0:T(8,128)(2,1)} %get-tuple-element.126), channel_id=1, source_target_pairs={{0,1},{1,2},{2,3},{3,0},{4,5},{5,6},{6,7},{7,4},{8,9},{9,10},{10,1... | collective-permute-start | bytes 589832 | tf_op jit(solution)/shard_map/ppermute | solution.py:42
  237.5 49.3 %collective-permute-start.22 = (bf16[512,192]{1,0:T(8,128)(2,1)}, bf16[512,192]{1,0:T(8,128)(2,1)S(1)}, u32[]{:S(2)}, u32[]{:S(2)}) collective-permute-start(bf16[512,192]{1,0:T(8,128)(2,1)} %get-tuple-element.125), channel_id=1, source_target_pairs={{0,2},{1,3},{2,0},{3,1},{4,6},{5,7},{6,4},{7,5},{8,10},{9,11},{10,... | collective-permute-start | bytes 589832 | tf_op jit(solution)/shard_map/ppermute | solution.py:42
  240.7 46.1 %collective-permute-start.23 = (bf16[512,192]{1,0:T(8,128)(2,1)S(1)}, bf16[512,192]{1,0:T(8,128)(2,1)S(1)}, u32[]{:S(2)}, u32[]{:S(2)}) collective-permute-start(bf16[512,192]{1,0:T(8,128)(2,1)S(1)} %get-tuple-element.124), channel_id=1, source_target_pairs={{0,3},{1,0},{2,1},{3,2},{4,7},{5,4},{6,5},{7,6},{8,11},{9,8},{10,9... | collective-permute-start | bytes 589832 | tf_op jit(solution)/shard_map/ppermute | solution.py:42
  342.6 24.1 %collective-permute-start.27 = (bf16[4,96,768]{2,1,0:T(8,128)(2,1)S(1)}, bf16[4,96,768]{2,1,0:T(8,128)(2,1)S(1)}, u32[]{:S(2)}, u32[]{:S(2)}) collective-permute-start(bf16[4,96,768]{2,1,0:T(8,128)(2,1)S(1)} %fusion.39), channel_id=1, source_target_pairs={{0,4},{4,0},{8,12},{12,8},{16,20},{20,16},{24,28},{28,24},{1,5},{5... | collective-permute-start | bytes 1769480 | tf_op jit(solution)/shard_map/ppermute | solution.py:46
  348.3 24.2 %collective-permute-start.24 = (bf16[512,768]{1,0:T(8,128)(2,1)S(1)}, bf16[512,768]{1,0:T(8,128)(2,1)S(1)}, u32[]{:S(2)}, u32[]{:S(2)}) collective-permute-start(bf16[512,768]{1,0:T(8,128)(2,1)S(1)} %convolution_convert_fusion), channel_id=1, source_target_pairs={{0,1},{1,2},{2,3},{3,0},{4,5},{5,6},{6,7},{7,4},{8,9},{9,10},{10,1... | collective-permute-start | bytes 2359304 | tf_op jit(solution)/shard_map/ppermute | solution.py:42
  350.6 16.1 %collective-permute-start.42 = (f32[2,768]{1,0:T(2,128)S(1)}, f32[2,768]{1,0:T(2,128)S(1)}, u32[]{:S(2)}, u32[]{:S(2)}) collective-permute-start(f32[2,768]{1,0:T(2,128)S(1)} %add.214), channel_id=1, source_target_pairs={{0,2},{1,3},{2,0},{3,1},{4,6},{5,7},{6,4},{7,5},{8,10},{9,11},{10,... | collective-permute-start | bytes 18440 | tf_op jit(solution)/shard_map/ppermute | solution.py:46
  371.4 32.7 %collective-permute-start.31 = (bf16[2,2,1,96,1728]{4,3,0,1,2:T(8,128)(2,1)S(1)}, bf16[2,2,1,96,1728]{4,3,0,1,2:T(8,128)(2,1)S(1)}, u32[]{:S(2)}, u32[]{:S(2)}) collective-permute-start(bf16[2,2,1,96,1728]{4,3,0,1,2:T(8,128)(2,1)S(1)} %fusion.4), channel_id=1, source_target_pairs={{0,8},{4,12},{8,0},{12,4},{16,24},{20,28},{24,16},{28,20},{1,9},{5... | collective-permute-start | bytes 3981320 | tf_op jit(solution)/shard_map/ppermute | solution.py:46
  374.6 20.0 %collective-permute-start.25 = (bf16[512,768]{1,0:T(8,128)(2,1)S(1)}, bf16[512,768]{1,0:T(8,128)(2,1)S(1)}, u32[]{:S(2)}, u32[]{:S(2)}) collective-permute-start(bf16[512,768]{1,0:T(8,128)(2,1)S(1)} %add_convert_fusion.1), channel_id=1, source_target_pairs={{0,1},{1,2},{2,3},{3,0},{4,5},{5,6},{6,7},{7,4},{8,9},{9,10},{10,1... | collective-permute-start | bytes 2359304 | tf_op jit(solution)/shard_map/ppermute | solution.py:42
  378.8 61.2 %collective-permute-start.29 = (bf16[1,96,768]{2,1,0:T(8,128)(2,1)}, bf16[1,96,768]{2,1,0:T(8,128)(2,1)S(1)}, u32[]{:S(2)}, u32[]{:S(2)}) collective-permute-start(bf16[1,96,768]{2,1,0:T(8,128)(2,1)} %dynamic-slice_convert_fusion.1), channel_id=1, source_target_pairs={{0,16},{4,20},{8,24},{12,28},{16,0},{20,4},{24,8},{28,12},{1,17},{... | collective-permute-start | bytes 442376 | tf_op jit(solution)/shard_map/ppermute | solution.py:46
  379.5 37.2 %collective-permute-start.33 = (bf16[2,1,2,96,1728]{4,3,0,2,1:T(8,128)(2,1)S(1)}, bf16[2,1,2,96,1728]{4,3,0,2,1:T(8,128)(2,1)S(1)}, u32[]{:S(2)}, u32[]{:S(2)}) collective-permute-start(bf16[2,1,2,96,1728]{4,3,0,2,1:T(8,128)(2,1)S(1)} %fusion.5), channel_id=1, source_target_pairs={{0,16},{4,20},{8,24},{12,28},{16,0},{20,4},{24,8},{28,12},{1,17},{... | collective-permute-start | bytes 3981320 | tf_op jit(solution)/shard_map/ppermute | solution.py:46
  397.6 50.9 %collective-permute-start.26 = (bf16[512,768]{1,0:T(8,128)(2,1)}, bf16[512,768]{1,0:T(8,128)(2,1)}, u32[]{:S(2)}, u32[]{:S(2)}) collective-permute-start(bf16[512,768]{1,0:T(8,128)(2,1)} %add_convert_fusion), channel_id=1, source_target_pairs={{0,1},{1,2},{2,3},{3,0},{4,5},{5,6},{6,7},{7,4},{8,9},{9,10},{10,1... | collective-permute-start | bytes 2359304 | tf_op jit(solution)/shard_map/ppermute | solution.py:42
  404.6 23.2 %collective-permute-start.32 = (bf16[2,1,1,96,1728]{4,3,2,1,0:T(8,128)(2,1)S(1)}, bf16[2,1,1,96,1728]{4,3,2,1,0:T(8,128)(2,1)S(1)}, u32[]{:S(2)}, u32[]{:S(2)}) collective-permute-start(bf16[2,1,1,96,1728]{4,3,2,1,0:T(8,128)(2,1)S(1)} %fusion.32), channel_id=1, source_target_pairs={{0,16},{4,20},{8,24},{12,28},{16,0},{20,4},{24,8},{28,12},{1,17},{... | collective-permute-start | bytes 1990664 | tf_op jit(solution)/shard_map/ppermute | solution.py:46
  (64 other events, 639.6 us)
Sparse Core Ops, SparseCore 0:
  286.4 137.3 all-reduce.7

commit v2 on v1

v2 whole, which is shorter than its diff:
```python
import functools

import jax
import jax.numpy as jnp
from jax import lax
from jax.experimental import pallas as pl
from jax.experimental.pallas import tpu as pltpu
from jax.sharding import PartitionSpec as P

HEAD_DIM = 64
CLASSES = 14
PIECE_BLOCK = 256
POOL_HEADS = 2
LANES = 128
NORM_EPS = 1e-05
MASK_FILL = -1e30
PRECISE = lax.Precision.HIGHEST
F32 = jnp.float32
BF16 = jnp.bfloat16
VMEM_LIMIT = 48 * 1024 * 1024
LIGHT = pl.CostEstimate(flops=1024, bytes_accessed=1024, transcendentals=0)


def dot_nn(a, b, precision=None):
    return lax.dot_general(
        a, b, (((1,), (0,)), ((), ())), preferred_element_type=F32, precision=precision
    )


def dot_nt(a, b, precision=None):
    return lax.dot_general(
        a, b, (((1,), (1,)), ((), ())), preferred_element_type=F32, precision=precision
    )


def dot_tn(a, b, precision=None):
    return lax.dot_general(
        a, b, (((0,), (0,)), ((), ())), preferred_element_type=F32, precision=precision
    )


def bits_of(size):
    return [1 << n for n in range(size.bit_length() - 1)]


def swapped(value, axis, size, bit):
    return lax.ppermute(value, axis, [(i, i ^ bit) for i in range(size)])


def shifted(value, axis, size, by):
    return lax.ppermute(value, axis, [(i, (i + by) % size) for i in range(size)])


def after(value, *others):
    return lax.optimization_barrier((value, others))[0]


def in_turn(mark, chains, turns):
    under_way, results = {}, {}

    def advance(name, value):
        try:
            under_way[name] = chains[name].send(value)
        except StopIteration as end:
            under_way.pop(name, None)
            results[name] = end.value

    for name in chains:
        advance(name, None)
    turns = list(turns)
    while under_way:
        turn = turns.pop(0) if turns else tuple(under_way)
        names = [name for name in turn if name in under_way]
        if not names:
            continue
        sent = [value for value, _ in under_way.values()]
        there, mark, _ = lax.optimization_barrier(
            ([under_way[name][1] for name in names], mark, sent)
        )
        for name, value in zip(names, there):
            advance(name, value)
    return [results[name] for name in chains]


def ring_chain(value, size, kept):
    kept.append(value)
    for _ in range(size - 1):
        value = yield value, shifted(value, "tensor", size, 1)
        kept.append(value)
    return kept


def gather_chain(value, axis, size):
    index = lax.axis_index(axis)
    for bit in bits_of(size):
        other = yield value, swapped(value, axis, size, bit)
        low = (index // bit) % 2 == 0
        value = jnp.where(
            low, jnp.concatenate([value, other], 0), jnp.concatenate([other, value], 0)
        )
    return value


def owner_chain(parts, rider, axis, size, other, other_size):
    index = lax.axis_index(axis)
    riding = rider.shape[0]
    for bit in bits_of(size):
        mine = (index // bit) % 2
        count, rows, columns = parts.shape
        pairs = parts.reshape(count // 2, 2, rows, columns)
        keep = lax.dynamic_index_in_dim(pairs, mine, 1, keepdims=False)
        give = lax.dynamic_index_in_dim(pairs, 1 - mine, 1, keepdims=False)
        give = give.reshape(count // 2 * rows, columns)
        give = jnp.concatenate([give, rider]).astype(BF16)
        got = yield give, swapped(give, axis, size, bit)
        parts = keep + got[:-riding].reshape(keep.shape).astype(F32)
        rider = rider.astype(BF16).astype(F32) + got[-riding:].astype(F32)
    got = yield rider, [shifted(rider, other, other_size, by) for by in range(1, other_size)]
    place = lax.axis_index(other)
    riders = jnp.zeros((other_size, *rider.shape), F32)
    for by, value in enumerate([rider] + list(got)):
        riders = lax.dynamic_update_index_in_dim(riders, value, (place - by) % other_size, 0)
    return parts[0], riders


INFO_Z, INFO_D, INFO_LABEL, INFO_PIECES = 0, 1, 2, 3


def part_of(info_ref, place, tensor):
    return lax.rem(info_ref[INFO_Z] - place + tensor, tensor)


def block_range(info_ref, block):
    first, stop, inside_any = block, block + 1, jnp.int32(0)
    pieces = (info_ref.shape[0] - INFO_PIECES) // 2
    for piece in range(pieces):
        begin, count = info_ref[INFO_PIECES + piece], info_ref[INFO_PIECES + pieces + piece]
        inside = jnp.logical_and(block >= begin, block < begin + count)
        first = jnp.where(inside, begin, first)
        stop = jnp.where(inside, begin + count, stop)
        inside_any = jnp.where(inside, jnp.int32(1), inside_any)
    return first, stop, inside_any


def head_lanes(shape, head):
    lane = lax.broadcasted_iota(jnp.int32, shape, len(shape) - 1)
    return (lane >= head * HEAD_DIM) & (lane < (head + 1) * HEAD_DIM)


def attend_forward_kernel(heads, info_ref, *refs):
    tensor = len(refs) - 2 - 3
    chunks = refs[:tensor]
    o_ref, lse_ref = refs[tensor : tensor + 2]
    q_s, k_s, vt_s = refs[tensor + 2 :]
    rows, padded = chunks[0].shape[0], chunks[0].shape[1] // 3
    blk = PIECE_BLOCK
    blocks = tensor * rows // blk
    per_chunk = rows // blk
    scale = HEAD_DIM ** (-0.5)
    for t in range(tensor):
        quarter = part_of(info_ref, t, tensor)
        for part in range(per_chunk):
            b = quarter * per_chunk + part
            here = pl.ds(part * blk, blk)
            q = chunks[t][here, 0:padded]
            for h in range(heads):
                q_s[h, b] = jnp.where(head_lanes(q.shape, h), q * scale, 0.0).astype(BF16)
            pair, at = b // 2, lax.rem(b, 2) * blk
            k_s[pair, pl.ds(at, blk), :] = chunks[t][here, padded : 2 * padded]
            vt = chunks[t][here, 2 * padded : 3 * padded].T
            for side in range(2):

                @pl.when(lax.rem(b, 2) == side)
                def _():
                    vt_s[pair, :, side * blk : (side + 1) * blk] = vt


    def one_query(i, carry):
        _, stop, inside = block_range(info_ref, i)
        q_h = [q_s[h, i] for h in range(heads)]
        query = i * blk + lax.broadcasted_iota(jnp.int32, (1, blk), 1)
        limit = jnp.maximum(query, jnp.where(inside > 0, stop * blk - 1, 0))

        def step(j, state, masked):
            tops, totals, mixed = state
            keys = 2 * blk
            if masked:
                key = j * keys + lax.broadcasted_iota(jnp.int32, (keys, blk), 0)
                seen = key <= limit
            k_j = k_s[j]
            scores = [dot_nt(k_j, q_h[h]) for h in range(heads)]
            if masked:
                scores = [jnp.where(seen, s, MASK_FILL) for s in scores]
            new_tops = [
                jnp.maximum(tops[h], jnp.max(scores[h], axis=0, keepdims=True))
                for h in range(heads)
            ]
            ps = [jnp.exp(scores[h] - new_tops[h]) for h in range(heads)]
            fades = [jnp.exp(tops[h] - new_tops[h]) for h in range(heads)]
            new_totals = [
                totals[h] * fades[h] + jnp.sum(ps[h], axis=0, keepdims=True) for h in range(heads)
            ]
            new_mixed = [
                mixed[h] * fades[h]
                + dot_nn(vt_s[j, h * HEAD_DIM : (h + 1) * HEAD_DIM, :], ps[h].astype(BF16))
                for h in range(heads)
            ]
            return tuple(new_tops), tuple(new_totals), tuple(new_mixed)

        state = (
            tuple(jnp.full((1, blk), MASK_FILL, F32) for _ in range(heads)),
            tuple(jnp.zeros((1, blk), F32) for _ in range(heads)),
            tuple(jnp.zeros((HEAD_DIM, blk), F32) for _ in range(heads)),
        )
        last = i // 2
        state = lax.fori_loop(0, last, lambda j, c: step(j, c, False), state)
        state = step(last, state, True)
        tops, totals, mixed = lax.fori_loop(
            last + 1, (stop + 1) // 2, lambda j, c: step(j, c, True), state
        )
        outs = [mixed[h] * (1.0 / totals[h]) for h in range(heads)]
        lses = [tops[h] + jnp.log(totals[h]) for h in range(heads)]
        t = part_of(info_ref, i // per_chunk, tensor)
        here = pl.ds(lax.rem(i, per_chunk) * blk, blk)
        o_ref[t, here, :] = jnp.concatenate(outs, axis=0).T.astype(BF16)
        lse_ref[i] = jnp.concatenate(lses + [jnp.zeros((8 - heads, blk), F32)], axis=0)
        return carry

    lax.fori_loop(0, blocks, one_query, 0)


def attend_forward(info, chunks, heads):
    tensor = len(chunks)
    rows, width = chunks[0].shape
    padded = width // 3
    seq, blk = tensor * rows, PIECE_BLOCK
    blocks = seq // blk
    smem = pl.BlockSpec(memory_space=pltpu.SMEM)
    vmem = pl.BlockSpec(memory_space=pltpu.VMEM)
    return pl.pallas_call(
        functools.partial(attend_forward_kernel, heads),
        out_shape=(
            jax.ShapeDtypeStruct((tensor, rows, heads * HEAD_DIM), BF16),
            jax.ShapeDtypeStruct((blocks, 8, blk), F32),
        ),
        in_specs=[smem] + [vmem] * tensor,
        out_specs=(vmem, vmem),
        scratch_shapes=[
            pltpu.VMEM((heads, blocks, blk, padded), BF16),
            pltpu.VMEM((blocks // 2, 2 * blk, padded), BF16),
            pltpu.VMEM((blocks // 2, padded, 2 * blk), BF16),
        ],
        compiler_params=pltpu.CompilerParams(vmem_limit_bytes=VMEM_LIMIT),
        cost_estimate=LIGHT,
        name="attend_forward",
    )(info, *chunks)


def attend_backward_kernel(heads, info_ref, *refs):
    tensor = (len(refs) - 2 - 2 - 9) // 2
    chunks, grads = refs[:tensor], refs[tensor : 2 * tensor]
    o_ref, lse_ref, dqkv_ref, bias_ref = refs[2 * tensor : 2 * tensor + 4]
    q_s, k_s, kt_s, v_s, g_s, delta_s, dqt_s, dk_s, dv_s = refs[2 * tensor + 4 :]
    rows, padded = chunks[0].shape[0], chunks[0].shape[1] // 3
    width = heads * HEAD_DIM
    blk = PIECE_BLOCK
    blocks = tensor * rows // blk
    per_chunk = rows // blk
    scale = HEAD_DIM ** (-0.5)
    for t in range(tensor):
        quarter = part_of(info_ref, t, tensor)
        for part in range(per_chunk):
            b = quarter * per_chunk + part
            here = pl.ds(part * blk, blk)
            q = chunks[t][here, 0:padded]
            g = grads[t][here, :]
            for h in range(heads):
                q_s[h, b] = jnp.where(head_lanes(q.shape, h), q * scale, 0.0).astype(BF16)
                g_s[h, b, :, 0:width] = jnp.where(head_lanes(g.shape, h), g, 0.0).astype(BF16)
                if padded > width:
                    g_s[h, b, :, width:padded] = jnp.zeros((blk, padded - width), BF16)
            k = chunks[t][here, padded : 2 * padded]
            pair, at = b // 2, lax.rem(b, 2) * blk
            k_s[pair, pl.ds(at, blk), :] = k
            v_s[pair, pl.ds(at, blk), :] = chunks[t][here, 2 * padded : 3 * padded]
            kt = k.T
            for side in range(2):

                @pl.when(lax.rem(b, 2) == side)
                def _():
                    kt_s[pair, :, side * blk : (side + 1) * blk] = kt

            prod = (g.astype(F32) * o_ref[t, here, :].astype(F32)).T
            sums = [
                jnp.sum(prod[h * HEAD_DIM : (h + 1) * HEAD_DIM, :], axis=0, keepdims=True)
                for h in range(heads)
            ]
            delta_s[b] = jnp.concatenate(sums + [jnp.zeros((8 - heads, blk), F32)], axis=0)
            dqt_s[b] = jnp.zeros((padded, blk), F32)
    bias_ref[...] = jnp.zeros_like(bias_ref)

    keys = 2 * blk

    def one_pair(j, carry):
        first, _, _ = block_range(info_ref, 2 * j)
        also, _, _ = block_range(info_ref, 2 * j + 1)
        dk_s[...] = jnp.zeros_like(dk_s)
        dv_s[...] = jnp.zeros_like(dv_s)

        def step(i, masked):
            lse, delta = lse_ref[i], delta_s[i]
            if masked:
                _, stop, inside = block_range(info_ref, i)
                query = i * blk + lax.broadcasted_iota(jnp.int32, (1, blk), 1)
                limit = jnp.maximum(query, jnp.where(inside > 0, stop * blk - 1, 0))
                key = j * keys + lax.broadcasted_iota(jnp.int32, (keys, blk), 0)
                seen = key <= limit
            k_j, v_j = k_s[j], v_s[j]
            q_h = [q_s[h, i] for h in range(heads)]
            g_h = [g_s[h, i] for h in range(heads)]
            lows, ds = [], []
            for h in range(heads):
                p = jnp.exp(dot_nt(k_j, q_h[h]) - lse[h : h + 1, :])
                dp = dot_nt(v_j, g_h[h])
                if masked:
                    p = jnp.where(seen, p, 0.0)
                lows.append(p.astype(BF16))
                ds.append((p * (dp - delta[h : h + 1, :])).astype(BF16))
            dv_s[...] += dot_nn(jnp.concatenate(lows, axis=1), jnp.concatenate(g_h, axis=0))
            dk_s[...] += dot_nn(jnp.concatenate(ds, axis=1), jnp.concatenate(q_h, axis=0))
            for h in range(heads):
                lo, hi = h * HEAD_DIM, (h + 1) * HEAD_DIM
                dqt_s[i, lo:hi, :] += dot_nn(kt_s[j, lo:hi, :], ds[h])

        def masked_step(i, c):
            step(i, True)
            return c

        def open_step(i, c):
            step(i, False)
            return c

        lax.fori_loop(jnp.minimum(first, also), 2 * j + 2, masked_step, 0)
        lax.fori_loop(2 * j + 2, blocks, open_step, 0)
        for part in range(2):
            b = 2 * j + part
            t = part_of(info_ref, b // per_chunk, tensor)
            here = pl.ds(lax.rem(b, per_chunk) * blk, blk)
            side = slice(part * blk, (part + 1) * blk)
            dqkv_ref[t, here, padded : 2 * padded] = dk_s[side, :].astype(BF16)
            dqkv_ref[t, here, 2 * padded : 3 * padded] = dv_s[side, :].astype(BF16)
        bias_ref[1:2, :] = bias_ref[1:2, :] + jnp.sum(dv_s[...], axis=0, keepdims=True)
        return carry

    lax.fori_loop(0, blocks // 2, one_pair, 0)

    def one_query(i, carry):
        dq = dqt_s[i].T * scale
        t = part_of(info_ref, i // per_chunk, tensor)
        here = pl.ds(lax.rem(i, per_chunk) * blk, blk)
        dqkv_ref[t, here, 0:padded] = dq.astype(BF16)
        bias_ref[0:1, :] = bias_ref[0:1, :] + jnp.sum(dq, axis=0, keepdims=True)
        return carry

    lax.fori_loop(0, blocks, one_query, 0)


def attend_backward(info, chunks, grads, mixed, lse, heads):
    tensor = len(chunks)
    rows, width = chunks[0].shape
    padded = width // 3
    seq, blk = tensor * rows, PIECE_BLOCK
    blocks = seq // blk
    smem = pl.BlockSpec(memory_space=pltpu.SMEM)
    vmem = pl.BlockSpec(memory_space=pltpu.VMEM)
    return pl.pallas_call(
        functools.partial(attend_backward_kernel, heads),
        out_shape=(
            jax.ShapeDtypeStruct((tensor, rows, width), BF16),
            jax.ShapeDtypeStruct((8, padded), F32),
        ),
        in_specs=[smem] + [vmem] * (2 * tensor + 2),
        out_specs=(vmem, vmem),
        scratch_shapes=[
            pltpu.VMEM((heads, blocks, blk, padded), BF16),
            pltpu.VMEM((blocks // 2, 2 * blk, padded), BF16),
            pltpu.VMEM((blocks // 2, padded, 2 * blk), BF16),
            pltpu.VMEM((blocks // 2, 2 * blk, padded), BF16),
            pltpu.VMEM((heads, blocks, blk, padded), BF16),
            pltpu.VMEM((blocks, 8, blk), F32),
            pltpu.VMEM((blocks, padded, blk), F32),
            pltpu.VMEM((2 * blk, padded), F32),
            pltpu.VMEM((2 * blk, padded), F32),
        ],
        compiler_params=pltpu.CompilerParams(vmem_limit_bytes=VMEM_LIMIT),
        cost_estimate=LIGHT,
        name="attend_backward",
    )(info, *chunks, *grads, mixed, lse)


def start_weights(pieces, w_s, wo_s, sems, o_sem):
    wide = w_s.shape[2]
    copies = []
    t = 0
    for piece in pieces:
        blocks, parts, rows, _ = piece.shape
        for part in range(parts):
            for n in range(blocks):
                copies.append((piece.at[n, part], t, pl.ds(n * rows, rows)))
            t += 1
    for source, t, here in copies:
        pltpu.make_async_copy(source.at[:, wide:], wo_s.at[t, here, :], o_sem).start()
    for source, t, here in copies:
        pltpu.make_async_copy(source.at[:, :wide], w_s.at[t, here, :], sems.at[t]).start()


def center(values):
    mean = jnp.mean(values, axis=-1, keepdims=True)
    centered = values - mean
    spread = jnp.mean(centered * centered, axis=-1, keepdims=True)
    return centered, lax.rsqrt(spread + NORM_EPS)


def same_head(value):
    row = lax.broadcasted_iota(jnp.int32, (value, value), 0) // (value // POOL_HEADS)
    col = lax.broadcasted_iota(jnp.int32, (value, value), 1) // (value // POOL_HEADS)
    return (row == col).astype(F32)


def rows_forward_kernel(tensor, arrays, info_ref, *refs):
    mixed = refs[:tensor]
    tok_ref, vec_ref, bias_ref, proj_ref, cvec_ref = refs[tensor : tensor + 5]
    pieces = refs[tensor + 5 : tensor + 5 + arrays]
    (
        low_ref, xlow_ref, act_ref, slope_ref, xh1_ref, xh2_ref, rs_ref, stud_ref, mall_ref,
        e_ref, stats_ref, acc_s, w_s, wo_s, sems, o_sem,
    ) = refs[tensor + 5 + arrays :]
    j = pl.program_id(0)
    hidden = act_ref.shape[2]

    @pl.when(j == 0)
    def _():
        start_weights(pieces, w_s, wo_s, sems, o_sem)
        total = tok_ref[...].astype(F32) + vec_ref[2:3, :]
        pltpu.make_async_copy(wo_s, wo_s, o_sem).wait()
        for s in range(tensor):
            piece = mixed[s][...]
            mall_ref[s] = piece
            total = total + dot_nt(piece, wo_s[s])
        centered, rstd = center(total)
        xhat = centered * rstd
        xh1_ref[...] = xhat
        rs_ref[:, 0:1] = rstd
        x_one = xhat * vec_ref[3:4, :] + vec_ref[4:5, :]
        xlow_ref[...] = x_one.astype(BF16)
        acc_s[...] = x_one + vec_ref[5:6, :]

    pltpu.make_async_copy(w_s.at[j], w_s.at[j], sems.at[j]).wait()
    upper = dot_nn(xlow_ref[...], w_s[j, :, 0:hidden]) + bias_ref[0]
    phi = 0.5 * (1.0 + lax.erf(upper * (0.5**0.5)))
    act = (upper * phi).astype(BF16)
    slope = phi + upper * (jnp.exp(-0.5 * upper * upper) * 0.3989422804014327)
    act_ref[0] = act
    slope_ref[0] = slope.astype(BF16)
    acc_s[...] = acc_s[...] + dot_nt(act, w_s[j, :, hidden:])

    @pl.when(j == pl.num_programs(0) - 1)
    def _():
        centered, rstd = center(acc_s[...])
        xhat = centered * rstd
        xh2_ref[...] = xhat
        rs_ref[:, 1:2] = rstd
        low = (xhat * vec_ref[6:7, :] + vec_ref[7:8, :]).astype(BF16)
        low_ref[...] = low
        student = dot_nn(low, proj_ref[...]) + cvec_ref[0:1, :]
        stud_ref[...] = student
        width = student.shape[1]
        scale = (width // POOL_HEADS) ** (-0.5)
        e = dot_nn(student * (cvec_ref[1:2, :] * scale), same_head(width), PRECISE)
        e_ref[...] = e
        top = jnp.max(e, axis=0, keepdims=True)
        w = jnp.exp(e - top)
        stats_ref[...] = jnp.concatenate(
            [
                top,
                jnp.sum(w, axis=0, keepdims=True),
                jnp.sum(w * student, axis=0, keepdims=True),
                jnp.zeros((5, width), F32),
            ],
            axis=0,
        )


def whole(*shape):
    return pl.BlockSpec(shape, lambda j, *_: (0,) * len(shape))


def block(*shape):
    return pl.BlockSpec((1,) + shape, lambda j, *_: (j,) + (0,) * len(shape))


def rows_forward(info, pieces, mixed, tokens, vec_table, ff_bias, cls_proj, cls_vec):
    tensor = len(mixed)
    rows, width = tokens.shape
    head_width = mixed[0].shape[1]
    hidden = ff_bias.shape[2]
    ch = cls_proj.shape[1]
    far = pl.BlockSpec(memory_space=pl.ANY)

    def of_block(j, info_ref):
        return (part_of(info_ref, j, tensor), 0, 0)

    return pl.pallas_call(
        functools.partial(rows_forward_kernel, tensor, len(pieces)),
        grid_spec=pltpu.PrefetchScalarGridSpec(
            num_scalar_prefetch=1,
            grid=(tensor,),
            in_specs=[whole(rows, head_width)] * tensor
            + [
                whole(rows, width),
                whole(8, width),
                pl.BlockSpec((1, 1, hidden), of_block),
                whole(width, ch),
                whole(3, ch),
            ]
            + [far] * len(pieces),
            out_specs=(
                whole(rows, width),
                whole(rows, width),
                block(rows, hidden),
                block(rows, hidden),
                whole(rows, width),
                whole(rows, width),
                whole(rows, 2),
                whole(rows, ch),
                whole(tensor, rows, head_width),
                whole(rows, ch),
                whole(8, ch),
            ),
            scratch_shapes=[
                pltpu.VMEM((rows, width), F32),
                pltpu.VMEM((tensor, width, 2 * hidden), BF16),
                pltpu.VMEM((tensor, width, head_width), BF16),
                pltpu.SemaphoreType.DMA((tensor,)),
                pltpu.SemaphoreType.DMA,
            ],
        ),
        out_shape=(
            jax.ShapeDtypeStruct((rows, width), BF16),
            jax.ShapeDtypeStruct((rows, width), BF16),
            jax.ShapeDtypeStruct((tensor, rows, hidden), BF16),
            jax.ShapeDtypeStruct((tensor, rows, hidden), BF16),
            jax.ShapeDtypeStruct((rows, width), F32),
            jax.ShapeDtypeStruct((rows, width), F32),
            jax.ShapeDtypeStruct((rows, 2), F32),
            jax.ShapeDtypeStruct((rows, ch), F32),
            jax.ShapeDtypeStruct((tensor, rows, head_width), BF16),
            jax.ShapeDtypeStruct((rows, ch), F32),
            jax.ShapeDtypeStruct((8, ch), F32),
        ),
        compiler_params=pltpu.CompilerParams(vmem_limit_bytes=VMEM_LIMIT),
        cost_estimate=LIGHT,
        name="rows_forward",
    )(info, *mixed, tokens, vec_table, ff_bias, cls_proj, cls_vec, *pieces)


def norm_back(grad, xhat, rstd, gain):
    g = grad * gain
    return (
        g - jnp.mean(g, axis=-1, keepdims=True) - xhat * jnp.mean(g * xhat, axis=-1, keepdims=True)
    ) * rstd


def rows_backward_kernel(tensor, arrays, info_ref, *refs):
    stats_refs = refs[:tensor]
    (
        stud_ref, e_ref, cot_ref, xh1_ref, xh2_ref, rs_ref, slope_ref, vec_ref, proj_ref,
        cvec_ref, chid_ref, cout_ref, cbias_ref,
    ) = refs[tensor : tensor + 13]
    pieces = refs[tensor + 13 : tensor + 13 + arrays]
    (
        logit_ref, two_ref, gu_ref, one_ref, gh1_ref, gm_ref, gsl_ref, pack_ref, acc_s, w_s, wo_s,
        sems, o_sem,
    ) = refs[tensor + 13 + arrays :]
    j = pl.program_id(0)
    ch = stud_ref.shape[1]
    hidden = gu_ref.shape[2]
    scale = (ch // POOL_HEADS) ** (-0.5)
    width = cot_ref.shape[1]
    sums_at = 8 + 2 * ch
    bias_at = sums_at + 6 * (width // ch)

    def pack_row(row, value):
        at = sums_at + (row - 2) * (width // ch)
        for n in range(width // ch):
            pack_ref[at + n : at + n + 1, :] = value[:, n * ch : (n + 1) * ch]

    @pl.when(j == 0)
    def _():
        start_weights(pieces, w_s, wo_s, sems, o_sem)
        head_of = same_head(ch)
        first = (info_ref[INFO_Z] == 0).astype(F32)
        stats = [r[...] for r in stats_refs]
        top = functools.reduce(jnp.maximum, [v[0:1, :] for v in stats])
        weights = [jnp.exp(v[0:1, :] - top) for v in stats]
        total = sum(v[1:2, :] * w for v, w in zip(stats, weights))
        pooled = sum(v[2:3, :] * w for v, w in zip(stats, weights)) / total

        first_row = lax.broadcasted_iota(jnp.int32, (8, ch), 0) == 0
        lane = lax.broadcasted_iota(jnp.int32, (8, ch), 1)
        pooled8 = jnp.broadcast_to(pooled, (8, ch))
        chid = chid_ref[...].astype(F32)
        cout = cout_ref[...].astype(F32)
        hid = jnp.tanh(dot_nn(pooled8, chid, PRECISE) + cvec_ref[2:3, :])
        logits = dot_nn(hid, cout, PRECISE) + cbias_ref[...]
        logit_ref[...] = logits
        real = lane < CLASSES
        masked = jnp.where(real, logits, MASK_FILL)
        powers = jnp.where(real, jnp.exp(masked - jnp.max(masked, axis=1, keepdims=True)), 0.0)
        probs = powers / jnp.sum(powers, axis=1, keepdims=True)
        grad_logits = probs - (lane == info_ref[INFO_LABEL]).astype(F32)
        grad_pre = (1.0 - hid * hid) * dot_nt(grad_logits, cout, PRECISE)
        grad_pooled = dot_nt(grad_pre, chid, PRECISE)
        gl_row = jnp.where(first_row, grad_logits, 0.0) * first
        gp_row = jnp.where(first_row, grad_pre, 0.0) * first
        pack_ref[8 : 8 + ch, :] = dot_tn(pooled8, gp_row, PRECISE)
        pack_ref[8 + ch : 8 + 2 * ch, :] = dot_tn(hid, gl_row, PRECISE)
        base = dot_nn(grad_pooled * pooled8, head_of, PRECISE)[0:1, :]
        gp = grad_pooled[0:1, :]
        query = cvec_ref[1:2, :] * scale
        student = stud_ref[...]
        w = jnp.exp(e_ref[...] - top) / total
        grad_w = dot_nn(student * gp, head_of, PRECISE)
        grad_e = w * (grad_w - base)
        grad_student = w * gp + grad_e * query
        gsl = grad_student.astype(BF16)
        gsl_ref[...] = gsl
        pack_ref[0:8, :] = jnp.concatenate(
            [
                jnp.sum(grad_student, axis=0, keepdims=True),
                jnp.sum(grad_e * student, axis=0, keepdims=True) * scale,
                gp_row[0:1, :],
                gl_row[0:1, :],
                jnp.zeros((4, ch), F32),
            ],
            axis=0,
        )
        grad = cot_ref[...].astype(F32) + dot_nt(gsl, proj_ref[...])
        xhat = xh2_ref[...]
        pack_row(6, jnp.sum(grad * xhat, axis=0, keepdims=True))
        pack_row(7, jnp.sum(grad, axis=0, keepdims=True))
        two = norm_back(grad, xhat, rs_ref[:, 1:2], vec_ref[6:7, :])
        pack_row(5, jnp.sum(two, axis=0, keepdims=True))
        acc_s[...] = two
        two_ref[...] = two.astype(BF16)

    pltpu.make_async_copy(w_s.at[j], w_s.at[j], sems.at[j]).wait()
    upper = dot_nn(two_ref[...], w_s[j, :, hidden:]) * slope_ref[0].astype(F32)
    heads_row = part_of(info_ref, j, tensor)
    bias_row = jnp.sum(upper, axis=0, keepdims=True)
    for n in range(hidden // ch):
        pack_ref[pl.ds(bias_at + heads_row * (hidden // ch) + n, 1), :] = bias_row[
            :, n * ch : (n + 1) * ch
        ]
    low = upper.astype(BF16)
    gu_ref[0] = low
    acc_s[...] = acc_s[...] + dot_nt(low, w_s[j, :, 0:hidden])

    @pl.when(j == pl.num_programs(0) - 1)
    def _():
        grad = acc_s[...]
        xhat = xh1_ref[...]
        pack_row(3, jnp.sum(grad * xhat, axis=0, keepdims=True))
        pack_row(4, jnp.sum(grad, axis=0, keepdims=True))
        one = norm_back(grad, xhat, rs_ref[:, 0:1], vec_ref[3:4, :])
        pack_row(2, jnp.sum(one, axis=0, keepdims=True))
        gh1_ref[...] = one
        low = one.astype(BF16)
        one_ref[...] = low
        pltpu.make_async_copy(wo_s, wo_s, o_sem).wait()
        for s in range(tensor):
            gm_ref[s] = dot_nn(low, wo_s[s]).astype(BF16)


def rows_backward(
    info, pieces, stats, kept, cotangent, vec_table, cls_proj, cls_vec, cls_hidden,
    cls_out, cls_bias,
):
    _, _, _, slope, xh1, xh2, rs, student, mixed, pool_logit, _ = kept
    tensor, rows, hidden = slope.shape
    width = xh1.shape[1]
    head_width = mixed.shape[2]
    ch = student.shape[1]
    far = pl.BlockSpec(memory_space=pl.ANY)
    pack_rows = 8 + 2 * ch + (6 * width + tensor * hidden) // ch

    return pl.pallas_call(
        functools.partial(rows_backward_kernel, tensor, len(pieces)),
        grid_spec=pltpu.PrefetchScalarGridSpec(
            num_scalar_prefetch=1,
            grid=(tensor,),
            in_specs=[whole(8, ch)] * tensor
            + [
                whole(rows, ch),
                whole(rows, ch),
                whole(rows, width),
                whole(rows, width),
                whole(rows, width),
                whole(rows, 2),
                block(rows, hidden),
                whole(8, width),
                whole(width, ch),
                whole(3, ch),
                whole(ch, ch),
                whole(ch, ch),
                whole(1, ch),
            ]
            + [far] * len(pieces),
            out_specs=(
                whole(8, ch),
                whole(rows, width),
                block(rows, hidden),
                whole(rows, width),
                whole(rows, width),
                whole(tensor, rows, head_width),
                whole(rows, ch),
                whole(pack_rows, ch),
            ),
            scratch_shapes=[
                pltpu.VMEM((rows, width), F32),
                pltpu.VMEM((tensor, width, 2 * hidden), BF16),
                pltpu.VMEM((tensor, width, head_width), BF16),
                pltpu.SemaphoreType.DMA((tensor,)),
                pltpu.SemaphoreType.DMA,
            ],
        ),
        out_shape=(
            jax.ShapeDtypeStruct((8, ch), F32),
            jax.ShapeDtypeStruct((rows, width), BF16),
            jax.ShapeDtypeStruct((tensor, rows, hidden), BF16),
            jax.ShapeDtypeStruct((rows, width), BF16),
            jax.ShapeDtypeStruct((rows, width), F32),
            jax.ShapeDtypeStruct((tensor, rows, head_width), BF16),
            jax.ShapeDtypeStruct((rows, ch), BF16),
            jax.ShapeDtypeStruct((pack_rows, ch), F32),
        ),
        compiler_params=pltpu.CompilerParams(vmem_limit_bytes=VMEM_LIMIT),
        cost_estimate=LIGHT,
        name="rows_backward",
    )(
        info, *stats, student, pool_logit, cotangent, xh1, xh2, rs, slope, vec_table, cls_proj,
        cls_vec, cls_hidden, cls_out, cls_bias, *pieces,
    )


def weight_grads_kernel(
    dp, shard, info_ref, x_ref, two_ref, one_ref, gu_ref, act_ref, mix_ref, low_ref, gsl_ref,
    *refs,
):
    outs, proj_ref = refs[:-4], refs[-4]
    lefts = refs[-3:]
    j = pl.program_id(0)
    hidden = gu_ref.shape[2]
    width = x_ref.shape[1]
    apart = len(outs) == 2

    @pl.when(j == 0)
    def _():
        for source, left in zip((x_ref, two_ref, one_ref), lefts):
            turned = source[...].T
            if not apart:
                left[...] = turned
                continue
            for b in range(dp):
                offset = jnp.bitwise_xor(info_ref[INFO_D], b)
                at = lax.rem(offset, 2) * (dp // 2) + offset // 2
                left[pl.ds(at * shard, shard), :] = turned[b * shard : (b + 1) * shard, :]
        proj_ref[...] = dot_tn(low_ref[...], gsl_ref[...])

    count = width // len(outs)
    rights = (gu_ref[0], act_ref[0], mix_ref[0])
    ends = (0, hidden, 2 * hidden, 2 * hidden + mix_ref.shape[2])
    for n, out in enumerate(outs):
        here = slice(n * count, (n + 1) * count)
        for m in range(3):
            part = dot_nn(lefts[m][here, :], rights[m]).astype(BF16)
            out[0, :, :, ends[m] : ends[m + 1]] = part.reshape(
                out.shape[1], out.shape[2], ends[m + 1] - ends[m]
            )


def weight_grads(
    info, dp, shard, x_low, two_low, one_low, upper_low, act, mixed, out_low, student_low
):
    tensor, rows, hidden = upper_low.shape
    width = x_low.shape[1]
    head_width = mixed.shape[2]
    ch = student_low.shape[1]
    total = 2 * hidden + head_width
    if shard % 16:
        parts = [(1, width)]
    else:
        parts = [(dp // 2, shard)] * 2
    return pl.pallas_call(
        functools.partial(weight_grads_kernel, dp, shard),
        grid_spec=pltpu.PrefetchScalarGridSpec(
            num_scalar_prefetch=1,
            grid=(tensor,),
            in_specs=[
                whole(rows, width),
                whole(rows, width),
                whole(rows, width),
                block(rows, hidden),
                block(rows, hidden),
                block(rows, head_width),
                whole(rows, width),
                whole(rows, ch),
            ],
            out_specs=tuple(block(*part, total) for part in parts) + (whole(width, ch),),
            scratch_shapes=[pltpu.VMEM((width, rows), BF16)] * 3,
        ),
        out_shape=tuple(jax.ShapeDtypeStruct((tensor, *part, total), BF16) for part in parts)
        + (jax.ShapeDtypeStruct((width, ch), F32),),
        compiler_params=pltpu.CompilerParams(vmem_limit_bytes=VMEM_LIMIT),
        cost_estimate=LIGHT,
        name="weight_grads",
    )(info, x_low, two_low, one_low, upper_low, act, mixed, out_low, student_low)


def weights_to_owner(parts, dp, tensor, z):
    if len(parts) == 1:
        order = (z - jnp.arange(tensor)) % tensor
        whole_parts = jnp.take(parts[0], order, axis=0)
        owned = lax.psum_scatter(
            whole_parts.reshape(-1, whole_parts.shape[-1]), ("tensor", "dp"),
            scatter_dimension=0, tiled=True,
        ).astype(F32)

        def done(came, late):
            yield (), owned
            return owned

        return (), (), lambda sent: (), done
    keep, give = parts
    bits = bits_of(dp)
    got = swapped(give, "dp", dp, bits[0])
    half = tensor // 2
    orders = (bits[1:], bits[1:][::-1])
    sides = [slice(0, half), slice(half, tensor)]
    sent = []
    for side, order in zip(sides, orders):
        value = split_by(keep[side], bits[1:], order[0], 1).astype(F32)
        value = value + split_by(got[side], bits[1:], order[0], 1).astype(F32)
        sent.append(value.astype(BF16))

    def first(sent):
        return [swapped(sent[k], "dp", dp, orders[k][0]) for k in range(2)]

    def finish(came, late):
        sent = None
        values, lefts = [], [list(bits[1:]), list(bits[1:])]
        for side, order in zip(sides, orders):
            value = split_by(keep[side], bits[1:], order[0], 0).astype(F32)
            values.append(value + split_by(late[side], bits[1:], order[0], 0).astype(F32))
        for n in range(len(bits) - 1):
            if n:
                came = [swapped(sent[k], "dp", dp, orders[k][n]) for k in range(2)]
                came = yield sent, came
            sent = []
            for k in range(2):
                value = values[k] + came[k].astype(F32)
                lefts[k].remove(orders[k][n])
                if n + 2 < len(bits):
                    bit = orders[k][n + 1]
                    sent.append(split_by(value, lefts[k], bit, 1).astype(BF16))
                    value = split_by(value, lefts[k], bit, 0)
                values[k] = value
        own = [value[t, 0] for value in values for t in range(half)]
        total = own[1]
        for t in list(range(2, tensor)) + [0]:
            total = total.astype(BF16)
            came = yield total, shifted(total, "tensor", tensor, 1)
            total = own[t] + came.astype(F32)
        return total

    return sent, got, first, finish


def split_by(value, left, bit, side):
    shape = value.shape
    place = left.index(bit)
    low, high = 1 << place, 1 << (len(left) - 1 - place)
    pairs = value.reshape(shape[0], high, 2, low, *shape[2:])
    return pairs[:, :, side].reshape(shape[0], high * low, *shape[2:])


def first_rows_kernel(d_ref, w_ref, out_ref):
    out_ref[...] = dot_nt(d_ref[0], w_ref[...]).astype(BF16)


def first_rows(d_chunks, w_in):
    _, rows, width = d_chunks.shape
    return pl.pallas_call(
        first_rows_kernel,
        grid=(1,),
        out_shape=jax.ShapeDtypeStruct((rows, w_in.shape[0]), BF16),
        in_specs=[
            pl.BlockSpec((1, rows, width), lambda n: (1, 0, 0)),
            whole(*w_in.shape),
        ],
        out_specs=whole(rows, w_in.shape[0]),
        compiler_params=pltpu.CompilerParams(vmem_limit_bytes=VMEM_LIMIT),
        cost_estimate=LIGHT,
        name="first_rows",
    )(d_chunks, w_in)


def other_rows_kernel(tensor, d_ref, w_ref, *refs):
    seq_refs, (out_ref, grad_ref) = refs[:tensor], refs[tensor:]
    n = pl.program_id(0)
    for t in range(tensor):

        @pl.when(n == t)
        def _():
            part = dot_tn(seq_refs[t][...], d_ref[0])
            if t == 0:
                grad_ref[...] = part
            else:
                grad_ref[...] += part

    out_ref[0] = dot_nt(d_ref[0], w_ref[...]).astype(BF16)


def other_rows(d_chunks, w_in, seq_rows):
    tensor, rows, width = d_chunks.shape
    model = w_in.shape[0]
    return pl.pallas_call(
        functools.partial(other_rows_kernel, tensor),
        grid=(tensor,),
        out_shape=(
            jax.ShapeDtypeStruct((tensor, rows, model), BF16),
            jax.ShapeDtypeStruct((model, width), F32),
        ),
        in_specs=[block(rows, width), whole(*w_in.shape)] + [whole(rows, model)] * tensor,
        out_specs=(block(rows, model), whole(model, width)),
        compiler_params=pltpu.CompilerParams(vmem_limit_bytes=VMEM_LIMIT),
        cost_estimate=LIGHT,
        name="other_rows",
    )(d_chunks, w_in, *seq_rows)


def per_device(
    dp, tensor, tokens, cotangent, labels, piece_start, piece_len, w_qkv, w_out, w_up, w_down,
    vec_table, ff_bias, cls_proj, cls_vec, cls_hidden, cls_out, cls_bias,
):
    rows, width = tokens.shape
    local = w_qkv.shape[2]
    heads = local // HEAD_DIM
    padded = -(-local // LANES) * LANES
    shard = w_qkv.shape[0]
    hidden = w_up.shape[1]
    ch = cls_proj.shape[1]
    z = lax.axis_index("tensor")
    info = jnp.concatenate(
        [z.reshape(1), lax.axis_index("dp").reshape(1), labels, piece_start[0], piece_len[0]]
    ).astype(jnp.int32)

    extra = padded - local
    qkv_shard = jnp.pad(w_qkv, ((0, 0), (0, 0), (0, extra))).reshape(shard, 3 * padded)
    ff_ring, seq_rows = [], []
    ff_shard = jnp.concatenate([w_up, w_down.T, w_out.T], axis=1)
    _, _, w_in = in_turn(
        vec_table[0, 0],
        {
            "rows": ring_chain(tokens, tensor, seq_rows),
            "ff": ring_chain(ff_shard, tensor, ff_ring),
            "in": gather_chain(qkv_shard, "dp", dp),
        },
        [("in",), ("in", "ff"), ("in",), ("ff",), ("rows",), ("ff",), ("rows",), ("rows",)],
    )
    half = tensor // 2
    pieces = [
        lax.all_gather(jnp.stack(ff_ring[n : n + half]), "dp") for n in (0, half)
    ]
    if shard % 16:
        pieces = [
            p.transpose(1, 0, 2, 3).reshape(1, half, dp * shard, p.shape[-1]) for p in pieces
        ]

    q_bias = lax.dynamic_slice_in_dim(vec_table[0], z * local, local, 0)
    v_bias = lax.dynamic_slice_in_dim(vec_table[1], z * local, local, 0)
    in_bias = jnp.pad(
        jnp.stack([q_bias, jnp.zeros_like(q_bias), v_bias]), ((0, 0), (0, extra))
    ).reshape(1, 3 * padded)

    def exchanged(parts):
        return [parts[0]] + [
            shifted(parts[tensor - s], "tensor", tensor, s) for s in range(1, tensor)
        ]

    chunks = [
        (jnp.dot(part, w_in, preferred_element_type=F32) + in_bias).astype(BF16)
        for part in seq_rows
    ]
    mixed, lse = attend_forward(info, chunks, heads)
    kept = rows_forward(
        info, pieces, exchanged(mixed), tokens, vec_table,
        ff_bias.reshape(tensor, 1, hidden), cls_proj, cls_vec,
    )
    out_low, x_low, act, _, _, _, _, _, mixed_all, _, stats = kept
    all_stats = exchanged([stats] * tensor)
    (
        logits, two_low, upper_low, one_low, grad_h_one, grad_mixed, student_low, pack,
    ) = rows_backward(
        info, pieces, all_stats, kept, cotangent, vec_table, cls_proj, cls_vec,
        cls_hidden, jnp.pad(cls_out, ((0, 0), (0, ch - CLASSES))),
        jnp.pad(cls_bias, (0, ch - CLASSES)).reshape(1, ch),
    )
    grad_rows = exchanged(grad_mixed)
    *ff_parts, grad_proj = weight_grads(
        info, dp, shard, x_low, two_low, one_low, upper_low, act, mixed_all, out_low, student_low
    )
    small = jnp.concatenate([grad_proj, pack], axis=0).astype(BF16)
    bits = bits_of(tensor)
    small_came = swapped(small, "tensor", tensor, bits[0])
    sent, got, first, finish = weights_to_owner(ff_parts, dp, tensor, z)
    sent, grad_rows, small_came = lax.optimization_barrier((sent, grad_rows, small_came))
    small = small + small_came
    small, grad_rows = lax.optimization_barrier((small, grad_rows))
    small_came = swapped(small, "tensor", tensor, bits[1])

    d_chunks, bias_sums = attend_backward(info, chunks, grad_rows, mixed, lse, heads)
    d_chunks, bias_sums, came, late, small_came = lax.optimization_barrier(
        (d_chunks, bias_sums, first(sent), got, small_came)
    )
    first_part = first_rows(d_chunks, w_in)
    came, late = after((came, late), first_part)

    def small_chain():
        total = small + small_came
        for bit in bits[2:]:
            got = yield total, swapped(total, "tensor", tensor, bit)
            total = total + got
        for bit in bits_of(dp):
            got = yield total, swapped(total, "dp", dp, bit)
            total = total + got
        return total.astype(F32)

    shared = {}

    def rows_chain():
        total = first_part
        for t in range(2, tensor):
            came = yield total, shifted(total, "tensor", tensor, 1)
            total = (shared["parts"][t].astype(F32) + came.astype(F32)).astype(BF16)
        came = yield total, shifted(total, "tensor", tensor, 1)
        return grad_h_one + shared["parts"][0].astype(F32) + came.astype(F32)

    def in_chain():
        later = yield (), d_chunks
        shared["parts"], grad = other_rows(later, w_in, seq_rows)
        grad = yield (), grad
        rider = jnp.pad(bias_sums, ((0, 8), (0, 2 * padded)))
        return (
            yield from owner_chain(
                grad.reshape(dp, shard, 3 * padded), rider, "dp", dp, "tensor", tensor
            )
        )

    grad_tokens, ff_own, (grad_in, riders), sums = in_turn(
        bias_sums[0, 0],
        {
            "rows": rows_chain(),
            "ff": finish(came, late),
            "in": in_chain(),
            "small": small_chain(),
        },
        [
            ("in",), ("rows",), ("in",), ("small",), ("ff",), ("in",), ("small",), ("rows",),
            ("ff",), ("in",), ("small",), ("ff",), ("in",), ("small",), ("ff",), ("in",), ("rows",),
        ],
    )
    grad_w_qkv = grad_in.reshape(shard, 3, padded)[:, :, :local]
    bias_sum = riders[:, :2, :local].transpose(1, 0, 2).reshape(2, width)

    proj_sum, pack_sum = sums[:width], sums[width:]
    hid_sum = pack_sum[8 : 8 + ch]
    out_w_sum = pack_sum[8 + ch : 8 + 2 * ch, :CLASSES]
    at = 8 + 2 * ch
    vec_sum = pack_sum[at : at + 6 * width // ch].reshape(6, width)
    ff_bias_sum = pack_sum[at + 6 * width // ch :].reshape(-1)
    return (
        out_low,
        logits[0:1, :CLASSES],
        grad_tokens,
        grad_w_qkv,
        ff_own[:, 2 * hidden :].T,
        ff_own[:, :hidden],
        ff_own[:, hidden : 2 * hidden].T,
        jnp.concatenate([bias_sum, vec_sum], axis=0),
        ff_bias_sum,
        proj_sum,
        pack_sum[:3],
        hid_sum,
        out_w_sum,
        pack_sum[3, :CLASSES],
    )


def solution(mesh):
    dp, tensor = mesh.shape["dp"], mesh.shape["tensor"]
    rows = P(("dp", "tensor"), None)
    cut = P("dp", "tensor")
    turned_cut = P("tensor", "dp")
    return jax.shard_map(
        functools.partial(per_device, dp, tensor),
        mesh=mesh,
        in_specs=(
            rows, rows, P("dp"), P("dp", None), P("dp", None), P("dp", None, "tensor"),
            turned_cut, cut, turned_cut, P(), P(), P(), P(), P(), P(), P(),
        ),
        out_specs=(
            rows, P("dp", None), rows, P("dp", None, "tensor"), turned_cut, cut, turned_cut,
            P(), P(), P(), P(), P(), P(), P(),
        ),
        check_vma=False,
    )
```

time: 475 us -> 394 us (0.83)
  the two profiles are of different devices: /device:TPU:0 before, /device:TPU:8 now
where the time goes in v2:
time: 394 us; the launch traced here: 387 us
  waiting for transfers between devices  140 us (36%)
  Pallas kernels  109 us (28%)
  starting transfers between devices  46.1 us (12%)
  local copies, waits for them, and re-layouts  41 us (10%)
  other arithmetic  30.2 us (8%)
  between operations  16 us (4%)
  matrix products  4.54 us (1%)
    ppermute x24, waiting for transfers between devices, shifted(): lax.ppermute(value, axis, [(i, (i + by) % size) for i in range(size)])  124 us
    ppermute x24, starting transfers between devices, shifted(): lax.ppermute(value, axis, [(i, (i + by) % size) for i in range(size)])  34.3 us
    pallas_call x1, Pallas kernels, attend_backward(): pl.pallas_call(functools.partial(attend_backward_kernel, heads), out_shap...  31.1 us
    unnamed x117, local copies, waits for them, and re-layouts  23.9 us
    pallas_call x1, Pallas kernels, attend_forward(): pl.pallas_call(functools.partial(attend_forward_kernel, heads), out_shape...  21.6 us
    pallas_call x1, Pallas kernels, rows_forward(): pl.pallas_call(functools.partial(rows_forward_kernel, tensor, len(pieces)...  17.4 us
    pallas_call x1, Pallas kernels, rows_backward(): pl.pallas_call(functools.partial(rows_backward_kernel, tensor, len(pieces...  16.6 us
    ppermute x16, waiting for transfers between devices, swapped(): return lax.ppermute(value, axis, [(i, i ^ bit) for i in range(size)])  16 us
  transfers between devices with their start and end apart: 42, of which 18 were waited for; matrix products, arithmetic and copies ran while one was open for 13% of the time, Pallas kernels for 16%

profile of v2, /device:TPU:8, one launch (start us, length us, event | category | flops | bytes accessed | tf_op | source)
XLA Modules:
  0.0 387.1 jit_solution(14242590455880870685)
XLA Ops:
  13.7 7.3 %collective-permute-done.2 = bf16[96,1728]{1,0:T(8,128)(2,1)S(1)} collective-permute-done((bf16[96,1728]{1,0:T(8,128)(2,1)S(1)}, bf16[96,1728]{1,0:T(8,128)(2,1)S(1)}, u32[]{:S(2)}, u32[]{:S(2)}) %collective-permute-start.2) | collective-permute-done | bytes 331808 | tf_op jit(solution)/shard_map/ppermute | solution.py:51
  25.2 24.2 %collective-permute-done.5 = bf16[96,1728]{1,0:T(8,128)(2,1)S(1)} collective-permute-done((bf16[96,1728]{1,0:T(8,128)(2,1)S(1)}, bf16[96,1728]{1,0:T(8,128)(2,1)S(1)}, u32[]{:S(2)}, u32[]{:S(2)}) %collective-permute-start.5) | collective-permute-done | bytes 331808 | tf_op jit(solution)/shard_map/ppermute | solution.py:51
  50.2 10.0 %collective-permute-done.11 = bf16[96,1728]{1,0:T(8,128)(2,1)S(1)} collective-permute-done((bf16[96,1728]{1,0:T(8,128)(2,1)S(1)}, bf16[96,1728]{1,0:T(8,128)(2,1)S(1)}, u32[]{:S(2)}, u32[]{:S(2)}) %collective-permute-start.11) | collective-permute-done | bytes 331808 | tf_op jit(solution)/shard_map/ppermute | solution.py:51
  64.5 11.8 %collective-permute-done.3 = bf16[384,768]{1,0:T(8,128)(2,1)} collective-permute-done((bf16[384,768]{1,0:T(8,128)(2,1)}, bf16[384,768]{1,0:T(8,128)(2,1)}, u32[]{:S(2)}, u32[]{:S(2)}) %collective-permute-start.3) | collective-permute-done | bytes 589856 | tf_op jit(solution)/shard_map/ppermute | solution.py:47
  84.5 14.8 %collective-permute-done.7.refs_3_ = bf16[512,768]{1,0:T(8,128)(2,1)S(1)} collective-permute-done((bf16[512,768]{1,0:T(8,128)(2,1)}, bf16[512,768]{1,0:T(8,128)(2,1)S(1)}, u32[]{:S(2)}, u32[]{:S(2)}) %collective-permute-start.7) | collective-permute-done | bytes 786464 | tf_op jit(solution)/shard_map/ppermute | solution.py:51
  100.2 21.6 %attend_forward.1 = (bf16[4,512,192]{2,1,0:T(8,128)(2,1)S(1)}, f32[8,8,256]{2,1,0:T(8,128)S(1)}) custom-call(s32[7]{0:T(128)S(1)} %concatenate.43.info_ref, bf16[512,768]{1,0:T(8,128)(2,1)S(1)} %fusion.9.refs_0_, bf16[512,768]{1,0:T(8,128)(2,1)S(1)} %add_convert_fusion.4.refs_1_, bf16[512,768]{1,0:T(8,128)(2,1)S(1)} %add_convert_fusion.3.refs_2_, ...), custom_call_target="tpu_custom_call" | custom-call | flops 1024 | bytes 1024 | tf_op jit(solution)/shard_map/attend_forward/pallas_call | solution.py:240
  122.5 3.6 collective-permute-start.10
  128.7 12.9 %collective-permute-done.10.refs_3_ = bf16[512,192]{1,0:T(8,128)(2,1)S(1)} collective-permute-done((bf16[512,192]{1,0:T(8,128)(2,1)S(1)}, bf16[512,192]{1,0:T(8,128)(2,1)S(1)}, u32[]{:S(2)}, u32[]{:S(2)}) %collective-permute-start.10) | collective-permute-done | bytes 196640 | tf_op jit(solution)/shard_map/ppermute | solution.py:51
  147.4 17.4 %rows_forward.1 = (bf16[512,768]{1,0:T(8,128)(2,1)}, bf16[512,768]{1,0:T(8,128)(2,1)S(1)}, bf16[4,512,768]{2,1,0:T(8,128)(2,1)}, bf16[4,512,768]{2,1,0:T(8,128)(...) custom-call(s32[7]{0:T(128)S(1)} %concatenate.43.info_ref, ...), custom_call_target="tpu_custom_call" | custom-call | flops 1024 | bytes 1024 | tf_op jit(solution)/shard_map/rows_forward/pallas_call | solution.py:513
  169.3 4.0 %collective-permute-start.13 = (f32[8,128]{1,0:T(8,128)S(1)}, f32[8,128]{1,0:T(8,128)S(1)}, u32[]{:S(2)}, u32[]{:S(2)}) collective-permute-start(f32[8,128]{1,0:T(8,128)S(1)} %get-tuple-element.103.refs_0_), channel_id=1, source_target_pairs={{0,2},{1,3},{2,0},{3,1},{4,6},{5,7},{6,4},{7,5},{8,10},{9,11},{10,... | collective-permute-start | bytes 12296 | tf_op jit(solution)/shard_map/ppermute | solution.py:51
  180.9 16.6 %rows_backward.1 = (f32[8,128]{1,0:T(8,128)S(1)}, bf16[512,768]{1,0:T(8,128)(2,1)S(1)}, bf16[4,512,768]{2,1,0:T(8,128)(2,1)}, bf16[512,768]{1,0:T(8,128)(2,1)S(1...) custom-call(s32[7]{0:T(128)S(1)} %concatenate.43.info_ref, ...), custom_call_target="tpu_custom_call" | custom-call | flops 1024 | bytes 1024 | tf_op jit(solution)/shard_map/rows_backward/pallas_call | solution.py:697
  197.6 11.1 %weight_grads.1 = (bf16[4,4,96,1728]{3,2,1,0:T(8,128)(2,1)}, bf16[4,4,96,1728]{3,2,1,0:T(8,128)(2,1)}, f32[768,128]{1,0:T(8,128)S(1)}) custom-call(s32[7]{0:T(128)S(1)} %concatenate.43.info_ref, bf16[512,768]{1,0:T(8,128)(2,1)S(1)} %copy-done.19, bf16[512,768]{1,0:T(8,128)(2,1)S(1)} %get-tuple-element.113.two_ref, ...), custom_call_target="tpu_custom_call" | custom-call | flops 1024 | bytes 1024 | tf_op jit(solution)/shard_map/weight_grads/pallas_call | solution.py:804
  213.6 3.0 fusion.22
  224.0 10.5 %collective-permute-done.17.refs_6_ = bf16[512,192]{1,0:T(8,128)(2,1)S(1)} collective-permute-done((bf16[512,192]{1,0:T(8,128)(2,1)S(1)}, bf16[512,192]{1,0:T(8,128)(2,1)S(1)}, u32[]{:S(2)}, u32[]{:S(2)}) %collective-permute-start.17) | collective-permute-done | bytes 196640 | tf_op jit(solution)/shard_map/ppermute | solution.py:51
  240.3 31.1 %attend_backward.1 = (bf16[4,512,768]{2,1,0:T(8,128)(2,1)}, f32[8,256]{1,0:T(8,128)S(1)}) custom-call(s32[7]{0:T(128)S(1)} %concatenate.43.info_ref, bf16[512,768]{1,0:T(8,128)(2,1)S(1)} %copy-done.5, bf16[512,768]{1,0:T(8,128)(2,1)S(1)} %copy-done.3, bf16[512,768]{1,0:T(8,128)(2,1)S(1)} %copy-done.7, bf16[512,768]{1,0:T(8,128)(2,1)S(1)} %copy-done.9, ...), custom_call_target="tpu_custom_call" | custom-call | flops 1024 | bytes 1024 | tf_op jit(solution)/shard_map/attend_backward/pallas_call | solution.py:376
  278.3 2.8 fusion.1
  288.5 9.5 %other_rows.1 = (bf16[4,512,768]{2,1,0:T(8,128)(2,1)}, f32[768,768]{1,0:T(8,128)}) custom-call(bf16[4,512,768]{2,1,0:T(8,128)(2,1)} %get-tuple-element.148.d_ref, bf16[768,768]{1,0:T(8,128)(2,1)S(1)} %maximum_select_fusion.w_ref, bf16[512,768]{1,0:T(8,128)(2,1)S(1)} %copy-done.1, bf16[512,768]{1,0:T(8,128)(2,1)S(1)} %copy-done.14, ...), custom_call_target="tpu_custom_call" | custom-call | flops 1024 | bytes 1024 | tf_op jit(solution)/shard_map/other_rows/pallas_call | solution.py:937
  307.8 3.7 collective-permute-done.29
  311.9 8.2 %collective-permute-done.24 = bf16[512,768]{1,0:T(8,128)(2,1)S(1)} collective-permute-done((bf16[512,768]{1,0:T(8,128)(2,1)S(1)}, bf16[512,768]{1,0:T(8,128)(2,1)S(1)}, u32[]{:S(2)}, u32[]{:S(2)}) %collective-permute-start.24) | collective-permute-done | bytes 786464 | tf_op jit(solution)/shard_map/ppermute | solution.py:51
  324.1 3.4 collective-permute-done.32
  334.9 16.4 %collective-permute-done.34 = bf16[96,1728]{1,0:T(8,128)(2,1)S(1)} collective-permute-done((bf16[96,1728]{1,0:T(8,128)(2,1)S(1)}, bf16[96,1728]{1,0:T(8,128)(2,1)S(1)}, u32[]{:S(2)}, u32[]{:S(2)}) %collective-permute-start.34) | collective-permute-done | bytes 331808 | tf_op jit(solution)/shard_map/ppermute | solution.py:51
  354.5 3.8 collective-permute-start.37
  363.0 6.7 %collective-permute-done.38 = f32[16,768]{1,0:T(8,128)} collective-permute-done((f32[16,768]{1,0:T(8,128)}, f32[16,768]{1,0:T(8,128)}, u32[]{:S(2)}, u32[]{:S(2)}) %collective-permute-start.38) | collective-permute-done | bytes 49184 | tf_op jit(solution)/shard_map/ppermute | solution.py:51
  376.6 3.2 fusion.4
  (274 shorter events, 113.3 us)
Async XLA Ops:
  7.2 137.3 %all-gather.5.cloned.1.call-start = ((), (), s32[]{:S(2)}) async-start(), calls=%async_computation | async-start | bytes 6193152 | tf_op jit(solution)/shard_map/all_gather | solution.py:983
  22.3 122.3 %all-gather.7.cloned.1.call-start = ((), (), s32[]{:S(2)}) async-start(), calls=%async_computation.1 | async-start | bytes 6193152 | tf_op jit(solution)/shard_map/all_gather | solution.py:983
  22.3 27.8 %collective-permute-start.4 = (bf16[512,768]{1,0:T(8,128)(2,1)S(1)}, bf16[512,768]{1,0:T(8,128)(2,1)S(1)}, u32[]{:S(2)}, u32[]{:S(2)}) collective-permute-start(bf16[512,768]{1,0:T(8,128)(2,1)S(1)} %copy-done.1), channel_id=1, source_target_pairs={{0,1},{1,2},{2,3},{3,0},{4,5},{5,6},{6,7},{7,4},{8,9},{9,10},{10,1... | collective-permute-start | bytes 2359304 | tf_op jit(solution)/shard_map/ppermute | solution.py:51
  24.0 25.4 %collective-permute-start.5 = (bf16[96,1728]{1,0:T(8,128)(2,1)S(1)}, bf16[96,1728]{1,0:T(8,128)(2,1)S(1)}, u32[]{:S(2)}, u32[]{:S(2)}) collective-permute-start(bf16[96,1728]{1,0:T(8,128)(2,1)S(1)} %collective-permute-done.2), channel_id=1, source_target_pairs={{0,1},{1,2},{2,3},{3,0},{4,5},{5,6},{6,7},{7,4},{8,9},{9,10},{10,1... | collective-permute-start | bytes 995336 | tf_op jit(solution)/shard_map/ppermute | solution.py:51
  61.1 19.5 %collective-permute-start.6 = (bf16[512,768]{1,0:T(8,128)(2,1)S(1)}, bf16[512,768]{1,0:T(8,128)(2,1)}, u32[]{:S(2)}, u32[]{:S(2)}) collective-permute-start(bf16[512,768]{1,0:T(8,128)(2,1)S(1)} %collective-permute-done.4.refs_1_), channel_id=1, source_target_pairs={{0,1},{1,2},{2,3},{3,0},{4,5},{5,6},{6,7},{7,4},{8,9},{9,10},{10,1... | collective-permute-start | bytes 2359304 | tf_op jit(solution)/shard_map/ppermute | solution.py:51
  80.7 18.7 %collective-permute-start.7 = (bf16[512,768]{1,0:T(8,128)(2,1)}, bf16[512,768]{1,0:T(8,128)(2,1)S(1)}, u32[]{:S(2)}, u32[]{:S(2)}) collective-permute-start(bf16[512,768]{1,0:T(8,128)(2,1)} %collective-permute-done.6.refs_2_), channel_id=1, source_target_pairs={{0,1},{1,2},{2,3},{3,0},{4,5},{5,6},{6,7},{7,4},{8,9},{9,10},{10,1... | collective-permute-start | bytes 2359304 | tf_op jit(solution)/shard_map/ppermute | solution.py:51
  122.5 19.1 %collective-permute-start.10 = (bf16[512,192]{1,0:T(8,128)(2,1)S(1)}, bf16[512,192]{1,0:T(8,128)(2,1)S(1)}, u32[]{:S(2)}, u32[]{:S(2)}) collective-permute-start(bf16[512,192]{1,0:T(8,128)(2,1)S(1)} %get-tuple-element.226), channel_id=1, source_target_pairs={{0,3},{1,0},{2,1},{3,2},{4,7},{5,4},{6,5},{7,6},{8,11},{9,8},{10,9... | collective-permute-start | bytes 589832 | tf_op jit(solution)/shard_map/ppermute | solution.py:51
  126.3 17.5 %collective-permute-start.9 = (bf16[512,192]{1,0:T(8,128)(2,1)S(1)}, bf16[512,192]{1,0:T(8,128)(2,1)S(1)}, u32[]{:S(2)}, u32[]{:S(2)}) collective-permute-start(bf16[512,192]{1,0:T(8,128)(2,1)S(1)} %get-tuple-element.227), channel_id=1, source_target_pairs={{0,2},{1,3},{2,0},{3,1},{4,6},{5,7},{6,4},{7,5},{8,10},{9,11},{10,... | collective-permute-start | bytes 589832 | tf_op jit(solution)/shard_map/ppermute | solution.py:51
  208.8 27.9 %collective-permute-start.19 = (bf16[1092,128]{1,0:T(8,128)(2,1)S(1)}, bf16[1092,128]{1,0:T(8,128)(2,1)S(1)}, u32[]{:S(2)}, u32[]{:S(2)}) collective-permute-start(bf16[1092,128]{1,0:T(8,128)(2,1)S(1)} %pad_maximum_fusion.5), channel_id=1, source_target_pairs={{0,1},{1,0},{2,3},{3,2},{4,5},{5,4},{6,7},{7,6},{8,9},{9,8},{10,11... | collective-permute-start | bytes 838664 | tf_op jit(solution)/shard_map/ppermute | solution.py:47
  211.6 22.9 %collective-permute-start.17 = (bf16[512,192]{1,0:T(8,128)(2,1)S(1)}, bf16[512,192]{1,0:T(8,128)(2,1)S(1)}, u32[]{:S(2)}, u32[]{:S(2)}) collective-permute-start(bf16[512,192]{1,0:T(8,128)(2,1)S(1)} %get-tuple-element.223), channel_id=1, source_target_pairs={{0,2},{1,3},{2,0},{3,1},{4,6},{5,7},{6,4},{7,5},{8,10},{9,11},{10,... | collective-permute-start | bytes 589832 | tf_op jit(solution)/shard_map/ppermute | solution.py:51
  213.6 23.1 %collective-permute-start.18 = (bf16[512,192]{1,0:T(8,128)(2,1)S(1)}, bf16[512,192]{1,0:T(8,128)(2,1)S(1)}, u32[]{:S(2)}, u32[]{:S(2)}) collective-permute-start(bf16[512,192]{1,0:T(8,128)(2,1)S(1)} %get-tuple-element.222), channel_id=1, source_target_pairs={{0,3},{1,0},{2,1},{3,2},{4,7},{5,4},{6,5},{7,6},{8,11},{9,8},{10,9... | collective-permute-start | bytes 589832 | tf_op jit(solution)/shard_map/ppermute | solution.py:51
  236.7 34.7 %collective-permute-start.20 = (bf16[2,2,96,1728]{3,2,0,1:T(8,128)(2,1)}, bf16[2,2,96,1728]{3,2,0,1:T(8,128)(2,1)}, u32[]{:S(2)}, u32[]{:S(2)}) collective-permute-start(bf16[2,2,96,1728]{3,2,0,1:T(8,128)(2,1)} %fusion.5), channel_id=1, source_target_pairs={{0,8},{4,12},{8,0},{12,4},{16,24},{20,28},{24,16},{28,20},{1,9},{5... | collective-permute-start | bytes 3981320 | tf_op jit(solution)/shard_map/ppermute | solution.py:47
  237.5 33.9 %collective-permute-start.21 = (bf16[2,2,96,1728]{3,2,0,1:T(8,128)(2,1)}, bf16[2,2,96,1728]{3,2,0,1:T(8,128)(2,1)}, u32[]{:S(2)}, u32[]{:S(2)}) collective-permute-start(bf16[2,2,96,1728]{3,2,0,1:T(8,128)(2,1)} %fusion.6), channel_id=1, source_target_pairs={{0,16},{4,20},{8,24},{12,28},{16,0},{20,4},{24,8},{28,12},{1,17},{... | collective-permute-start | bytes 3981320 | tf_op jit(solution)/shard_map/ppermute | solution.py:47
  239.1 32.3 %collective-permute-start.22 = (bf16[1092,128]{1,0:T(8,128)(2,1)S(1)}, bf16[1092,128]{1,0:T(8,128)(2,1)S(1)}, u32[]{:S(2)}, u32[]{:S(2)}) collective-permute-start(bf16[1092,128]{1,0:T(8,128)(2,1)S(1)} %fusion.19), channel_id=1, source_target_pairs={{0,2},{1,3},{2,0},{3,1},{4,6},{5,7},{6,4},{7,5},{8,10},{9,11},{10,... | collective-permute-start | bytes 838664 | tf_op jit(solution)/shard_map/ppermute | solution.py:47
  275.1 22.9 %collective-permute-start.23 = (bf16[512,768]{1,0:T(8,128)(2,1)}, bf16[512,768]{1,0:T(8,128)(2,1)}, u32[]{:S(2)}, u32[]{:S(2)}) collective-permute-start(bf16[512,768]{1,0:T(8,128)(2,1)} %first_rows.1), channel_id=1, source_target_pairs={{0,1},{1,2},{2,3},{3,0},{4,5},{5,6},{6,7},{7,4},{8,9},{9,10},{10,1... | collective-permute-start | bytes 2359304 | tf_op jit(solution)/shard_map/ppermute | solution.py:51
  283.9 18.9 %collective-permute-start.26 = (bf16[2,1,96,1728]{3,2,1,0:T(8,128)(2,1)}, bf16[2,1,96,1728]{3,2,1,0:T(8,128)(2,1)}, u32[]{:S(2)}, u32[]{:S(2)}) collective-permute-start(bf16[2,1,96,1728]{3,2,1,0:T(8,128)(2,1)} %fusion.11), channel_id=1, source_target_pairs={{0,8},{4,12},{8,0},{12,4},{16,24},{20,28},{24,16},{28,20},{1,9},{5... | collective-permute-start | bytes 1990664 | tf_op jit(solution)/shard_map/ppermute | solution.py:47
  283.9 18.9 %collective-permute-start.25 = (bf16[2,1,96,1728]{3,2,1,0:T(8,128)(2,1)}, bf16[2,1,96,1728]{3,2,1,0:T(8,128)(2,1)}, u32[]{:S(2)}, u32[]{:S(2)}) collective-permute-start(bf16[2,1,96,1728]{3,2,1,0:T(8,128)(2,1)} %fusion.10), channel_id=1, source_target_pairs={{0,16},{4,20},{8,24},{12,28},{16,0},{20,4},{24,8},{28,12},{1,17},{... | collective-permute-start | bytes 1990664 | tf_op jit(solution)/shard_map/ppermute | solution.py:47
  299.8 20.4 %collective-permute-start.24 = (bf16[512,768]{1,0:T(8,128)(2,1)S(1)}, bf16[512,768]{1,0:T(8,128)(2,1)S(1)}, u32[]{:S(2)}, u32[]{:S(2)}) collective-permute-start(bf16[512,768]{1,0:T(8,128)(2,1)S(1)} %fusion.2), channel_id=1, source_target_pairs={{0,1},{1,2},{2,3},{3,0},{4,5},{5,6},{6,7},{7,4},{8,9},{9,10},{10,1... | collective-permute-start | bytes 2359304 | tf_op jit(solution)/shard_map/ppermute | solution.py:51
  304.6 22.9 %collective-permute-start.32 = (bf16[96,1728]{1,0:T(8,128)(2,1)S(1)}, bf16[96,1728]{1,0:T(8,128)(2,1)S(1)}, u32[]{:S(2)}, u32[]{:S(2)}) collective-permute-start(bf16[96,1728]{1,0:T(8,128)(2,1)S(1)} %fusion.17), channel_id=1, source_target_pairs={{0,1},{1,2},{2,3},{3,0},{4,5},{5,6},{6,7},{7,4},{8,9},{9,10},{10,1... | collective-permute-start | bytes 995336 | tf_op jit(solution)/shard_map/ppermute | solution.py:51
  307.0 22.4 %collective-permute-start.31 = (bf16[208,768]{1,0:T(8,128)(2,1)S(1)}, bf16[208,768]{1,0:T(8,128)(2,1)S(1)}, u32[]{:S(2)}, u32[]{:S(2)}) collective-permute-start(bf16[208,768]{1,0:T(8,128)(2,1)S(1)} %pad_maximum_fusion.4), channel_id=1, source_target_pairs={{0,8},{4,12},{8,0},{12,4},{16,24},{20,28},{24,16},{28,20},{1,9},{5... | collective-permute-start | bytes 958472 | tf_op jit(solution)/shard_map/ppermute | solution.py:47
  311.7 18.8 %collective-permute-start.39 = (bf16[1092,128]{1,0:T(8,128)(2,1)S(1)}, bf16[1092,128]{1,0:T(8,128)(2,1)S(1)}, u32[]{:S(2)}, u32[]{:S(2)}) collective-permute-start(bf16[1092,128]{1,0:T(8,128)(2,1)S(1)} %add.231), channel_id=1, source_target_pairs={{0,16},{4,20},{8,24},{12,28},{16,0},{20,4},{24,8},{28,12},{1,17},{... | collective-permute-start | bytes 838664 | tf_op jit(solution)/shard_map/ppermute | solution.py:47
  322.4 54.2 %collective-permute-start.30 = (bf16[512,768]{1,0:T(8,128)(2,1)}, bf16[512,768]{1,0:T(8,128)(2,1)}, u32[]{:S(2)}, u32[]{:S(2)}) collective-permute-start(bf16[512,768]{1,0:T(8,128)(2,1)} %fusion.3), channel_id=1, source_target_pairs={{0,1},{1,2},{2,3},{3,0},{4,5},{5,6},{6,7},{7,4},{8,9},{9,10},{10,1... | collective-permute-start | bytes 2359304 | tf_op jit(solution)/shard_map/ppermute | solution.py:51
  327.6 23.7 %collective-permute-start.34 = (bf16[96,1728]{1,0:T(8,128)(2,1)S(1)}, bf16[96,1728]{1,0:T(8,128)(2,1)S(1)}, u32[]{:S(2)}, u32[]{:S(2)}) collective-permute-start(bf16[96,1728]{1,0:T(8,128)(2,1)S(1)} %fusion.16), channel_id=1, source_target_pairs={{0,1},{1,2},{2,3},{3,0},{4,5},{5,6},{6,7},{7,4},{8,9},{9,10},{10,1... | collective-permute-start | bytes 995336 | tf_op jit(solution)/shard_map/ppermute | solution.py:51
  330.2 21.2 %collective-permute-start.33 = (bf16[112,768]{1,0:T(8,128)(2,1)}, bf16[112,768]{1,0:T(8,128)(2,1)}, u32[]{:S(2)}, u32[]{:S(2)}) collective-permute-start(bf16[112,768]{1,0:T(8,128)(2,1)} %pad_maximum_fusion.6), channel_id=1, source_target_pairs={{0,16},{4,20},{8,24},{12,28},{16,0},{20,4},{24,8},{28,12},{1,17},{... | collective-permute-start | bytes 516104 | tf_op jit(solution)/shard_map/ppermute | solution.py:47
  (73 other events, 726.2 us)
Sparse Core Ops, SparseCore 0:
  22.4 43.0 all-gather.4
  67.9 43.2 all-gather.6

commit v3 on v2

--- a/solution.py
+++ b/solution.py
@@ -17,8 +17,9 @@
 PRECISE = lax.Precision.HIGHEST
 F32 = jnp.float32
 BF16 = jnp.bfloat16
-VMEM_LIMIT = 48 * 1024 * 1024
+MIB = 1024 * 1024
 LIGHT = pl.CostEstimate(flops=1024, bytes_accessed=1024, transcendentals=0)
+HEAVY = pl.CostEstimate(flops=4 * 10**10, bytes_accessed=1024, transcendentals=0)
 
 
 def dot_nn(a, b, precision=None):
@@ -123,6 +124,10 @@
     return parts[0], riders
 
 
+def far_off(*values):
+    return [pltpu.with_memory_space_constraint(v, pltpu.HBM) for v in values]
+
+
 INFO_Z, INFO_D, INFO_LABEL, INFO_PIECES = 0, 1, 2, 3
 
 
@@ -159,20 +164,19 @@
     scale = HEAD_DIM ** (-0.5)
     for t in range(tensor):
         quarter = part_of(info_ref, t, tensor)
-        for part in range(per_chunk):
+
+        def one_block(part, carry):
             b = quarter * per_chunk + part
             here = pl.ds(part * blk, blk)
             q = chunks[t][here, 0:padded]
             for h in range(heads):
                 q_s[h, b] = jnp.where(head_lanes(q.shape, h), q * scale, 0.0).astype(BF16)
-            pair, at = b // 2, lax.rem(b, 2) * blk
+            pair, at = b // 2, pl.multiple_of(lax.rem(b, 2) * blk, blk)
             k_s[pair, pl.ds(at, blk), :] = chunks[t][here, padded : 2 * padded]
-            vt = chunks[t][here, 2 * padded : 3 * padded].T
-            for side in range(2):
-
-                @pl.when(lax.rem(b, 2) == side)
-                def _():
-                    vt_s[pair, :, side * blk : (side + 1) * blk] = vt
+            vt_s[pair, :, pl.ds(at, blk)] = chunks[t][here, 2 * padded : 3 * padded].T
+            return carry
+
+        lax.fori_loop(0, per_chunk, one_block, 0)
 
 
     def one_query(i, carry):
@@ -250,7 +254,7 @@
             pltpu.VMEM((blocks // 2, 2 * blk, padded), BF16),
             pltpu.VMEM((blocks // 2, padded, 2 * blk), BF16),
         ],
-        compiler_params=pltpu.CompilerParams(vmem_limit_bytes=VMEM_LIMIT),
+        compiler_params=pltpu.CompilerParams(vmem_limit_bytes=24 * MIB),
         cost_estimate=LIGHT,
         name="attend_forward",
     )(info, *chunks)
@@ -269,7 +273,8 @@
     scale = HEAD_DIM ** (-0.5)
     for t in range(tensor):
         quarter = part_of(info_ref, t, tensor)
-        for part in range(per_chunk):
+
+        def one_block(part, carry):
             b = quarter * per_chunk + part
             here = pl.ds(part * blk, blk)
             q = chunks[t][here, 0:padded]
@@ -280,16 +285,10 @@
                 if padded > width:
                     g_s[h, b, :, width:padded] = jnp.zeros((blk, padded - width), BF16)
             k = chunks[t][here, padded : 2 * padded]
-            pair, at = b // 2, lax.rem(b, 2) * blk
+            pair, at = b // 2, pl.multiple_of(lax.rem(b, 2) * blk, blk)
             k_s[pair, pl.ds(at, blk), :] = k
             v_s[pair, pl.ds(at, blk), :] = chunks[t][here, 2 * padded : 3 * padded]
-            kt = k.T
-            for side in range(2):
-
-                @pl.when(lax.rem(b, 2) == side)
-                def _():
-                    kt_s[pair, :, side * blk : (side + 1) * blk] = kt
-
+            kt_s[pair, :, pl.ds(at, blk)] = k.T
             prod = (g.astype(F32) * o_ref[t, here, :].astype(F32)).T
             sums = [
                 jnp.sum(prod[h * HEAD_DIM : (h + 1) * HEAD_DIM, :], axis=0, keepdims=True)
@@ -297,6 +296,9 @@
             ]
             delta_s[b] = jnp.concatenate(sums + [jnp.zeros((8 - heads, blk), F32)], axis=0)
             dqt_s[b] = jnp.zeros((padded, blk), F32)
+            return carry
+
+        lax.fori_loop(0, per_chunk, one_block, 0)
     bias_ref[...] = jnp.zeros_like(bias_ref)
 
     keys = 2 * blk
@@ -392,10 +394,10 @@
             pltpu.VMEM((2 * blk, padded), F32),
             pltpu.VMEM((2 * blk, padded), F32),
         ],
-        compiler_params=pltpu.CompilerParams(vmem_limit_bytes=VMEM_LIMIT),
+        compiler_params=pltpu.CompilerParams(vmem_limit_bytes=34 * MIB),
         cost_estimate=LIGHT,
         name="attend_backward",
-    )(info, *chunks, *grads, mixed, lse)
+    )(info, *far_off(*chunks, *grads, mixed, lse))
 
 
 def start_weights(pieces, w_s, wo_s, sems, o_sem):
@@ -432,8 +434,8 @@
     tok_ref, vec_ref, bias_ref, proj_ref, cvec_ref = refs[tensor : tensor + 5]
     pieces = refs[tensor + 5 : tensor + 5 + arrays]
     (
-        low_ref, xlow_ref, act_ref, slope_ref, xh1_ref, xh2_ref, rs_ref, stud_ref, mall_ref,
-        e_ref, stats_ref, acc_s, w_s, wo_s, sems, o_sem,
+        low_ref, xlow_ref, act_ref, slope_ref, xh1_ref, xh2_ref, rs_ref, stud_ref, e_ref,
+        stats_ref, acc_s, w_s, wo_s, sems, o_sem,
     ) = refs[tensor + 5 + arrays :]
     j = pl.program_id(0)
     hidden = act_ref.shape[2]
@@ -445,7 +447,6 @@
         pltpu.make_async_copy(wo_s, wo_s, o_sem).wait()
         for s in range(tensor):
             piece = mixed[s][...]
-            mall_ref[s] = piece
             total = total + dot_nt(piece, wo_s[s])
         centered, rstd = center(total)
         xhat = centered * rstd
@@ -456,13 +457,20 @@
         acc_s[...] = x_one + vec_ref[5:6, :]
 
     pltpu.make_async_copy(w_s.at[j], w_s.at[j], sems.at[j]).wait()
-    upper = dot_nn(xlow_ref[...], w_s[j, :, 0:hidden]) + bias_ref[0]
-    phi = 0.5 * (1.0 + lax.erf(upper * (0.5**0.5)))
-    act = (upper * phi).astype(BF16)
-    slope = phi + upper * (jnp.exp(-0.5 * upper * upper) * 0.3989422804014327)
-    act_ref[0] = act
-    slope_ref[0] = slope.astype(BF16)
-    acc_s[...] = acc_s[...] + dot_nt(act, w_s[j, :, hidden:])
+    half = min(256, xlow_ref.shape[0])
+
+    def rows_part(n, carry):
+        here = pl.ds(n * half, half)
+        upper = dot_nn(xlow_ref[here, :], w_s[j, :, 0:hidden]) + bias_ref[0]
+        phi = 0.5 * (1.0 + lax.erf(upper * (0.5**0.5)))
+        act = (upper * phi).astype(BF16)
+        slope = phi + upper * (jnp.exp(-0.5 * upper * upper) * 0.3989422804014327)
+        act_ref[0, here, :] = act
+        slope_ref[0, here, :] = slope.astype(BF16)
+        acc_s[here, :] = acc_s[here, :] + dot_nt(act, w_s[j, :, hidden:])
+        return carry
+
+    lax.fori_loop(0, xlow_ref.shape[0] // half, rows_part, 0)
 
     @pl.when(j == pl.num_programs(0) - 1)
     def _():
@@ -533,7 +541,6 @@
                 whole(rows, width),
                 whole(rows, 2),
                 whole(rows, ch),
-                whole(tensor, rows, head_width),
                 whole(rows, ch),
                 whole(8, ch),
             ),
@@ -546,22 +553,22 @@
             ],
         ),
         out_shape=(
-            jax.ShapeDtypeStruct((rows, width), BF16),
-            jax.ShapeDtypeStruct((rows, width), BF16),
-            jax.ShapeDtypeStruct((tensor, rows, hidden), BF16),
-            jax.ShapeDtypeStruct((tensor, rows, hidden), BF16),
-            jax.ShapeDtypeStruct((rows, width), F32),
-            jax.ShapeDtypeStruct((rows, width), F32),
-            jax.ShapeDtypeStruct((rows, 2), F32),
-            jax.ShapeDtypeStruct((rows, ch), F32),
-            jax.ShapeDtypeStruct((tensor, rows, head_width), BF16),
-            jax.ShapeDtypeStruct((rows, ch), F32),
+            pltpu.HBM((rows, width), BF16),
+            pltpu.HBM((rows, width), BF16),
+            pltpu.HBM((tensor, rows, hidden), BF16),
+            pltpu.HBM((tensor, rows, hidden), BF16),
+            pltpu.HBM((rows, width), F32),
+            pltpu.HBM((rows, width), F32),
+            pltpu.HBM((rows, 2), F32),
+            pltpu.HBM((rows, ch), F32),
+            pltpu.HBM((rows, ch), F32),
             jax.ShapeDtypeStruct((8, ch), F32),
         ),
-        compiler_params=pltpu.CompilerParams(vmem_limit_bytes=VMEM_LIMIT),
+        compiler_params=pltpu.CompilerParams(vmem_limit_bytes=34 * MIB),
         cost_estimate=LIGHT,
         name="rows_forward",
-    )(info, *mixed, tokens, vec_table, ff_bias, cls_proj, cls_vec, *pieces)
+    )(info, *far_off(*mixed, tokens), vec_table, ff_bias, cls_proj, cls_vec,
+      *far_off(*pieces))
 
 
 def norm_back(grad, xhat, rstd, gain):
@@ -575,13 +582,13 @@
     stats_refs = refs[:tensor]
     (
         stud_ref, e_ref, cot_ref, xh1_ref, xh2_ref, rs_ref, slope_ref, vec_ref, proj_ref,
-        cvec_ref, chid_ref, cout_ref, cbias_ref,
-    ) = refs[tensor : tensor + 13]
-    pieces = refs[tensor + 13 : tensor + 13 + arrays]
+        cvec_ref, chid_ref, cout_ref, cbias_ref, outlow_ref,
+    ) = refs[tensor : tensor + 14]
+    pieces = refs[tensor + 14 : tensor + 14 + arrays]
     (
-        logit_ref, two_ref, gu_ref, one_ref, gh1_ref, gm_ref, gsl_ref, pack_ref, acc_s, w_s, wo_s,
-        sems, o_sem,
-    ) = refs[tensor + 13 + arrays :]
+        logit_ref, two_ref, gu_ref, one_ref, gh1_ref, gm_ref, small_ref, acc_s, pack_ref, w_s,
+        wo_s, sems, o_sem,
+    ) = refs[tensor + 14 + arrays :]
     j = pl.program_id(0)
     ch = stud_ref.shape[1]
     hidden = gu_ref.shape[2]
@@ -634,7 +641,7 @@
         grad_e = w * (grad_w - base)
         grad_student = w * gp + grad_e * query
         gsl = grad_student.astype(BF16)
-        gsl_ref[...] = gsl
+        small_ref[0:width, :] = dot_tn(outlow_ref[...], gsl).astype(BF16)
         pack_ref[0:8, :] = jnp.concatenate(
             [
                 jnp.sum(grad_student, axis=0, keepdims=True),
@@ -655,16 +662,24 @@
         two_ref[...] = two.astype(BF16)
 
     pltpu.make_async_copy(w_s.at[j], w_s.at[j], sems.at[j]).wait()
-    upper = dot_nn(two_ref[...], w_s[j, :, hidden:]) * slope_ref[0].astype(F32)
     heads_row = part_of(info_ref, j, tensor)
-    bias_row = jnp.sum(upper, axis=0, keepdims=True)
+    half = min(256, two_ref.shape[0])
+
+    def rows_part(n, bias_row):
+        here = pl.ds(n * half, half)
+        upper = dot_nn(two_ref[here, :], w_s[j, :, hidden:]) * slope_ref[0, here, :].astype(F32)
+        low = upper.astype(BF16)
+        gu_ref[0, here, :] = low
+        acc_s[here, :] = acc_s[here, :] + dot_nt(low, w_s[j, :, 0:hidden])
+        return bias_row + jnp.sum(upper, axis=0, keepdims=True)
+
+    bias_row = lax.fori_loop(
+        0, two_ref.shape[0] // half, rows_part, jnp.zeros((1, hidden), F32)
+    )
     for n in range(hidden // ch):
         pack_ref[pl.ds(bias_at + heads_row * (hidden // ch) + n, 1), :] = bias_row[
             :, n * ch : (n + 1) * ch
         ]
-    low = upper.astype(BF16)
-    gu_ref[0] = low
-    acc_s[...] = acc_s[...] + dot_nt(low, w_s[j, :, 0:hidden])
 
     @pl.when(j == pl.num_programs(0) - 1)
     def _():
@@ -680,16 +695,17 @@
         pltpu.make_async_copy(wo_s, wo_s, o_sem).wait()
         for s in range(tensor):
             gm_ref[s] = dot_nn(low, wo_s[s]).astype(BF16)
+        small_ref[width:, :] = pack_ref[...].astype(BF16)
 
 
 def rows_backward(
     info, pieces, stats, kept, cotangent, vec_table, cls_proj, cls_vec, cls_hidden,
     cls_out, cls_bias,
 ):
-    _, _, _, slope, xh1, xh2, rs, student, mixed, pool_logit, _ = kept
+    out_low, _, _, slope, xh1, xh2, rs, student, pool_logit, _ = kept
     tensor, rows, hidden = slope.shape
     width = xh1.shape[1]
-    head_width = mixed.shape[2]
+    head_width = pieces[0].shape[3] - 2 * hidden
     ch = student.shape[1]
     far = pl.BlockSpec(memory_space=pl.ANY)
     pack_rows = 8 + 2 * ch + (6 * width + tensor * hidden) // ch
@@ -714,6 +730,7 @@
                 whole(ch, ch),
                 whole(ch, ch),
                 whole(1, ch),
+                whole(rows, width),
             ]
             + [far] * len(pieces),
             out_specs=(
@@ -723,11 +740,11 @@
                 whole(rows, width),
                 whole(rows, width),
                 whole(tensor, rows, head_width),
-                whole(rows, ch),
-                whole(pack_rows, ch),
+                whole(width + pack_rows, ch),
             ),
             scratch_shapes=[
                 pltpu.VMEM((rows, width), F32),
+                pltpu.VMEM((pack_rows, ch), F32),
                 pltpu.VMEM((tensor, width, 2 * hidden), BF16),
                 pltpu.VMEM((tensor, width, head_width), BF16),
                 pltpu.SemaphoreType.DMA((tensor,)),
@@ -741,46 +758,43 @@
             jax.ShapeDtypeStruct((rows, width), BF16),
             jax.ShapeDtypeStruct((rows, width), F32),
             jax.ShapeDtypeStruct((tensor, rows, head_width), BF16),
-            jax.ShapeDtypeStruct((rows, ch), BF16),
-            jax.ShapeDtypeStruct((pack_rows, ch), F32),
+            jax.ShapeDtypeStruct((width + pack_rows, ch), BF16),
         ),
-        compiler_params=pltpu.CompilerParams(vmem_limit_bytes=VMEM_LIMIT),
+        compiler_params=pltpu.CompilerParams(vmem_limit_bytes=34 * MIB),
         cost_estimate=LIGHT,
         name="rows_backward",
     )(
-        info, *stats, student, pool_logit, cotangent, xh1, xh2, rs, slope, vec_table, cls_proj,
-        cls_vec, cls_hidden, cls_out, cls_bias, *pieces,
-    )
-
-
-def weight_grads_kernel(
-    dp, shard, info_ref, x_ref, two_ref, one_ref, gu_ref, act_ref, mix_ref, low_ref, gsl_ref,
-    *refs,
-):
-    outs, proj_ref = refs[:-4], refs[-4]
-    lefts = refs[-3:]
+        info, *stats, *far_off(student, pool_logit, cotangent, xh1, xh2, rs, slope), vec_table,
+        cls_proj, cls_vec, cls_hidden, cls_out, cls_bias, *far_off(out_low, *pieces),
+    )
+
+
+def weight_grads_kernel(dp, shard, tensor, info_ref, x_ref, two_ref, one_ref, gu_ref, act_ref, *refs):
+    mixed, outs, lefts, mixed_s = refs[:tensor], refs[tensor:-4], refs[-4:-1], refs[-1]
     j = pl.program_id(0)
     hidden = gu_ref.shape[2]
     width = x_ref.shape[1]
-    apart = len(outs) == 2
+    halves = 2 if len(outs) == 4 else 1
 
     @pl.when(j == 0)
     def _():
+        for t in range(tensor):
+            mixed_s[t] = mixed[t][...]
         for source, left in zip((x_ref, two_ref, one_ref), lefts):
             turned = source[...].T
-            if not apart:
+            if halves == 1:
                 left[...] = turned
                 continue
             for b in range(dp):
                 offset = jnp.bitwise_xor(info_ref[INFO_D], b)
                 at = lax.rem(offset, 2) * (dp // 2) + offset // 2
                 left[pl.ds(at * shard, shard), :] = turned[b * shard : (b + 1) * shard, :]
-        proj_ref[...] = dot_tn(low_ref[...], gsl_ref[...])
-
-    count = width // len(outs)
-    rights = (gu_ref[0], act_ref[0], mix_ref[0])
-    ends = (0, hidden, 2 * hidden, 2 * hidden + mix_ref.shape[2])
-    for n, out in enumerate(outs):
+
+    count = width // halves
+    rights = (gu_ref[0], act_ref[0], mixed_s[j])
+    ends = (0, hidden, 2 * hidden, 2 * hidden + mixed_s.shape[2])
+
+    def write(out, n):
         here = slice(n * count, (n + 1) * count)
         for m in range(3):
             part = dot_nn(lefts[m][here, :], rights[m]).astype(BF16)
@@ -788,21 +802,33 @@
                 out.shape[1], out.shape[2], ends[m + 1] - ends[m]
             )
 
-
-def weight_grads(
-    info, dp, shard, x_low, two_low, one_low, upper_low, act, mixed, out_low, student_low
-):
+    if halves == 1:
+        write(outs[0], 0)
+    for side in range(halves if halves > 1 else 0):
+
+        @pl.when((j < tensor // 2) if side == 0 else (j >= tensor // 2))
+        def _():
+            write(outs[side], 0)
+            write(outs[2 + side], 1)
+
+
+def weight_grads(info, dp, shard, x_low, two_low, one_low, upper_low, act, mixed):
     tensor, rows, hidden = upper_low.shape
     width = x_low.shape[1]
-    head_width = mixed.shape[2]
-    ch = student_low.shape[1]
+    head_width = mixed[0].shape[1]
     total = 2 * hidden + head_width
+    half = tensor // 2
     if shard % 16:
-        parts = [(1, width)]
+        out_specs = (block(1, width, total),)
+        shapes = (jax.ShapeDtypeStruct((tensor, 1, width, total), BF16),)
     else:
-        parts = [(dp // 2, shard)] * 2
+        shape = (dp // 2, shard, total)
+        near = pl.BlockSpec((1,) + shape, lambda j, *_: (jnp.minimum(j, half - 1), 0, 0, 0))
+        far = pl.BlockSpec((1,) + shape, lambda j, *_: (jnp.maximum(j - half, 0), 0, 0, 0))
+        out_specs = (near, far) * 2
+        shapes = (jax.ShapeDtypeStruct((half,) + shape, BF16),) * 4
     return pl.pallas_call(
-        functools.partial(weight_grads_kernel, dp, shard),
+        functools.partial(weight_grads_kernel, dp, shard, tensor),
         grid_spec=pltpu.PrefetchScalarGridSpec(
             num_scalar_prefetch=1,
             grid=(tensor,),
@@ -812,19 +838,17 @@
                 whole(rows, width),
                 block(rows, hidden),
                 block(rows, hidden),
-                block(rows, head_width),
-                whole(rows, width),
-                whole(rows, ch),
-            ],
-            out_specs=tuple(block(*part, total) for part in parts) + (whole(width, ch),),
-            scratch_shapes=[pltpu.VMEM((width, rows), BF16)] * 3,
+            ]
+            + [whole(rows, head_width)] * tensor,
+            out_specs=out_specs,
+            scratch_shapes=[pltpu.VMEM((width, rows), BF16)] * 3
+            + [pltpu.VMEM((tensor, rows, head_width), BF16)],
         ),
-        out_shape=tuple(jax.ShapeDtypeStruct((tensor, *part, total), BF16) for part in parts)
-        + (jax.ShapeDtypeStruct((width, ch), F32),),
-        compiler_params=pltpu.CompilerParams(vmem_limit_bytes=VMEM_LIMIT),
+        out_shape=shapes,
+        compiler_params=pltpu.CompilerParams(vmem_limit_bytes=26 * MIB),
         cost_estimate=LIGHT,
         name="weight_grads",
-    )(info, x_low, two_low, one_low, upper_low, act, mixed, out_low, student_low)
+    )(info, *far_off(x_low), two_low, one_low, upper_low, *far_off(act, *mixed))
 
 
 def weights_to_owner(parts, dp, tensor, z):
@@ -841,14 +865,13 @@
             return owned
 
         return (), (), lambda sent: (), done
-    keep, give = parts
+    keep, give = parts[:2], parts[2:]
     bits = bits_of(dp)
-    got = swapped(give, "dp", dp, bits[0])
+    got = [swapped(v, "dp", dp, bits[0]) for v in give]
     half = tensor // 2
     orders = (bits[1:], bits[1:][::-1])
-    sides = [slice(0, half), slice(half, tensor)]
     sent = []
-    for side, order in zip(sides, orders):
+    for side, order in enumerate(orders):
         value = split_by(keep[side], bits[1:], order[0], 1).astype(F32)
         value = value + split_by(got[side], bits[1:], order[0], 1).astype(F32)
         sent.append(value.astype(BF16))
@@ -859,7 +882,7 @@
     def finish(came, late):
         sent = None
         values, lefts = [], [list(bits[1:]), list(bits[1:])]
-        for side, order in zip(sides, orders):
+        for side, order in enumerate(orders):
             value = split_by(keep[side], bits[1:], order[0], 0).astype(F32)
             values.append(value + split_by(late[side], bits[1:], order[0], 0).astype(F32))
         for n in range(len(bits) - 1):
@@ -909,14 +932,36 @@
             whole(*w_in.shape),
         ],
         out_specs=whole(rows, w_in.shape[0]),
-        compiler_params=pltpu.CompilerParams(vmem_limit_bytes=VMEM_LIMIT),
+        compiler_params=pltpu.CompilerParams(vmem_limit_bytes=12 * MIB),
         cost_estimate=LIGHT,
         name="first_rows",
     )(d_chunks, w_in)
 
 
-def other_rows_kernel(tensor, d_ref, w_ref, *refs):
-    seq_refs, (out_ref, grad_ref) = refs[:tensor], refs[tensor:]
+def rest_rows_kernel(d_ref, w_ref, out_ref):
+    out_ref[0] = dot_nt(d_ref[0], w_ref[...]).astype(BF16)
+
+
+def rest_rows(d_chunks, w_in):
+    tensor, rows, width = d_chunks.shape
+    model = w_in.shape[0]
+    return pl.pallas_call(
+        rest_rows_kernel,
+        grid=(tensor - 1,),
+        out_shape=jax.ShapeDtypeStruct((tensor - 1, rows, model), BF16),
+        in_specs=[
+            pl.BlockSpec((1, rows, width), lambda n: (lax.rem(n + 2, tensor), 0, 0)),
+            whole(*w_in.shape),
+        ],
+        out_specs=block(rows, model),
+        compiler_params=pltpu.CompilerParams(vmem_limit_bytes=12 * MIB),
+        cost_estimate=LIGHT,
+        name="rest_rows",
+    )(d_chunks, w_in)
+
+
+def in_grad_kernel(tensor, d_ref, *refs):
+    seq_refs, grad_ref = refs[:tensor], refs[tensor]
     n = pl.program_id(0)
     for t in range(tensor):
 
@@ -928,25 +973,20 @@
             else:
                 grad_ref[...] += part
 
-    out_ref[0] = dot_nt(d_ref[0], w_ref[...]).astype(BF16)
-
-
-def other_rows(d_chunks, w_in, seq_rows):
+
+def in_grad(d_chunks, seq_rows):
     tensor, rows, width = d_chunks.shape
-    model = w_in.shape[0]
+    model = seq_rows[0].shape[1]
     return pl.pallas_call(
-        functools.partial(other_rows_kernel, tensor),
+        functools.partial(in_grad_kernel, tensor),
         grid=(tensor,),
-        out_shape=(
-            jax.ShapeDtypeStruct((tensor, rows, model), BF16),
-            jax.ShapeDtypeStruct((model, width), F32),
-        ),
-        in_specs=[block(rows, width), whole(*w_in.shape)] + [whole(rows, model)] * tensor,
-        out_specs=(block(rows, model), whole(model, width)),
-        compiler_params=pltpu.CompilerParams(vmem_limit_bytes=VMEM_LIMIT),
-        cost_estimate=LIGHT,
-        name="other_rows",
-    )(d_chunks, w_in, *seq_rows)
+        out_shape=jax.ShapeDtypeStruct((model, width), F32),
+        in_specs=[block(rows, width)] + [whole(rows, model)] * tensor,
+        out_specs=whole(model, width),
+        compiler_params=pltpu.CompilerParams(vmem_limit_bytes=16 * MIB),
+        cost_estimate=HEAVY,
+        name="in_grad",
+    )(d_chunks, *seq_rows)
 
 
 def per_device(
@@ -1003,30 +1043,32 @@
         for part in seq_rows
     ]
     mixed, lse = attend_forward(info, chunks, heads)
+    mixed_parts = exchanged(mixed)
     kept = rows_forward(
-        info, pieces, exchanged(mixed), tokens, vec_table,
+        info, pieces, mixed_parts, tokens, vec_table,
         ff_bias.reshape(tensor, 1, hidden), cls_proj, cls_vec,
     )
-    out_low, x_low, act, _, _, _, _, _, mixed_all, _, stats = kept
+    out_low, x_low, act, _, _, _, _, _, _, stats = kept
     all_stats = exchanged([stats] * tensor)
     (
-        logits, two_low, upper_low, one_low, grad_h_one, grad_mixed, student_low, pack,
+        logits, two_low, upper_low, one_low, grad_h_one, grad_mixed, small,
     ) = rows_backward(
         info, pieces, all_stats, kept, cotangent, vec_table, cls_proj, cls_vec,
         cls_hidden, jnp.pad(cls_out, ((0, 0), (0, ch - CLASSES))),
         jnp.pad(cls_bias, (0, ch - CLASSES)).reshape(1, ch),
     )
     grad_rows = exchanged(grad_mixed)
-    *ff_parts, grad_proj = weight_grads(
-        info, dp, shard, x_low, two_low, one_low, upper_low, act, mixed_all, out_low, student_low
-    )
-    small = jnp.concatenate([grad_proj, pack], axis=0).astype(BF16)
     bits = bits_of(tensor)
     small_came = swapped(small, "tensor", tensor, bits[0])
+    ff_parts = weight_grads(
+        info, dp, shard, x_low, two_low, one_low, upper_low, act, mixed_parts
+    )
+    ff_parts, grad_rows[1], small_came = lax.optimization_barrier(
+        (ff_parts, grad_rows[1], small_came)
+    )
     sent, got, first, finish = weights_to_owner(ff_parts, dp, tensor, z)
-    sent, grad_rows, small_came = lax.optimization_barrier((sent, grad_rows, small_came))
     small = small + small_came
-    small, grad_rows = lax.optimization_barrier((small, grad_rows))
+    sent, small, grad_rows = lax.optimization_barrier((sent, small, grad_rows))
     small_came = swapped(small, "tensor", tensor, bits[1])
 
     d_chunks, bias_sums = attend_backward(info, chunks, grad_rows, mixed, lse, heads)
@@ -1046,19 +1088,21 @@
             total = total + got
         return total.astype(F32)
 
-    shared = {}
-
     def rows_chain():
+        came = shifted(first_part, "tensor", tensor, 1)
+        later = yield first_part, d_chunks
+        rest = rest_rows(later, w_in)
         total = first_part
         for t in range(2, tensor):
-            came = yield total, shifted(total, "tensor", tensor, 1)
-            total = (shared["parts"][t].astype(F32) + came.astype(F32)).astype(BF16)
-        came = yield total, shifted(total, "tensor", tensor, 1)
-        return grad_h_one + shared["parts"][0].astype(F32) + came.astype(F32)
+            came = yield (total, rest), came
+            total = (rest[t - 2].astype(F32) + came.astype(F32)).astype(BF16)
+            came = shifted(total, "tensor", tensor, 1)
+        came = yield total, came
+        return grad_h_one + rest[tensor - 2].astype(F32) + came.astype(F32)
 
     def in_chain():
         later = yield (), d_chunks
-        shared["parts"], grad = other_rows(later, w_in, seq_rows)
+        grad = in_grad(later, seq_rows)
         grad = yield (), grad
         rider = jnp.pad(bias_sums, ((0, 8), (0, 2 * padded)))
         return (
@@ -1076,8 +1120,9 @@
             "small": small_chain(),
         },
         [
-            ("in",), ("rows",), ("in",), ("small",), ("ff",), ("in",), ("small",), ("rows",),
-            ("ff",), ("in",), ("small",), ("ff",), ("in",), ("small",), ("ff",), ("in",), ("rows",),
+            ("rows",), ("rows",), ("in",), ("ff",), ("in",), ("small",), ("in",), ("small",),
+            ("rows",), ("in",), ("ff",), ("small",), ("in",), ("ff",), ("in",), ("small",),
+            ("rows",), ("ff",),
         ],
     )
     grad_w_qkv = grad_in.reshape(shard, 3, padded)[:, :, :local]

time: 394 us -> 365 us (0.926)
  the two profiles are of different devices: /device:TPU:8 before, /device:TPU:0 now
where the time goes in v3:
time: 365 us
  waiting for transfers between devices  149 us (41%)
  Pallas kernels  108 us (30%)
  starting transfers between devices  38 us (10%)
  other arithmetic  27.2 us (7%)
  local copies, waits for them, and re-layouts  23.1 us (6%)
  between operations  15.6 us (4%)
  matrix products  4.56 us (1%)
    ppermute x24, waiting for transfers between devices, shifted(): lax.ppermute(value, axis, [(i, (i + by) % size) for i in range(size)])  133 us
    pallas_call x1, Pallas kernels, attend_backward(): pl.pallas_call(functools.partial(attend_backward_kernel, heads), out_shap...  31.2 us
    ppermute x24, starting transfers between devices, shifted(): lax.ppermute(value, axis, [(i, (i + by) % size) for i in range(size)])  24.4 us
    pallas_call x1, Pallas kernels, attend_forward(): pl.pallas_call(functools.partial(attend_forward_kernel, heads), out_shape...  21.6 us
    pallas_call x1, Pallas kernels, rows_forward(): pl.pallas_call(functools.partial(rows_forward_kernel, tensor, len(pieces)...  20.3 us
    pallas_call x1, Pallas kernels, rows_backward(): pl.pallas_call(functools.partial(rows_backward_kernel, tensor, len(pieces...  16.8 us
    ppermute x17, waiting for transfers between devices, swapped(): return lax.ppermute(value, axis, [(i, i ^ bit) for i in range(size)])  16.7 us
    ppermute x17, starting transfers between devices, swapped(): return lax.ppermute(value, axis, [(i, i ^ bit) for i in range(size)])  13.6 us
  transfers between devices with their start and end apart: 43, of which 19 were waited for; matrix products, arithmetic and copies ran while one was open for 12% of the time, Pallas kernels for 19%

profile of v3, /device:TPU:0, one launch (start us, length us, event | category | flops | bytes accessed | tf_op | source)
XLA Modules:
  0.0 365.3 jit_solution(4959251767844180925)
XLA Ops:
  15.1 9.1 %collective-permute-done.2 = bf16[96,1728]{1,0:T(8,128)(2,1)S(1)} collective-permute-done((bf16[96,1728]{1,0:T(8,128)(2,1)S(1)}, bf16[96,1728]{1,0:T(8,128)(2,1)S(1)}, u32[]{:S(2)}, u32[]{:S(2)}) %collective-permute-start.2) | collective-permute-done | bytes 331808 | tf_op jit(solution)/shard_map/ppermute | solution.py:52
  26.9 26.9 %collective-permute-done.5 = bf16[96,1728]{1,0:T(8,128)(2,1)S(1)} collective-permute-done((bf16[96,1728]{1,0:T(8,128)(2,1)S(1)}, bf16[96,1728]{1,0:T(8,128)(2,1)S(1)}, u32[]{:S(2)}, u32[]{:S(2)}) %collective-permute-start.5) | collective-permute-done | bytes 331808 | tf_op jit(solution)/shard_map/ppermute | solution.py:52
  53.8 10.8 %collective-permute-done.11 = bf16[96,1728]{1,0:T(8,128)(2,1)S(1)} collective-permute-done((bf16[96,1728]{1,0:T(8,128)(2,1)S(1)}, bf16[96,1728]{1,0:T(8,128)(2,1)S(1)}, u32[]{:S(2)}, u32[]{:S(2)}) %collective-permute-start.11) | collective-permute-done | bytes 331808 | tf_op jit(solution)/shard_map/ppermute | solution.py:52
  68.2 11.2 %collective-permute-done.3 = bf16[384,768]{1,0:T(8,128)(2,1)} collective-permute-done((bf16[384,768]{1,0:T(8,128)(2,1)S(1)}, bf16[384,768]{1,0:T(8,128)(2,1)}, u32[]{:S(2)}, u32[]{:S(2)}) %collective-permute-start.3) | collective-permute-done | bytes 589856 | tf_op jit(solution)/shard_map/ppermute | solution.py:48
  81.1 4.1 %collective-permute-done.6.refs_2_ = bf16[512,768]{1,0:T(8,128)(2,1)} collective-permute-done((bf16[512,768]{1,0:T(8,128)(2,1)S(1)}, bf16[512,768]{1,0:T(8,128)(2,1)}, u32[]{:S(2)}, u32[]{:S(2)}) %collective-permute-start.6) | collective-permute-done | bytes 786464 | tf_op jit(solution)/shard_map/ppermute | solution.py:52
  89.0 14.8 %collective-permute-done.7.refs_3_ = bf16[512,768]{1,0:T(8,128)(2,1)S(1)} collective-permute-done((bf16[512,768]{1,0:T(8,128)(2,1)}, bf16[512,768]{1,0:T(8,128)(2,1)S(1)}, u32[]{:S(2)}, u32[]{:S(2)}) %collective-permute-start.7) | collective-permute-done | bytes 786464 | tf_op jit(solution)/shard_map/ppermute | solution.py:52
  105.5 21.6 %attend_forward.1 = (bf16[4,512,192]{2,1,0:T(8,128)(2,1)S(1)}, f32[8,8,256]{2,1,0:T(8,128)S(1)}) custom-call(s32[7]{0:T(128)S(1)} %concatenate.39.info_ref, bf16[512,768]{1,0:T(8,128)(2,1)S(1)} %fusion.9.refs_0_, bf16[512,768]{1,0:T(8,128)(2,1)S(1)} %add_convert_fusion.4.refs_1_, bf16[512,768]{1,0:T(8,128)(2,1)S(1)} %add_convert_fusion.3.refs_2_, ...), custom_call_target="tpu_custom_call" | custom-call | flops 1024 | bytes 1024 | tf_op jit(solution)/shard_map/attend_forward/pallas_call | solution.py:244
  130.0 10.1 %collective-permute-done.10.refs_3_ = bf16[512,192]{1,0:T(8,128)(2,1)S(1)} collective-permute-done((bf16[512,192]{1,0:T(8,128)(2,1)S(1)}, bf16[512,192]{1,0:T(8,128)(2,1)S(1)}, u32[]{:S(2)}, u32[]{:S(2)}) %collective-permute-start.10) | collective-permute-done | bytes 196640 | tf_op jit(solution)/shard_map/ppermute | solution.py:52
  140.1 9.0 %collective-permute-done.9.refs_2_ = bf16[512,192]{1,0:T(8,128)(2,1)S(1)} collective-permute-done((bf16[512,192]{1,0:T(8,128)(2,1)S(1)}, bf16[512,192]{1,0:T(8,128)(2,1)S(1)}, u32[]{:S(2)}, u32[]{:S(2)}) %collective-permute-start.9) | collective-permute-done | bytes 196640 | tf_op jit(solution)/shard_map/ppermute | solution.py:52
  149.9 20.3 %rows_forward.1 = (bf16[512,768]{1,0:T(8,128)(2,1)}, bf16[512,768]{1,0:T(8,128)(2,1)}, bf16[4,512,768]{2,1,0:T(8,128)(2,1)}, bf16[4,512,768]{2,1,0:T(8,128)(2,1)...) custom-call(s32[7]{0:T(128)S(1)} %concatenate.39.info_ref, ...), custom_call_target="tpu_custom_call" | custom-call | flops 1024 | bytes 1024 | tf_op jit(solution)/shard_map/rows_forward/pallas_call | solution.py:521
  170.6 3.4 collective-permute-start.13
  177.6 16.8 %rows_backward.1 = (f32[8,128]{1,0:T(8,128)S(1)}, bf16[512,768]{1,0:T(8,128)(2,1)S(1)}, bf16[4,512,768]{2,1,0:T(8,128)(2,1)S(1)}, bf16[512,768]{1,0:T(8,128)(2,1...) custom-call(s32[7]{0:T(128)S(1)} %concatenate.39.info_ref, ...), custom_call_target="tpu_custom_call" | custom-call | flops 1024 | bytes 1024 | tf_op jit(solution)/shard_map/rows_backward/pallas_call | solution.py:713
  197.3 9.9 %weight_grads.1 = (bf16[2,4,96,1728]{3,2,1,0:T(8,128)(2,1)S(1)}, bf16[2,4,96,1728]{3,2,1,0:T(8,128)(2,1)S(1)}, bf16[2,4,96,1728]{3,2,1,0:T(8,128)(2,1)S(1)}, bf16[2,4,96,1728]{3,2,1,0:T(8,128)(2,1)S(1)}) custom-call(s32[7]{0:T(128)S(1)} %concatenate.39.info_ref, bf16[512,768]{1,0:T(8,128)(2,1)} %get-tuple-element.114.x_ref, ...), custom_call_target="tpu_custom_call" | custom-call | flops 1024 | bytes 1024 | tf_op jit(solution)/shard_map/weight_grads/pallas_call | solution.py:830
  218.3 4.8 %collective-permute-done.19.refs_6_ = bf16[512,192]{1,0:T(8,128)(2,1)S(1)} collective-permute-done((bf16[512,192]{1,0:T(8,128)(2,1)S(1)}, bf16[512,192]{1,0:T(8,128)(2,1)S(1)}, u32[]{:S(2)}, u32[]{:S(2)}) %collective-permute-start.19) | collective-permute-done | bytes 196640 | tf_op jit(solution)/shard_map/ppermute | solution.py:52
  224.7 4.5 %collective-permute-start.23 = (bf16[1092,128]{1,0:T(8,128)(2,1)S(1)}, bf16[1092,128]{1,0:T(8,128)(2,1)S(1)}, u32[]{:S(2)}, u32[]{:S(2)}) collective-permute-start(bf16[1092,128]{1,0:T(8,128)(2,1)S(1)} %add.214), channel_id=1, source_target_pairs={{0,2},{1,3},{2,0},{3,1},{4,6},{5,7},{6,4},{7,5},{8,10},{9,11},{10,... | collective-permute-start | bytes 838664 | tf_op jit(solution)/shard_map/ppermute | solution.py:48
  229.2 31.2 %attend_backward.1 = (bf16[4,512,768]{2,1,0:T(8,128)(2,1)S(1)}, f32[8,256]{1,0:T(8,128)S(1)}) custom-call(s32[7]{0:T(128)S(1)} %concatenate.39.info_ref, bf16[512,768]{1,0:T(8,128)(2,1)} %copy-done.2, bf16[512,768]{1,0:T(8,128)(2,1)} %copy-done.1, bf16[512,768]{1,0:T(8,128)(2,1)} %copy-done.3, bf16[512,768]{1,0:T(8,128)(2,1)} %copy-done.4, ...), custom_call_target="tpu_custom_call" | custom-call | flops 1024 | bytes 1024 | tf_op jit(solution)/shard_map/attend_backward/pallas_call | solution.py:378
  273.1 10.0 %collective-permute-done.24 = bf16[512,768]{1,0:T(8,128)(2,1)S(1)} collective-permute-done((bf16[512,768]{1,0:T(8,128)(2,1)S(1)}, bf16[512,768]{1,0:T(8,128)(2,1)S(1)}, u32[]{:S(2)}, u32[]{:S(2)}) %collective-permute-start.24) | collective-permute-done | bytes 786464 | tf_op jit(solution)/shard_map/ppermute | solution.py:52
  283.4 4.6 %in_grad.1 = f32[768,768]{1,0:T(8,128)S(1)} custom-call(bf16[4,512,768]{2,1,0:T(8,128)(2,1)S(1)} %get-tuple-element.157.d_ref, bf16[512,768]{1,0:T(8,128)(2,1)S(1)} %copy-done.8, bf16[512,768]{1,0:T(8,128)(2,1)S(1)} %copy-done.17, bf16[512,768]{1,0:T(8,128)(2,1)} %collective-permute-done.6.refs_2_, bf16[512,768]{1,0:T(8,128)(2,1)S(1)} %copy-done.19), custom_call_target="tpu_custom_call" | custom-call | flops 40000000000 | bytes 1024 | tf_op jit(solution)/shard_map/in_grad/pallas_call | solution.py:980
  300.3 3.9 %collective-permute-done.30 = bf16[1092,128]{1,0:T(8,128)(2,1)S(1)} collective-permute-done((bf16[1092,128]{1,0:T(8,128)(2,1)S(1)}, bf16[1092,128]{1,0:T(8,128)(2,1)S(1)}, u32[]{:S(2)}, u32[]{:S(2)}) %collective-permute-start.30) | collective-permute-done | bytes 279584 | tf_op jit(solution)/shard_map/ppermute | solution.py:48
  304.4 9.4 %collective-permute-done.25 = bf16[512,768]{1,0:T(8,128)(2,1)S(1)} collective-permute-done((bf16[512,768]{1,0:T(8,128)(2,1)S(1)}, bf16[512,768]{1,0:T(8,128)(2,1)S(1)}, u32[]{:S(2)}, u32[]{:S(2)}) %collective-permute-start.25) | collective-permute-done | bytes 786464 | tf_op jit(solution)/shard_map/ppermute | solution.py:52
  315.7 5.5 %collective-permute-done.32 = bf16[96,1728]{1,0:T(8,128)(2,1)S(1)} collective-permute-done((bf16[96,1728]{1,0:T(8,128)(2,1)S(1)}, bf16[96,1728]{1,0:T(8,128)(2,1)S(1)}, u32[]{:S(2)}, u32[]{:S(2)}) %collective-permute-start.32) | collective-permute-done | bytes 331808 | tf_op jit(solution)/shard_map/ppermute | solution.py:52
  328.8 4.3 %collective-permute-start.38 = (f32[16,768]{1,0:T(8,128)S(1)}, f32[16,768]{1,0:T(8,128)S(1)}, u32[]{:S(2)}, u32[]{:S(2)}) collective-permute-start(f32[16,768]{1,0:T(8,128)S(1)} %convert_add_fusion.4), channel_id=1, source_target_pairs={{0,2},{1,3},{2,0},{3,1},{4,6},{5,7},{6,4},{7,5},{8,10},{9,11},{10,... | collective-permute-start | bytes 147464 | tf_op jit(solution)/shard_map/ppermute | solution.py:52
  335.7 9.9 %collective-permute-done.34 = bf16[96,1728]{1,0:T(8,128)(2,1)} collective-permute-done((bf16[96,1728]{1,0:T(8,128)(2,1)}, bf16[96,1728]{1,0:T(8,128)(2,1)}, u32[]{:S(2)}, u32[]{:S(2)}) %collective-permute-start.34) | collective-permute-done | bytes 331808 | tf_op jit(solution)/shard_map/ppermute | solution.py:52
  352.9 3.9 %collective-permute-done.36 = bf16[96,1728]{1,0:T(8,128)(2,1)S(1)} collective-permute-done((bf16[96,1728]{1,0:T(8,128)(2,1)S(1)}, bf16[96,1728]{1,0:T(8,128)(2,1)S(1)}, u32[]{:S(2)}, u32[]{:S(2)}) %collective-permute-start.36) | collective-permute-done | bytes 331808 | tf_op jit(solution)/shard_map/ppermute | solution.py:52
  (247 shorter events, 89.7 us)
Async XLA Ops:
  7.2 142.0 %all-gather.5.cloned.1.call-start = ((), (), s32[]{:S(2)}) async-start(), calls=%async_computation | async-start | bytes 6193152 | tf_op jit(solution)/shard_map/all_gather | solution.py:1023
  25.2 124.0 %all-gather.7.cloned.1.call-start = ((), (), s32[]{:S(2)}) async-start(), calls=%async_computation.1 | async-start | bytes 6193152 | tf_op jit(solution)/shard_map/all_gather | solution.py:1023
  25.2 28.6 %collective-permute-start.4 = (bf16[512,768]{1,0:T(8,128)(2,1)S(1)}, bf16[512,768]{1,0:T(8,128)(2,1)S(1)}, u32[]{:S(2)}, u32[]{:S(2)}) collective-permute-start(bf16[512,768]{1,0:T(8,128)(2,1)S(1)} %copy-done.7), channel_id=1, source_target_pairs={{0,1},{1,2},{2,3},{3,0},{4,5},{5,6},{6,7},{7,4},{8,9},{9,10},{10,1... | collective-permute-start | bytes 2359304 | tf_op jit(solution)/shard_map/ppermute | solution.py:52
  25.4 28.5 %collective-permute-start.5 = (bf16[96,1728]{1,0:T(8,128)(2,1)S(1)}, bf16[96,1728]{1,0:T(8,128)(2,1)S(1)}, u32[]{:S(2)}, u32[]{:S(2)}) collective-permute-start(bf16[96,1728]{1,0:T(8,128)(2,1)S(1)} %collective-permute-done.2), channel_id=1, source_target_pairs={{0,1},{1,2},{2,3},{3,0},{4,5},{5,6},{6,7},{7,4},{8,9},{9,10},{10,1... | collective-permute-start | bytes 995336 | tf_op jit(solution)/shard_map/ppermute | solution.py:52
  65.6 19.5 %collective-permute-start.6 = (bf16[512,768]{1,0:T(8,128)(2,1)S(1)}, bf16[512,768]{1,0:T(8,128)(2,1)}, u32[]{:S(2)}, u32[]{:S(2)}) collective-permute-start(bf16[512,768]{1,0:T(8,128)(2,1)S(1)} %collective-permute-done.4.refs_1_), channel_id=1, source_target_pairs={{0,1},{1,2},{2,3},{3,0},{4,5},{5,6},{6,7},{7,4},{8,9},{9,10},{10,1... | collective-permute-start | bytes 2359304 | tf_op jit(solution)/shard_map/ppermute | solution.py:52
  85.2 18.7 %collective-permute-start.7 = (bf16[512,768]{1,0:T(8,128)(2,1)}, bf16[512,768]{1,0:T(8,128)(2,1)S(1)}, u32[]{:S(2)}, u32[]{:S(2)}) collective-permute-start(bf16[512,768]{1,0:T(8,128)(2,1)} %collective-permute-done.6.refs_2_), channel_id=1, source_target_pairs={{0,1},{1,2},{2,3},{3,0},{4,5},{5,6},{6,7},{7,4},{8,9},{9,10},{10,1... | collective-permute-start | bytes 2359304 | tf_op jit(solution)/shard_map/ppermute | solution.py:52
  130.0 19.1 %collective-permute-start.9 = (bf16[512,192]{1,0:T(8,128)(2,1)S(1)}, bf16[512,192]{1,0:T(8,128)(2,1)S(1)}, u32[]{:S(2)}, u32[]{:S(2)}) collective-permute-start(bf16[512,192]{1,0:T(8,128)(2,1)S(1)} %get-tuple-element.225), channel_id=1, source_target_pairs={{0,2},{1,3},{2,0},{3,1},{4,6},{5,7},{6,4},{7,5},{8,10},{9,11},{10,... | collective-permute-start | bytes 589832 | tf_op jit(solution)/shard_map/ppermute | solution.py:52
  207.8 15.3 %collective-permute-start.19 = (bf16[512,192]{1,0:T(8,128)(2,1)S(1)}, bf16[512,192]{1,0:T(8,128)(2,1)S(1)}, u32[]{:S(2)}, u32[]{:S(2)}) collective-permute-start(bf16[512,192]{1,0:T(8,128)(2,1)S(1)} %get-tuple-element.221), channel_id=1, source_target_pairs={{0,2},{1,3},{2,0},{3,1},{4,6},{5,7},{6,4},{7,5},{8,10},{9,11},{10,... | collective-permute-start | bytes 589832 | tf_op jit(solution)/shard_map/ppermute | solution.py:52
  208.8 14.4 %collective-permute-start.20 = (bf16[512,192]{1,0:T(8,128)(2,1)S(1)}, bf16[512,192]{1,0:T(8,128)(2,1)S(1)}, u32[]{:S(2)}, u32[]{:S(2)}) collective-permute-start(bf16[512,192]{1,0:T(8,128)(2,1)S(1)} %get-tuple-element.220), channel_id=1, source_target_pairs={{0,3},{1,0},{2,1},{3,2},{4,7},{5,4},{6,5},{7,6},{8,11},{9,8},{10,9... | collective-permute-start | bytes 589832 | tf_op jit(solution)/shard_map/ppermute | solution.py:52
  223.2 37.2 %collective-permute-start.21 = (bf16[2,2,96,1728]{3,2,0,1:T(8,128)(2,1)}, bf16[2,2,96,1728]{3,2,0,1:T(8,128)(2,1)}, u32[]{:S(2)}, u32[]{:S(2)}) collective-permute-start(bf16[2,2,96,1728]{3,2,0,1:T(8,128)(2,1)} %fusion.5), channel_id=1, source_target_pairs={{0,8},{4,12},{8,0},{12,4},{16,24},{20,28},{24,16},{28,20},{1,9},{5... | collective-permute-start | bytes 3981320 | tf_op jit(solution)/shard_map/ppermute | solution.py:48
  223.8 36.5 %collective-permute-start.22 = (bf16[2,2,96,1728]{3,2,0,1:T(8,128)(2,1)}, bf16[2,2,96,1728]{3,2,0,1:T(8,128)(2,1)}, u32[]{:S(2)}, u32[]{:S(2)}) collective-permute-start(bf16[2,2,96,1728]{3,2,0,1:T(8,128)(2,1)} %fusion.6), channel_id=1, source_target_pairs={{0,16},{4,20},{8,24},{12,28},{16,0},{20,4},{24,8},{28,12},{1,17},{... | collective-permute-start | bytes 3981320 | tf_op jit(solution)/shard_map/ppermute | solution.py:48
  224.7 35.6 %collective-permute-start.23 = (bf16[1092,128]{1,0:T(8,128)(2,1)S(1)}, bf16[1092,128]{1,0:T(8,128)(2,1)S(1)}, u32[]{:S(2)}, u32[]{:S(2)}) collective-permute-start(bf16[1092,128]{1,0:T(8,128)(2,1)S(1)} %add.214), channel_id=1, source_target_pairs={{0,2},{1,3},{2,0},{3,1},{4,6},{5,7},{6,4},{7,5},{8,10},{9,11},{10,... | collective-permute-start | bytes 838664 | tf_op jit(solution)/shard_map/ppermute | solution.py:48
  262.0 21.1 %collective-permute-start.24 = (bf16[512,768]{1,0:T(8,128)(2,1)S(1)}, bf16[512,768]{1,0:T(8,128)(2,1)S(1)}, u32[]{:S(2)}, u32[]{:S(2)}) collective-permute-start(bf16[512,768]{1,0:T(8,128)(2,1)S(1)} %first_rows.1), channel_id=1, source_target_pairs={{0,1},{1,2},{2,3},{3,0},{4,5},{5,6},{6,7},{7,4},{8,9},{9,10},{10,1... | collective-permute-start | bytes 2359304 | tf_op jit(solution)/shard_map/ppermute | solution.py:52
  267.0 21.0 %collective-permute-start.27 = (bf16[2,1,96,1728]{3,2,1,0:T(8,128)(2,1)S(1)}, bf16[2,1,96,1728]{3,2,1,0:T(8,128)(2,1)S(1)}, u32[]{:S(2)}, u32[]{:S(2)}) collective-permute-start(bf16[2,1,96,1728]{3,2,1,0:T(8,128)(2,1)S(1)} %fusion.11), channel_id=1, source_target_pairs={{0,8},{4,12},{8,0},{12,4},{16,24},{20,28},{24,16},{28,20},{1,9},{5... | collective-permute-start | bytes 1990664 | tf_op jit(solution)/shard_map/ppermute | solution.py:48
  269.8 18.2 %collective-permute-start.26 = (bf16[2,1,96,1728]{3,2,1,0:T(8,128)(2,1)S(1)}, bf16[2,1,96,1728]{3,2,1,0:T(8,128)(2,1)S(1)}, u32[]{:S(2)}, u32[]{:S(2)}) collective-permute-start(bf16[2,1,96,1728]{3,2,1,0:T(8,128)(2,1)S(1)} %fusion.10), channel_id=1, source_target_pairs={{0,16},{4,20},{8,24},{12,28},{16,0},{20,4},{24,8},{28,12},{1,17},{... | collective-permute-start | bytes 1990664 | tf_op jit(solution)/shard_map/ppermute | solution.py:48
  291.6 22.2 %collective-permute-start.25 = (bf16[512,768]{1,0:T(8,128)(2,1)S(1)}, bf16[512,768]{1,0:T(8,128)(2,1)S(1)}, u32[]{:S(2)}, u32[]{:S(2)}) collective-permute-start(bf16[512,768]{1,0:T(8,128)(2,1)S(1)} %fusion.2), channel_id=1, source_target_pairs={{0,1},{1,2},{2,3},{3,0},{4,5},{5,6},{6,7},{7,4},{8,9},{9,10},{10,1... | collective-permute-start | bytes 2359304 | tf_op jit(solution)/shard_map/ppermute | solution.py:52
  293.2 28.0 %collective-permute-start.32 = (bf16[96,1728]{1,0:T(8,128)(2,1)S(1)}, bf16[96,1728]{1,0:T(8,128)(2,1)S(1)}, u32[]{:S(2)}, u32[]{:S(2)}) collective-permute-start(bf16[96,1728]{1,0:T(8,128)(2,1)S(1)} %fusion.17), channel_id=1, source_target_pairs={{0,1},{1,2},{2,3},{3,0},{4,5},{5,6},{6,7},{7,4},{8,9},{9,10},{10,1... | collective-permute-start | bytes 995336 | tf_op jit(solution)/shard_map/ppermute | solution.py:52
  298.1 16.8 %collective-permute-start.33 = (bf16[208,768]{1,0:T(8,128)(2,1)S(1)}, bf16[208,768]{1,0:T(8,128)(2,1)S(1)}, u32[]{:S(2)}, u32[]{:S(2)}) collective-permute-start(bf16[208,768]{1,0:T(8,128)(2,1)S(1)} %pad_maximum_fusion.4), channel_id=1, source_target_pairs={{0,8},{4,12},{8,0},{12,4},{16,24},{20,28},{24,16},{28,20},{1,9},{5... | collective-permute-start | bytes 958472 | tf_op jit(solution)/shard_map/ppermute | solution.py:48
  304.3 17.7 %collective-permute-start.40 = (bf16[1092,128]{1,0:T(8,128)(2,1)S(1)}, bf16[1092,128]{1,0:T(8,128)(2,1)S(1)}, u32[]{:S(2)}, u32[]{:S(2)}) collective-permute-start(bf16[1092,128]{1,0:T(8,128)(2,1)S(1)} %add.231), channel_id=1, source_target_pairs={{0,16},{4,20},{8,24},{12,28},{16,0},{20,4},{24,8},{28,12},{1,17},{... | collective-permute-start | bytes 838664 | tf_op jit(solution)/shard_map/ppermute | solution.py:48
  314.9 35.0 %collective-permute-start.31 = (bf16[512,768]{1,0:T(8,128)(2,1)}, bf16[512,768]{1,0:T(8,128)(2,1)}, u32[]{:S(2)}, u32[]{:S(2)}) collective-permute-start(bf16[512,768]{1,0:T(8,128)(2,1)} %fusion.3), channel_id=1, source_target_pairs={{0,1},{1,2},{2,3},{3,0},{4,5},{5,6},{6,7},{7,4},{8,9},{9,10},{10,1... | collective-permute-start | bytes 2359304 | tf_op jit(solution)/shard_map/ppermute | solution.py:52
  322.0 23.7 %collective-permute-start.34 = (bf16[96,1728]{1,0:T(8,128)(2,1)}, bf16[96,1728]{1,0:T(8,128)(2,1)}, u32[]{:S(2)}, u32[]{:S(2)}) collective-permute-start(bf16[96,1728]{1,0:T(8,128)(2,1)} %fusion.14), channel_id=1, source_target_pairs={{0,1},{1,2},{2,3},{3,0},{4,5},{5,6},{6,7},{7,4},{8,9},{9,10},{10,1... | collective-permute-start | bytes 995336 | tf_op jit(solution)/shard_map/ppermute | solution.py:52
  328.7 18.3 %collective-permute-start.37 = (f32[16,768]{1,0:T(8,128)S(1)}, f32[16,768]{1,0:T(8,128)S(1)}, u32[]{:S(2)}, u32[]{:S(2)}) collective-permute-start(f32[16,768]{1,0:T(8,128)S(1)} %convert_add_fusion.4), channel_id=1, source_target_pairs={{0,1},{1,2},{2,3},{3,0},{4,5},{5,6},{6,7},{7,4},{8,9},{9,10},{10,1... | collective-permute-start | bytes 147464 | tf_op jit(solution)/shard_map/ppermute | solution.py:52
  328.8 18.9 %collective-permute-start.38 = (f32[16,768]{1,0:T(8,128)S(1)}, f32[16,768]{1,0:T(8,128)S(1)}, u32[]{:S(2)}, u32[]{:S(2)}) collective-permute-start(f32[16,768]{1,0:T(8,128)S(1)} %convert_add_fusion.4), channel_id=1, source_target_pairs={{0,2},{1,3},{2,0},{3,1},{4,6},{5,7},{6,4},{7,5},{8,10},{9,11},{10,... | collective-permute-start | bytes 147464 | tf_op jit(solution)/shard_map/ppermute | solution.py:52
  333.1 14.7 %collective-permute-start.39 = (f32[16,768]{1,0:T(8,128)S(1)}, f32[16,768]{1,0:T(8,128)S(1)}, u32[]{:S(2)}, u32[]{:S(2)}) collective-permute-start(f32[16,768]{1,0:T(8,128)S(1)} %convert_add_fusion.4), channel_id=1, source_target_pairs={{0,3},{1,0},{2,1},{3,2},{4,7},{5,4},{6,5},{7,6},{8,11},{9,8},{10,9... | collective-permute-start | bytes 147464 | tf_op jit(solution)/shard_map/ppermute | solution.py:52
  (62 other events, 652.2 us)
Sparse Core Ops, SparseCore 0:
  25.3 41.5 all-gather.4
  69.4 42.2 all-gather.6

commit v4 on v3

--- a/solution.py
+++ b/solution.py
@@ -116,11 +116,14 @@
         got = yield give, swapped(give, axis, size, bit)
         parts = keep + got[:-riding].reshape(keep.shape).astype(F32)
         rider = rider.astype(BF16).astype(F32) + got[-riding:].astype(F32)
+    rider = rider[:2]
     got = yield rider, [shifted(rider, other, other_size, by) for by in range(1, other_size)]
-    place = lax.axis_index(other)
-    riders = jnp.zeros((other_size, *rider.shape), F32)
+    index = lax.axis_index(other)
+    places = jnp.arange(other_size)[:, None, None]
+    riders = 0.0
     for by, value in enumerate([rider] + list(got)):
-        riders = lax.dynamic_update_index_in_dim(riders, value, (place - by) % other_size, 0)
+        mine = places == (index - by) % other_size
+        riders = riders + jnp.where(mine, value[None], 0.0)
     return parts[0], riders
 
 
@@ -218,9 +221,8 @@
         )
         last = i // 2
         state = lax.fori_loop(0, last, lambda j, c: step(j, c, False), state)
-        state = step(last, state, True)
         tops, totals, mixed = lax.fori_loop(
-            last + 1, (stop + 1) // 2, lambda j, c: step(j, c, True), state
+            last, (stop + 1) // 2, lambda j, c: step(j, c, True), state
         )
         outs = [mixed[h] * (1.0 / totals[h]) for h in range(heads)]
         lses = [tops[h] + jnp.log(totals[h]) for h in range(heads)]
@@ -439,25 +441,31 @@
     ) = refs[tensor + 5 + arrays :]
     j = pl.program_id(0)
     hidden = act_ref.shape[2]
+    rows = tok_ref.shape[0]
+    half = min(256, rows)
 
     @pl.when(j == 0)
     def _():
         start_weights(pieces, w_s, wo_s, sems, o_sem)
-        total = tok_ref[...].astype(F32) + vec_ref[2:3, :]
         pltpu.make_async_copy(wo_s, wo_s, o_sem).wait()
-        for s in range(tensor):
-            piece = mixed[s][...]
-            total = total + dot_nt(piece, wo_s[s])
-        centered, rstd = center(total)
-        xhat = centered * rstd
-        xh1_ref[...] = xhat
-        rs_ref[:, 0:1] = rstd
-        x_one = xhat * vec_ref[3:4, :] + vec_ref[4:5, :]
-        xlow_ref[...] = x_one.astype(BF16)
-        acc_s[...] = x_one + vec_ref[5:6, :]
+
+        def first_part(n, carry):
+            here = pl.ds(n * half, half)
+            total = tok_ref[here, :].astype(F32) + vec_ref[2:3, :]
+            for s in range(tensor):
+                total = total + dot_nt(mixed[s][here, :], wo_s[s])
+            centered, rstd = center(total)
+            xhat = centered * rstd
+            xh1_ref[here, :] = xhat
+            rs_ref[here, 0:1] = rstd
+            x_one = xhat * vec_ref[3:4, :] + vec_ref[4:5, :]
+            xlow_ref[here, :] = x_one.astype(BF16)
+            acc_s[here, :] = x_one + vec_ref[5:6, :]
+            return carry
+
+        lax.fori_loop(0, rows // half, first_part, 0)
 
     pltpu.make_async_copy(w_s.at[j], w_s.at[j], sems.at[j]).wait()
-    half = min(256, xlow_ref.shape[0])
 
     def rows_part(n, carry):
         here = pl.ds(n * half, half)
@@ -470,18 +478,23 @@
         acc_s[here, :] = acc_s[here, :] + dot_nt(act, w_s[j, :, hidden:])
         return carry
 
-    lax.fori_loop(0, xlow_ref.shape[0] // half, rows_part, 0)
+    lax.fori_loop(0, rows // half, rows_part, 0)
 
     @pl.when(j == pl.num_programs(0) - 1)
     def _():
-        centered, rstd = center(acc_s[...])
-        xhat = centered * rstd
-        xh2_ref[...] = xhat
-        rs_ref[:, 1:2] = rstd
-        low = (xhat * vec_ref[6:7, :] + vec_ref[7:8, :]).astype(BF16)
-        low_ref[...] = low
-        student = dot_nn(low, proj_ref[...]) + cvec_ref[0:1, :]
-        stud_ref[...] = student
+        def last_part(n, carry):
+            here = pl.ds(n * half, half)
+            centered, rstd = center(acc_s[here, :])
+            xhat = centered * rstd
+            xh2_ref[here, :] = xhat
+            rs_ref[here, 1:2] = rstd
+            low = (xhat * vec_ref[6:7, :] + vec_ref[7:8, :]).astype(BF16)
+            low_ref[here, :] = low
+            stud_ref[here, :] = dot_nn(low, proj_ref[...]) + cvec_ref[0:1, :]
+            return carry
+
+        lax.fori_loop(0, rows // half, last_part, 0)
+        student = stud_ref[...]
         width = student.shape[1]
         scale = (width // POOL_HEADS) ** (-0.5)
         e = dot_nn(student * (cvec_ref[1:2, :] * scale), same_head(width), PRECISE)
@@ -586,14 +599,15 @@
     ) = refs[tensor : tensor + 14]
     pieces = refs[tensor + 14 : tensor + 14 + arrays]
     (
-        logit_ref, two_ref, gu_ref, one_ref, gh1_ref, gm_ref, small_ref, acc_s, pack_ref, w_s,
-        wo_s, sems, o_sem,
+        logit_ref, two_ref, gu_ref, one_ref, gh1_ref, gm_ref, small_ref, acc_s, pack_ref, gsl_s,
+        w_s, wo_s, sems, o_sem,
     ) = refs[tensor + 14 + arrays :]
     j = pl.program_id(0)
     ch = stud_ref.shape[1]
     hidden = gu_ref.shape[2]
     scale = (ch // POOL_HEADS) ** (-0.5)
-    width = cot_ref.shape[1]
+    rows, width = cot_ref.shape
+    half = min(256, rows)
     sums_at = 8 + 2 * ch
     bias_at = sums_at + 6 * (width // ch)
 
@@ -652,18 +666,24 @@
             ],
             axis=0,
         )
-        grad = cot_ref[...].astype(F32) + dot_nt(gsl, proj_ref[...])
-        xhat = xh2_ref[...]
-        pack_row(6, jnp.sum(grad * xhat, axis=0, keepdims=True))
-        pack_row(7, jnp.sum(grad, axis=0, keepdims=True))
-        two = norm_back(grad, xhat, rs_ref[:, 1:2], vec_ref[6:7, :])
-        pack_row(5, jnp.sum(two, axis=0, keepdims=True))
-        acc_s[...] = two
-        two_ref[...] = two.astype(BF16)
+        gsl_s[...] = gsl
+
+        def first_part(n, sums):
+            here = pl.ds(n * half, half)
+            grad = cot_ref[here, :].astype(F32) + dot_nt(gsl_s[here, :], proj_ref[...])
+            xhat = xh2_ref[here, :]
+            two = norm_back(grad, xhat, rs_ref[here, 1:2], vec_ref[6:7, :])
+            acc_s[here, :] = two
+            two_ref[here, :] = two.astype(BF16)
+            parts = (two, grad * xhat, grad)
+            return tuple(s + jnp.sum(v, axis=0, keepdims=True) for s, v in zip(sums, parts))
+
+        sums = lax.fori_loop(0, rows // half, first_part, (jnp.zeros((1, width), F32),) * 3)
+        for n in range(3):
+            pack_row(5 + n, sums[n])
 
     pltpu.make_async_copy(w_s.at[j], w_s.at[j], sems.at[j]).wait()
     heads_row = part_of(info_ref, j, tensor)
-    half = min(256, two_ref.shape[0])
 
     def rows_part(n, bias_row):
         here = pl.ds(n * half, half)
@@ -674,7 +694,7 @@
         return bias_row + jnp.sum(upper, axis=0, keepdims=True)
 
     bias_row = lax.fori_loop(
-        0, two_ref.shape[0] // half, rows_part, jnp.zeros((1, hidden), F32)
+        0, rows // half, rows_part, jnp.zeros((1, hidden), F32)
     )
     for n in range(hidden // ch):
         pack_ref[pl.ds(bias_at + heads_row * (hidden // ch) + n, 1), :] = bias_row[
@@ -683,18 +703,24 @@
 
     @pl.when(j == pl.num_programs(0) - 1)
     def _():
-        grad = acc_s[...]
-        xhat = xh1_ref[...]
-        pack_row(3, jnp.sum(grad * xhat, axis=0, keepdims=True))
-        pack_row(4, jnp.sum(grad, axis=0, keepdims=True))
-        one = norm_back(grad, xhat, rs_ref[:, 0:1], vec_ref[3:4, :])
-        pack_row(2, jnp.sum(one, axis=0, keepdims=True))
-        gh1_ref[...] = one
-        low = one.astype(BF16)
-        one_ref[...] = low
         pltpu.make_async_copy(wo_s, wo_s, o_sem).wait()
-        for s in range(tensor):
-            gm_ref[s] = dot_nn(low, wo_s[s]).astype(BF16)
+
+        def last_part(n, sums):
+            here = pl.ds(n * half, half)
+            grad = acc_s[here, :]
+            xhat = xh1_ref[here, :]
+            one = norm_back(grad, xhat, rs_ref[here, 0:1], vec_ref[3:4, :])
+            gh1_ref[here, :] = one
+            low = one.astype(BF16)
+            one_ref[here, :] = low
+            for s in range(tensor):
+                gm_ref[s, here, :] = dot_nn(low, wo_s[s]).astype(BF16)
+            parts = (one, grad * xhat, grad)
+            return tuple(s + jnp.sum(v, axis=0, keepdims=True) for s, v in zip(sums, parts))
+
+        sums = lax.fori_loop(0, rows // half, last_part, (jnp.zeros((1, width), F32),) * 3)
+        for n in range(3):
+            pack_row(2 + n, sums[n])
         small_ref[width:, :] = pack_ref[...].astype(BF16)
 
 
@@ -745,6 +771,7 @@
             scratch_shapes=[
                 pltpu.VMEM((rows, width), F32),
                 pltpu.VMEM((pack_rows, ch), F32),
+                pltpu.VMEM((rows, ch), BF16),
                 pltpu.VMEM((tensor, width, 2 * hidden), BF16),
                 pltpu.VMEM((tensor, width, head_width), BF16),
                 pltpu.SemaphoreType.DMA((tensor,)),
@@ -1120,9 +1147,9 @@
             "small": small_chain(),
         },
         [
-            ("rows",), ("rows",), ("in",), ("ff",), ("in",), ("small",), ("in",), ("small",),
-            ("rows",), ("in",), ("ff",), ("small",), ("in",), ("ff",), ("in",), ("small",),
-            ("rows",), ("ff",),
+            ("rows",), ("rows",), ("ff",), ("in",), ("in",), ("small",), ("rows",), ("in",),
+            ("small",), ("ff",), ("in",), ("small",), ("in",), ("ff",), ("in",), ("rows",),
+            ("ff",),
         ],
     )
     grad_w_qkv = grad_in.reshape(shard, 3, padded)[:, :, :local]

time: 365 us -> 359 us (0.984); the launches traced: 365 us -> 355 us
  other arithmetic: 27.2 us -> 21.6 us
  starting transfers between devices: 38 us -> 43.1 us
  waiting for transfers between devices: 149 us -> 145 us
    ppermute x24, waiting for transfers between devices: 133 us -> 122 us  [shifted(): lax.ppermute(value, axis, [(i, (i + by) % size) for i in range(size)])]
    ppermute x17, starting transfers between devices: 13.6 us -> 20.5 us  [swapped(): return lax.ppermute(value, axis, [(i, i ^ bit) for i in range(size)])]
    ppermute x17, waiting for transfers between devices: 16.7 us -> 23.1 us  [swapped(): return lax.ppermute(value, axis, [(i, i ^ bit) for i in range(size)])]
    reshape x2, other arithmetic: 4.57 us -> 0.89 us  [split_by(): pairs = value.reshape(shape[0], high, 2, low, *shape[2:])]
  transfers between devices with their start and end apart: 43 -> 43, of which waited for: 19 -> 24; matrix products, arithmetic and copies ran while one was open for 12% -> 9% of each run, Pallas kernels for 19% -> 19%
where the time goes in v4:
time: 359 us; the launch traced here: 355 us
  waiting for transfers between devices  145 us (40%)
  Pallas kernels  107 us (30%)
  starting transfers between devices  43.1 us (12%)
  other arithmetic  21.6 us (6%)
  local copies, waits for them, and re-layouts  19.5 us (5%)
  between operations  15.6 us (4%)
    ppermute x24, waiting for transfers between devices, shifted(): lax.ppermute(value, axis, [(i, (i + by) % size) for i in range(size)])  122 us
    pallas_call x1, Pallas kernels, attend_backward(): pl.pallas_call(functools.partial(attend_backward_kernel, heads), out_shap...  31.2 us
    ppermute x17, waiting for transfers between devices, swapped(): return lax.ppermute(value, axis, [(i, i ^ bit) for i in range(size)])  23.1 us
    ppermute x24, starting transfers between devices, shifted(): lax.ppermute(value, axis, [(i, (i + by) % size) for i in range(size)])  22.6 us
    pallas_call x1, Pallas kernels, attend_forward(): pl.pallas_call(functools.partial(attend_forward_kernel, heads), out_shape...  21.8 us
    ppermute x17, starting transfers between devices, swapped(): return lax.ppermute(value, axis, [(i, i ^ bit) for i in range(size)])  20.5 us
    pallas_call x1, Pallas kernels, rows_forward(): pl.pallas_call(functools.partial(rows_forward_kernel, tensor, len(pieces)...  20.4 us
    pallas_call x1, Pallas kernels, rows_backward(): pl.pallas_call(functools.partial(rows_backward_kernel, tensor, len(pieces...  16.3 us
  transfers between devices with their start and end apart: 43, of which 24 were waited for; matrix products, arithmetic and copies ran while one was open for 9% of the time, Pallas kernels for 19%

profile of v4, /device:TPU:0, one launch (start us, length us, event | category | flops | bytes accessed | tf_op | source)
XLA Modules:
  0.0 355.2 jit_solution(14462811669957725653)
XLA Ops:
  15.1 9.1 %collective-permute-done.2 = bf16[96,1728]{1,0:T(8,128)(2,1)S(1)} collective-permute-done((bf16[96,1728]{1,0:T(8,128)(2,1)S(1)}, bf16[96,1728]{1,0:T(8,128)(2,1)S(1)}, u32[]{:S(2)}, u32[]{:S(2)}) %collective-permute-start.2) | collective-permute-done | bytes 331808 | tf_op jit(solution)/shard_map/ppermute | solution.py:52
  27.0 26.9 %collective-permute-done.5 = bf16[96,1728]{1,0:T(8,128)(2,1)S(1)} collective-permute-done((bf16[96,1728]{1,0:T(8,128)(2,1)S(1)}, bf16[96,1728]{1,0:T(8,128)(2,1)S(1)}, u32[]{:S(2)}, u32[]{:S(2)}) %collective-permute-start.5) | collective-permute-done | bytes 331808 | tf_op jit(solution)/shard_map/ppermute | solution.py:52
  53.9 10.8 %collective-permute-done.11 = bf16[96,1728]{1,0:T(8,128)(2,1)S(1)} collective-permute-done((bf16[96,1728]{1,0:T(8,128)(2,1)S(1)}, bf16[96,1728]{1,0:T(8,128)(2,1)S(1)}, u32[]{:S(2)}, u32[]{:S(2)}) %collective-permute-start.11) | collective-permute-done | bytes 331808 | tf_op jit(solution)/shard_map/ppermute | solution.py:52
  69.3 11.9 %collective-permute-done.3 = bf16[384,768]{1,0:T(8,128)(2,1)} collective-permute-done((bf16[384,768]{1,0:T(8,128)(2,1)S(1)}, bf16[384,768]{1,0:T(8,128)(2,1)}, u32[]{:S(2)}, u32[]{:S(2)}) %collective-permute-start.3) | collective-permute-done | bytes 589856 | tf_op jit(solution)/shard_map/ppermute | solution.py:48
  87.5 16.0 %collective-permute-done.7.refs_3_ = bf16[512,768]{1,0:T(8,128)(2,1)S(1)} collective-permute-done((bf16[512,768]{1,0:T(8,128)(2,1)S(1)}, bf16[512,768]{1,0:T(8,128)(2,1)S(1)}, u32[]{:S(2)}, u32[]{:S(2)}) %collective-permute-start.7) | collective-permute-done | bytes 786464 | tf_op jit(solution)/shard_map/ppermute | solution.py:52
  105.3 21.8 %attend_forward.1 = (bf16[4,512,192]{2,1,0:T(8,128)(2,1)S(1)}, f32[8,8,256]{2,1,0:T(8,128)S(1)}) custom-call(s32[7]{0:T(128)S(1)} %concatenate.39.info_ref, bf16[512,768]{1,0:T(8,128)(2,1)S(1)} %fusion.9.refs_0_, bf16[512,768]{1,0:T(8,128)(2,1)S(1)} %add_convert_fusion.4.refs_1_, bf16[512,768]{1,0:T(8,128)(2,1)S(1)} %add_convert_fusion.3.refs_2_, ...), custom_call_target="tpu_custom_call" | custom-call | flops 1024 | bytes 1024 | tf_op jit(solution)/shard_map/attend_forward/pallas_call | solution.py:246
  130.9 5.5 %collective-permute-done.10.refs_3_ = bf16[512,192]{1,0:T(8,128)(2,1)S(1)} collective-permute-done((bf16[512,192]{1,0:T(8,128)(2,1)S(1)}, bf16[512,192]{1,0:T(8,128)(2,1)S(1)}, u32[]{:S(2)}, u32[]{:S(2)}) %collective-permute-start.10) | collective-permute-done | bytes 196640 | tf_op jit(solution)/shard_map/ppermute | solution.py:52
  139.1 8.4 %collective-permute-done.9.refs_2_ = bf16[512,192]{1,0:T(8,128)(2,1)S(1)} collective-permute-done((bf16[512,192]{1,0:T(8,128)(2,1)S(1)}, bf16[512,192]{1,0:T(8,128)(2,1)S(1)}, u32[]{:S(2)}, u32[]{:S(2)}) %collective-permute-start.9) | collective-permute-done | bytes 196640 | tf_op jit(solution)/shard_map/ppermute | solution.py:52
  148.3 20.4 %rows_forward.1 = (bf16[512,768]{1,0:T(8,128)(2,1)}, bf16[512,768]{1,0:T(8,128)(2,1)}, bf16[4,512,768]{2,1,0:T(8,128)(2,1)}, bf16[4,512,768]{2,1,0:T(8,128)(2,1)...) custom-call(s32[7]{0:T(128)S(1)} %concatenate.39.info_ref, ...), custom_call_target="tpu_custom_call" | custom-call | flops 1024 | bytes 1024 | tf_op jit(solution)/shard_map/rows_forward/pallas_call | solution.py:534
  169.0 3.4 collective-permute-start.13
  176.0 16.3 %rows_backward.1 = (f32[8,128]{1,0:T(8,128)S(1)}, bf16[512,768]{1,0:T(8,128)(2,1)S(1)}, bf16[4,512,768]{2,1,0:T(8,128)(2,1)S(1)}, bf16[512,768]{1,0:T(8,128)(2,1...) custom-call(s32[7]{0:T(128)S(1)} %concatenate.39.info_ref, ...), custom_call_target="tpu_custom_call" | custom-call | flops 1024 | bytes 1024 | tf_op jit(solution)/shard_map/rows_backward/pallas_call | solution.py:739
  195.2 9.9 %weight_grads.1 = (bf16[2,4,96,1728]{3,2,1,0:T(8,128)(2,1)S(1)}, bf16[2,4,96,1728]{3,2,1,0:T(8,128)(2,1)S(1)}, bf16[2,4,96,1728]{3,2,1,0:T(8,128)(2,1)S(1)}, bf16[2,4,96,1728]{3,2,1,0:T(8,128)(2,1)S(1)}) custom-call(s32[7]{0:T(128)S(1)} %concatenate.39.info_ref, bf16[512,768]{1,0:T(8,128)(2,1)} %get-tuple-element.114.x_ref, ...), custom_call_target="tpu_custom_call" | custom-call | flops 1024 | bytes 1024 | tf_op jit(solution)/shard_map/weight_grads/pallas_call | solution.py:857
  210.6 3.6 %collective-permute-done.17 = bf16[2,4,96,1728]{3,2,1,0:T(8,128)(2,1)S(1)} collective-permute-done((bf16[2,4,96,1728]{3,2,1,0:T(8,128)(2,1)S(1)}, bf16[2,4,96,1728]{3,2,1,0:T(8,128)(2,1)S(1)}, u32[]{:S(2)}, u32[]{:S(2)}) %collective-permute-start.17) | collective-permute-done | bytes 2654240 | tf_op jit(solution)/shard_map/ppermute | solution.py:48
  214.6 6.6 %collective-permute-done.19.refs_6_ = bf16[512,192]{1,0:T(8,128)(2,1)S(1)} collective-permute-done((bf16[512,192]{1,0:T(8,128)(2,1)S(1)}, bf16[512,192]{1,0:T(8,128)(2,1)S(1)}, u32[]{:S(2)}, u32[]{:S(2)}) %collective-permute-start.19) | collective-permute-done | bytes 196640 | tf_op jit(solution)/shard_map/ppermute | solution.py:52
  221.2 3.4 collective-permute-start.21
  224.6 4.5 %collective-permute-start.23 = (bf16[1092,128]{1,0:T(8,128)(2,1)S(1)}, bf16[1092,128]{1,0:T(8,128)(2,1)S(1)}, u32[]{:S(2)}, u32[]{:S(2)}) collective-permute-start(bf16[1092,128]{1,0:T(8,128)(2,1)S(1)} %add.210), channel_id=1, source_target_pairs={{0,2},{1,3},{2,0},{3,1},{4,6},{5,7},{6,4},{7,5},{8,10},{9,11},{10,... | collective-permute-start | bytes 838664 | tf_op jit(solution)/shard_map/ppermute | solution.py:48
  229.0 31.2 %attend_backward.1 = (bf16[4,512,768]{2,1,0:T(8,128)(2,1)S(1)}, f32[8,256]{1,0:T(8,128)S(1)}) custom-call(s32[7]{0:T(128)S(1)} %concatenate.39.info_ref, bf16[512,768]{1,0:T(8,128)(2,1)} %copy-done.6, bf16[512,768]{1,0:T(8,128)(2,1)} %copy-done.5, bf16[512,768]{1,0:T(8,128)(2,1)} %copy-done.7, bf16[512,768]{1,0:T(8,128)(2,1)} %copy-done.8, ...), custom_call_target="tpu_custom_call" | custom-call | flops 1024 | bytes 1024 | tf_op jit(solution)/shard_map/attend_backward/pallas_call | solution.py:380
  269.1 4.3 %collective-permute-start.26 = (bf16[2,1,96,1728]{3,2,1,0:T(8,128)(2,1)}, bf16[2,1,96,1728]{3,2,1,0:T(8,128)(2,1)}, u32[]{:S(2)}, u32[]{:S(2)}) collective-permute-start(bf16[2,1,96,1728]{3,2,1,0:T(8,128)(2,1)} %fusion.10), channel_id=1, source_target_pairs={{0,16},{4,20},{8,24},{12,28},{16,0},{20,4},{24,8},{28,12},{1,17},{... | collective-permute-start | bytes 1990664 | tf_op jit(solution)/shard_map/ppermute | solution.py:48
  288.8 3.4 in_grad.1
  295.3 10.2 %collective-permute-done.25 = bf16[512,768]{1,0:T(8,128)(2,1)S(1)} collective-permute-done((bf16[512,768]{1,0:T(8,128)(2,1)S(1)}, bf16[512,768]{1,0:T(8,128)(2,1)S(1)}, u32[]{:S(2)}, u32[]{:S(2)}) %collective-permute-start.25) | collective-permute-done | bytes 786464 | tf_op jit(solution)/shard_map/ppermute | solution.py:52
  309.6 3.2 collective-permute-done.30
  322.0 3.7 %collective-permute-start.38 = (f32[2,768]{1,0:T(2,128)S(1)}, f32[2,768]{1,0:T(2,128)S(1)}, u32[]{:S(2)}, u32[]{:S(2)}) collective-permute-start(f32[2,768]{1,0:T(2,128)S(1)} %convert_add_fusion.4), channel_id=1, source_target_pairs={{0,2},{1,3},{2,0},{3,1},{4,6},{5,7},{6,4},{7,5},{8,10},{9,11},{10,... | collective-permute-start | bytes 18440 | tf_op jit(solution)/shard_map/ppermute | solution.py:52
  325.6 8.9 %collective-permute-done.33 = bf16[96,1728]{1,0:T(8,128)(2,1)} collective-permute-done((bf16[96,1728]{1,0:T(8,128)(2,1)}, bf16[96,1728]{1,0:T(8,128)(2,1)}, u32[]{:S(2)}, u32[]{:S(2)}) %collective-permute-start.33) | collective-permute-done | bytes 331808 | tf_op jit(solution)/shard_map/ppermute | solution.py:52
  340.7 5.0 %collective-permute-done.36 = bf16[96,1728]{1,0:T(8,128)(2,1)} collective-permute-done((bf16[96,1728]{1,0:T(8,128)(2,1)}, bf16[96,1728]{1,0:T(8,128)(2,1)}, u32[]{:S(2)}, u32[]{:S(2)}) %collective-permute-start.36) | collective-permute-done | bytes 331808 | tf_op jit(solution)/shard_map/ppermute | solution.py:52
  (247 shorter events, 91.2 us)
Async XLA Ops:
  7.2 140.4 %all-gather.5.cloned.1.call-start = ((), (), s32[]{:S(2)}) async-start(), calls=%async_computation | async-start | bytes 6193152 | tf_op jit(solution)/shard_map/all_gather | solution.py:1050
  25.2 122.3 %all-gather.7.cloned.1.call-start = ((), (), s32[]{:S(2)}) async-start(), calls=%async_computation.1 | async-start | bytes 6193152 | tf_op jit(solution)/shard_map/all_gather | solution.py:1050
  25.3 28.6 %collective-permute-start.4 = (bf16[512,768]{1,0:T(8,128)(2,1)S(1)}, bf16[512,768]{1,0:T(8,128)(2,1)S(1)}, u32[]{:S(2)}, u32[]{:S(2)}) collective-permute-start(bf16[512,768]{1,0:T(8,128)(2,1)S(1)} %copy-done.11), channel_id=1, source_target_pairs={{0,1},{1,2},{2,3},{3,0},{4,5},{5,6},{6,7},{7,4},{8,9},{9,10},{10,1... | collective-permute-start | bytes 2359304 | tf_op jit(solution)/shard_map/ppermute | solution.py:52
  25.4 28.5 %collective-permute-start.5 = (bf16[96,1728]{1,0:T(8,128)(2,1)S(1)}, bf16[96,1728]{1,0:T(8,128)(2,1)S(1)}, u32[]{:S(2)}, u32[]{:S(2)}) collective-permute-start(bf16[96,1728]{1,0:T(8,128)(2,1)S(1)} %collective-permute-done.2), channel_id=1, source_target_pairs={{0,1},{1,2},{2,3},{3,0},{4,5},{5,6},{6,7},{7,4},{8,9},{9,10},{10,1... | collective-permute-start | bytes 995336 | tf_op jit(solution)/shard_map/ppermute | solution.py:52
  65.7 19.4 %collective-permute-start.6 = (bf16[512,768]{1,0:T(8,128)(2,1)S(1)}, bf16[512,768]{1,0:T(8,128)(2,1)S(1)}, u32[]{:S(2)}, u32[]{:S(2)}) collective-permute-start(bf16[512,768]{1,0:T(8,128)(2,1)S(1)} %collective-permute-done.4.refs_1_), channel_id=1, source_target_pairs={{0,1},{1,2},{2,3},{3,0},{4,5},{5,6},{6,7},{7,4},{8,9},{9,10},{10,1... | collective-permute-start | bytes 2359304 | tf_op jit(solution)/shard_map/ppermute | solution.py:52
  85.1 18.5 %collective-permute-start.7 = (bf16[512,768]{1,0:T(8,128)(2,1)S(1)}, bf16[512,768]{1,0:T(8,128)(2,1)S(1)}, u32[]{:S(2)}, u32[]{:S(2)}) collective-permute-start(bf16[512,768]{1,0:T(8,128)(2,1)S(1)} %collective-permute-done.6.refs_2_), channel_id=1, source_target_pairs={{0,1},{1,2},{2,3},{3,0},{4,5},{5,6},{6,7},{7,4},{8,9},{9,10},{10,1... | collective-permute-start | bytes 2359304 | tf_op jit(solution)/shard_map/ppermute | solution.py:52
  130.9 16.6 %collective-permute-start.9 = (bf16[512,192]{1,0:T(8,128)(2,1)S(1)}, bf16[512,192]{1,0:T(8,128)(2,1)S(1)}, u32[]{:S(2)}, u32[]{:S(2)}) collective-permute-start(bf16[512,192]{1,0:T(8,128)(2,1)S(1)} %get-tuple-element.225), channel_id=1, source_target_pairs={{0,2},{1,3},{2,0},{3,1},{4,6},{5,7},{6,4},{7,5},{8,10},{9,11},{10,... | collective-permute-start | bytes 589832 | tf_op jit(solution)/shard_map/ppermute | solution.py:52
  205.7 15.4 %collective-permute-start.19 = (bf16[512,192]{1,0:T(8,128)(2,1)S(1)}, bf16[512,192]{1,0:T(8,128)(2,1)S(1)}, u32[]{:S(2)}, u32[]{:S(2)}) collective-permute-start(bf16[512,192]{1,0:T(8,128)(2,1)S(1)} %get-tuple-element.221), channel_id=1, source_target_pairs={{0,2},{1,3},{2,0},{3,1},{4,6},{5,7},{6,4},{7,5},{8,10},{9,11},{10,... | collective-permute-start | bytes 589832 | tf_op jit(solution)/shard_map/ppermute | solution.py:52
  206.6 14.5 %collective-permute-start.20 = (bf16[512,192]{1,0:T(8,128)(2,1)S(1)}, bf16[512,192]{1,0:T(8,128)(2,1)S(1)}, u32[]{:S(2)}, u32[]{:S(2)}) collective-permute-start(bf16[512,192]{1,0:T(8,128)(2,1)S(1)} %get-tuple-element.220), channel_id=1, source_target_pairs={{0,3},{1,0},{2,1},{3,2},{4,7},{5,4},{6,5},{7,6},{8,11},{9,8},{10,9... | collective-permute-start | bytes 589832 | tf_op jit(solution)/shard_map/ppermute | solution.py:52
  221.2 39.2 %collective-permute-start.21 = (bf16[2,2,96,1728]{3,2,0,1:T(8,128)(2,1)S(1)}, bf16[2,2,96,1728]{3,2,0,1:T(8,128)(2,1)S(1)}, u32[]{:S(2)}, u32[]{:S(2)}) collective-permute-start(bf16[2,2,96,1728]{3,2,0,1:T(8,128)(2,1)S(1)} %fusion.5), channel_id=1, source_target_pairs={{0,8},{4,12},{8,0},{12,4},{16,24},{20,28},{24,16},{28,20},{1,9},{5... | collective-permute-start | bytes 3981320 | tf_op jit(solution)/shard_map/ppermute | solution.py:48
  224.6 35.8 %collective-permute-start.22 = (bf16[2,2,96,1728]{3,2,0,1:T(8,128)(2,1)S(1)}, bf16[2,2,96,1728]{3,2,0,1:T(8,128)(2,1)S(1)}, u32[]{:S(2)}, u32[]{:S(2)}) collective-permute-start(bf16[2,2,96,1728]{3,2,0,1:T(8,128)(2,1)S(1)} %fusion.6), channel_id=1, source_target_pairs={{0,16},{4,20},{8,24},{12,28},{16,0},{20,4},{24,8},{28,12},{1,17},{... | collective-permute-start | bytes 3981320 | tf_op jit(solution)/shard_map/ppermute | solution.py:48
  224.6 35.7 %collective-permute-start.23 = (bf16[1092,128]{1,0:T(8,128)(2,1)S(1)}, bf16[1092,128]{1,0:T(8,128)(2,1)S(1)}, u32[]{:S(2)}, u32[]{:S(2)}) collective-permute-start(bf16[1092,128]{1,0:T(8,128)(2,1)S(1)} %add.210), channel_id=1, source_target_pairs={{0,2},{1,3},{2,0},{3,1},{4,6},{5,7},{6,4},{7,5},{8,10},{9,11},{10,... | collective-permute-start | bytes 838664 | tf_op jit(solution)/shard_map/ppermute | solution.py:48
  262.1 19.7 %collective-permute-start.24 = (bf16[512,768]{1,0:T(8,128)(2,1)}, bf16[512,768]{1,0:T(8,128)(2,1)}, u32[]{:S(2)}, u32[]{:S(2)}) collective-permute-start(bf16[512,768]{1,0:T(8,128)(2,1)} %first_rows.1), channel_id=1, source_target_pairs={{0,1},{1,2},{2,3},{3,0},{4,5},{5,6},{6,7},{7,4},{8,9},{9,10},{10,1... | collective-permute-start | bytes 2359304 | tf_op jit(solution)/shard_map/ppermute | solution.py:52
  269.0 16.7 %collective-permute-start.27 = (bf16[2,1,96,1728]{3,2,1,0:T(8,128)(2,1)}, bf16[2,1,96,1728]{3,2,1,0:T(8,128)(2,1)}, u32[]{:S(2)}, u32[]{:S(2)}) collective-permute-start(bf16[2,1,96,1728]{3,2,1,0:T(8,128)(2,1)} %fusion.11), channel_id=1, source_target_pairs={{0,8},{4,12},{8,0},{12,4},{16,24},{20,28},{24,16},{28,20},{1,9},{5... | collective-permute-start | bytes 1990664 | tf_op jit(solution)/shard_map/ppermute | solution.py:48
  269.1 18.0 %collective-permute-start.26 = (bf16[2,1,96,1728]{3,2,1,0:T(8,128)(2,1)}, bf16[2,1,96,1728]{3,2,1,0:T(8,128)(2,1)}, u32[]{:S(2)}, u32[]{:S(2)}) collective-permute-start(bf16[2,1,96,1728]{3,2,1,0:T(8,128)(2,1)} %fusion.10), channel_id=1, source_target_pairs={{0,16},{4,20},{8,24},{12,28},{16,0},{20,4},{24,8},{28,12},{1,17},{... | collective-permute-start | bytes 1990664 | tf_op jit(solution)/shard_map/ppermute | solution.py:48
  275.0 17.4 %collective-permute-start.28 = (bf16[1092,128]{1,0:T(8,128)(2,1)S(1)}, bf16[1092,128]{1,0:T(8,128)(2,1)S(1)}, u32[]{:S(2)}, u32[]{:S(2)}) collective-permute-start(bf16[1092,128]{1,0:T(8,128)(2,1)S(1)} %add.217), channel_id=1, source_target_pairs={{0,4},{4,0},{8,12},{12,8},{16,20},{20,16},{24,28},{28,24},{1,5},{5... | collective-permute-start | bytes 838664 | tf_op jit(solution)/shard_map/ppermute | solution.py:48
  283.2 22.3 %collective-permute-start.25 = (bf16[512,768]{1,0:T(8,128)(2,1)S(1)}, bf16[512,768]{1,0:T(8,128)(2,1)S(1)}, u32[]{:S(2)}, u32[]{:S(2)}) collective-permute-start(bf16[512,768]{1,0:T(8,128)(2,1)S(1)} %fusion.2), channel_id=1, source_target_pairs={{0,1},{1,2},{2,3},{3,0},{4,5},{5,6},{6,7},{7,4},{8,9},{9,10},{10,1... | collective-permute-start | bytes 2359304 | tf_op jit(solution)/shard_map/ppermute | solution.py:52
  288.4 24.5 %collective-permute-start.30 = (bf16[96,1728]{1,0:T(8,128)(2,1)S(1)}, bf16[96,1728]{1,0:T(8,128)(2,1)S(1)}, u32[]{:S(2)}, u32[]{:S(2)}) collective-permute-start(bf16[96,1728]{1,0:T(8,128)(2,1)S(1)} %fusion.17), channel_id=1, source_target_pairs={{0,1},{1,2},{2,3},{3,0},{4,5},{5,6},{6,7},{7,4},{8,9},{9,10},{10,1... | collective-permute-start | bytes 995336 | tf_op jit(solution)/shard_map/ppermute | solution.py:52
  292.3 14.3 %collective-permute-start.31 = (bf16[400,768]{1,0:T(8,128)(2,1)S(1)}, bf16[400,768]{1,0:T(8,128)(2,1)S(1)}, u32[]{:S(2)}, u32[]{:S(2)}) collective-permute-start(bf16[400,768]{1,0:T(8,128)(2,1)S(1)} %pad_maximum_fusion.2), channel_id=1, source_target_pairs={{0,4},{4,0},{8,12},{12,8},{16,20},{20,16},{24,28},{28,24},{1,5},{5... | collective-permute-start | bytes 1843208 | tf_op jit(solution)/shard_map/ppermute | solution.py:48
  292.5 17.0 %collective-permute-start.32 = (bf16[1092,128]{1,0:T(8,128)(2,1)S(1)}, bf16[1092,128]{1,0:T(8,128)(2,1)S(1)}, u32[]{:S(2)}, u32[]{:S(2)}) collective-permute-start(bf16[1092,128]{1,0:T(8,128)(2,1)S(1)} %add.222), channel_id=1, source_target_pairs={{0,8},{4,12},{8,0},{12,4},{16,24},{20,28},{24,16},{28,20},{1,9},{5... | collective-permute-start | bytes 838664 | tf_op jit(solution)/shard_map/ppermute | solution.py:48
  306.7 31.5 %collective-permute-start.29 = (bf16[512,768]{1,0:T(8,128)(2,1)}, bf16[512,768]{1,0:T(8,128)(2,1)S(1)}, u32[]{:S(2)}, u32[]{:S(2)}) collective-permute-start(bf16[512,768]{1,0:T(8,128)(2,1)} %fusion.3), channel_id=1, source_target_pairs={{0,1},{1,2},{2,3},{3,0},{4,5},{5,6},{6,7},{7,4},{8,9},{9,10},{10,1... | collective-permute-start | bytes 2359304 | tf_op jit(solution)/shard_map/ppermute | solution.py:52
  313.7 20.8 %collective-permute-start.33 = (bf16[96,1728]{1,0:T(8,128)(2,1)}, bf16[96,1728]{1,0:T(8,128)(2,1)}, u32[]{:S(2)}, u32[]{:S(2)}) collective-permute-start(bf16[96,1728]{1,0:T(8,128)(2,1)} %fusion.14), channel_id=1, source_target_pairs={{0,1},{1,2},{2,3},{3,0},{4,5},{5,6},{6,7},{7,4},{8,9},{9,10},{10,1... | collective-permute-start | bytes 995336 | tf_op jit(solution)/shard_map/ppermute | solution.py:52
  321.5 15.8 %collective-permute-start.37 = (f32[2,768]{1,0:T(2,128)S(1)}, f32[2,768]{1,0:T(2,128)S(1)}, u32[]{:S(2)}, u32[]{:S(2)}) collective-permute-start(f32[2,768]{1,0:T(2,128)S(1)} %convert_add_fusion.4), channel_id=1, source_target_pairs={{0,1},{1,2},{2,3},{3,0},{4,5},{5,6},{6,7},{7,4},{8,9},{9,10},{10,1... | collective-permute-start | bytes 18440 | tf_op jit(solution)/shard_map/ppermute | solution.py:52
  322.0 15.3 %collective-permute-start.38 = (f32[2,768]{1,0:T(2,128)S(1)}, f32[2,768]{1,0:T(2,128)S(1)}, u32[]{:S(2)}, u32[]{:S(2)}) collective-permute-start(f32[2,768]{1,0:T(2,128)S(1)} %convert_add_fusion.4), channel_id=1, source_target_pairs={{0,2},{1,3},{2,0},{3,1},{4,6},{5,7},{6,4},{7,5},{8,10},{9,11},{10,... | collective-permute-start | bytes 18440 | tf_op jit(solution)/shard_map/ppermute | solution.py:52
  (62 other events, 625.4 us)
Sparse Core Ops, SparseCore 0:
  25.3 41.5 all-gather.4
  69.4 43.3 all-gather.6

commit v5 on v4

--- a/solution.py
+++ b/solution.py
@@ -1034,16 +1034,39 @@
 
     extra = padded - local
     qkv_shard = jnp.pad(w_qkv, ((0, 0), (0, 0), (0, extra))).reshape(shard, 3 * padded)
-    ff_ring, seq_rows = [], []
+    ff_ring, seq_rows, shared = [], [], {}
+    q_bias = lax.dynamic_slice_in_dim(vec_table[0], z * local, local, 0)
+    v_bias = lax.dynamic_slice_in_dim(vec_table[1], z * local, local, 0)
+    in_bias = jnp.pad(
+        jnp.stack([q_bias, jnp.zeros_like(q_bias), v_bias]), ((0, 0), (0, extra))
+    ).reshape(1, 3 * padded)
+
+
+    def in_weights_chain():
+        shared["in"] = yield from gather_chain(qkv_shard, "dp", dp)
+        return shared["in"]
+
+    def project_chain():
+        done = []
+        while len(done) < tensor:
+            if "in" in shared:
+                for part in seq_rows[len(done) :]:
+                    value = jnp.dot(part, shared["in"], preferred_element_type=F32) + in_bias
+                    done.append(value.astype(BF16))
+            if len(done) < tensor:
+                yield done, ()
+        return done
+
     ff_shard = jnp.concatenate([w_up, w_down.T, w_out.T], axis=1)
-    _, _, w_in = in_turn(
+    _, _, w_in, chunks = in_turn(
         vec_table[0, 0],
         {
             "rows": ring_chain(tokens, tensor, seq_rows),
             "ff": ring_chain(ff_shard, tensor, ff_ring),
-            "in": gather_chain(qkv_shard, "dp", dp),
+            "in": in_weights_chain(),
+            "project": project_chain(),
         },
-        [("in",), ("in", "ff"), ("in",), ("ff",), ("rows",), ("ff",), ("rows",), ("rows",)],
+        [("in",)] + [("rows", "ff", "in", "project")] * 3,
     )
     half = tensor // 2
     pieces = [
@@ -1054,21 +1077,11 @@
             p.transpose(1, 0, 2, 3).reshape(1, half, dp * shard, p.shape[-1]) for p in pieces
         ]
 
-    q_bias = lax.dynamic_slice_in_dim(vec_table[0], z * local, local, 0)
-    v_bias = lax.dynamic_slice_in_dim(vec_table[1], z * local, local, 0)
-    in_bias = jnp.pad(
-        jnp.stack([q_bias, jnp.zeros_like(q_bias), v_bias]), ((0, 0), (0, extra))
-    ).reshape(1, 3 * padded)
-
     def exchanged(parts):
         return [parts[0]] + [
             shifted(parts[tensor - s], "tensor", tensor, s) for s in range(1, tensor)
         ]
 
-    chunks = [
-        (jnp.dot(part, w_in, preferred_element_type=F32) + in_bias).astype(BF16)
-        for part in seq_rows
-    ]
     mixed, lse = attend_forward(info, chunks, heads)
     mixed_parts = exchanged(mixed)
     kept = rows_forward(

time: 359 us -> 353 us (0.983)
  waiting for transfers between devices: 145 us -> 129 us
  starting transfers between devices: 43.1 us -> 47 us
    ppermute x17, waiting for transfers between devices: 23.1 us -> 6.6 us  [swapped(): return lax.ppermute(value, axis, [(i, i ^ bit) for i in range(size)])]
    ppermute x24, starting transfers between devices: 22.6 us -> 30 us  [shifted(): lax.ppermute(value, axis, [(i, (i + by) % size) for i in range(size)])]
    ppermute x17, starting transfers between devices: 20.5 us -> 16.8 us  [swapped(): return lax.ppermute(value, axis, [(i, i ^ bit) for i in range(size)])]
    unnamed x93 -> x83, local copies, waits for them, and re-layouts: 10.1 us -> 11.2 us
  transfers between devices with their start and end apart: 43 -> 43, of which waited for: 24 -> 17; matrix products, arithmetic and copies ran while one was open for 9% -> 11% of each run, Pallas kernels for 19% -> 20%
where the time goes in v5:
time: 353 us; the launch traced here: 347 us
  waiting for transfers between devices  129 us (37%)
  Pallas kernels  109 us (31%)
  starting transfers between devices  47 us (13%)
  local copies, waits for them, and re-layouts  21.4 us (6%)
  other arithmetic  20.3 us (6%)
  between operations  15.6 us (4%)
  matrix products  5.83 us (2%)
    ppermute x24, waiting for transfers between devices, shifted(): lax.ppermute(value, axis, [(i, (i + by) % size) for i in range(size)])  122 us
    pallas_call x1, Pallas kernels, attend_backward(): pl.pallas_call(functools.partial(attend_backward_kernel, heads), out_shap...  31.2 us
    ppermute x24, starting transfers between devices, shifted(): lax.ppermute(value, axis, [(i, (i + by) % size) for i in range(size)])  30 us
    pallas_call x1, Pallas kernels, attend_forward(): pl.pallas_call(functools.partial(attend_forward_kernel, heads), out_shape...  21.8 us
    pallas_call x1, Pallas kernels, rows_forward(): pl.pallas_call(functools.partial(rows_forward_kernel, tensor, len(pieces)...  20.5 us
    ppermute x17, starting transfers between devices, swapped(): return lax.ppermute(value, axis, [(i, i ^ bit) for i in range(size)])  16.8 us
    pallas_call x1, Pallas kernels, rows_backward(): pl.pallas_call(functools.partial(rows_backward_kernel, tensor, len(pieces...  16.3 us
    unnamed x83, local copies, waits for them, and re-layouts  11.2 us
  transfers between devices with their start and end apart: 43, of which 17 were waited for; matrix products, arithmetic and copies ran while one was open for 11% of the time, Pallas kernels for 20%

profile of v5, /device:TPU:0, one launch (start us, length us, event | category | flops | bytes accessed | tf_op | source)
XLA Modules:
  0.0 347.3 jit_solution(8050150172992363899)
XLA Ops:
  7.2 3.1 collective-permute-start.1
  16.7 20.7 %collective-permute-done.2 = bf16[96,1728]{1,0:T(8,128)(2,1)S(1)} collective-permute-done((bf16[96,1728]{1,0:T(8,128)(2,1)S(1)}, bf16[96,1728]{1,0:T(8,128)(2,1)S(1)}, u32[]{:S(2)}, u32[]{:S(2)}) %collective-permute-start.2) | collective-permute-done | bytes 331808 | tf_op jit(solution)/shard_map/ppermute | solution.py:52
  42.7 23.9 %collective-permute-done.5 = bf16[96,1728]{1,0:T(8,128)(2,1)} collective-permute-done((bf16[96,1728]{1,0:T(8,128)(2,1)S(1)}, bf16[96,1728]{1,0:T(8,128)(2,1)}, u32[]{:S(2)}, u32[]{:S(2)}) %collective-permute-start.5) | collective-permute-done | bytes 331808 | tf_op jit(solution)/shard_map/ppermute | solution.py:52
  71.8 22.0 %collective-permute-done.8 = bf16[96,1728]{1,0:T(8,128)(2,1)S(1)} collective-permute-done((bf16[96,1728]{1,0:T(8,128)(2,1)}, bf16[96,1728]{1,0:T(8,128)(2,1)S(1)}, u32[]{:S(2)}, u32[]{:S(2)}) %collective-permute-start.8) | collective-permute-done | bytes 331808 | tf_op jit(solution)/shard_map/ppermute | solution.py:52
  98.4 21.8 %attend_forward.1 = (bf16[4,512,192]{2,1,0:T(8,128)(2,1)S(1)}, f32[8,8,256]{2,1,0:T(8,128)S(1)}) custom-call(s32[7]{0:T(128)S(1)} %concatenate.39.info_ref, bf16[512,768]{1,0:T(8,128)(2,1)S(1)} %fusion.9.refs_0_, bf16[512,768]{1,0:T(8,128)(2,1)S(1)} %add_convert_fusion.4.refs_1_, bf16[512,768]{1,0:T(8,128)(2,1)S(1)} %add_convert_fusion.3.refs_2_, ...), custom_call_target="tpu_custom_call" | custom-call | flops 1024 | bytes 1024 | tf_op jit(solution)/shard_map/attend_forward/pallas_call | solution.py:246
  124.1 15.1 %collective-permute-done.10.refs_2_ = bf16[512,192]{1,0:T(8,128)(2,1)S(1)} collective-permute-done((bf16[512,192]{1,0:T(8,128)(2,1)S(1)}, bf16[512,192]{1,0:T(8,128)(2,1)S(1)}, u32[]{:S(2)}, u32[]{:S(2)}) %collective-permute-start.10) | collective-permute-done | bytes 196640 | tf_op jit(solution)/shard_map/ppermute | solution.py:52
  140.1 20.5 %rows_forward.1 = (bf16[512,768]{1,0:T(8,128)(2,1)}, bf16[512,768]{1,0:T(8,128)(2,1)}, bf16[4,512,768]{2,1,0:T(8,128)(2,1)}, bf16[4,512,768]{2,1,0:T(8,128)(2,1)...) custom-call(s32[7]{0:T(128)S(1)} %concatenate.39.info_ref, ...), custom_call_target="tpu_custom_call" | custom-call | flops 1024 | bytes 1024 | tf_op jit(solution)/shard_map/rows_forward/pallas_call | solution.py:534
  160.6 3.3 collective-permute-start.12
  163.9 2.8 collective-permute-start.14
  168.4 16.3 %rows_backward.1 = (f32[8,128]{1,0:T(8,128)S(1)}, bf16[512,768]{1,0:T(8,128)(2,1)S(1)}, bf16[4,512,768]{2,1,0:T(8,128)(2,1)S(1)}, bf16[512,768]{1,0:T(8,128)(2,1...) custom-call(s32[7]{0:T(128)S(1)} %concatenate.39.info_ref, ...), custom_call_target="tpu_custom_call" | custom-call | flops 1024 | bytes 1024 | tf_op jit(solution)/shard_map/rows_backward/pallas_call | solution.py:739
  187.6 9.9 %weight_grads.1 = (bf16[2,4,96,1728]{3,2,1,0:T(8,128)(2,1)S(1)}, bf16[2,4,96,1728]{3,2,1,0:T(8,128)(2,1)S(1)}, bf16[2,4,96,1728]{3,2,1,0:T(8,128)(2,1)S(1)}, bf16[2,4,96,1728]{3,2,1,0:T(8,128)(2,1)S(1)}) custom-call(s32[7]{0:T(128)S(1)} %concatenate.39.info_ref, bf16[512,768]{1,0:T(8,128)(2,1)} %get-tuple-element.114.x_ref, ...), custom_call_target="tpu_custom_call" | custom-call | flops 1024 | bytes 1024 | tf_op jit(solution)/shard_map/weight_grads/pallas_call | solution.py:857
  200.6 2.7 collective-permute-start.20
  204.1 2.6 collective-permute-done.17
  207.1 6.8 %collective-permute-done.19.refs_6_ = bf16[512,192]{1,0:T(8,128)(2,1)S(1)} collective-permute-done((bf16[512,192]{1,0:T(8,128)(2,1)S(1)}, bf16[512,192]{1,0:T(8,128)(2,1)S(1)}, u32[]{:S(2)}, u32[]{:S(2)}) %collective-permute-start.19) | collective-permute-done | bytes 196640 | tf_op jit(solution)/shard_map/ppermute | solution.py:52
  216.3 4.2 %collective-permute-start.23 = (bf16[1092,128]{1,0:T(8,128)(2,1)S(1)}, bf16[1092,128]{1,0:T(8,128)(2,1)S(1)}, u32[]{:S(2)}, u32[]{:S(2)}) collective-permute-start(bf16[1092,128]{1,0:T(8,128)(2,1)S(1)} %add.210), channel_id=1, source_target_pairs={{0,2},{1,3},{2,0},{3,1},{4,6},{5,7},{6,4},{7,5},{8,10},{9,11},{10,... | collective-permute-start | bytes 838664 | tf_op jit(solution)/shard_map/ppermute | solution.py:48
  220.5 31.2 %attend_backward.1 = (bf16[4,512,768]{2,1,0:T(8,128)(2,1)S(1)}, f32[8,256]{1,0:T(8,128)S(1)}) custom-call(s32[7]{0:T(128)S(1)} %concatenate.39.info_ref, bf16[512,768]{1,0:T(8,128)(2,1)} %copy-done.7, bf16[512,768]{1,0:T(8,128)(2,1)} %copy-done.6, bf16[512,768]{1,0:T(8,128)(2,1)} %copy-done.5, bf16[512,768]{1,0:T(8,128)(2,1)} %copy-done.8, ...), custom_call_target="tpu_custom_call" | custom-call | flops 1024 | bytes 1024 | tf_op jit(solution)/shard_map/attend_backward/pallas_call | solution.py:380
  253.5 3.6 %collective-permute-start.24 = (bf16[512,768]{1,0:T(8,128)(2,1)}, bf16[512,768]{1,0:T(8,128)(2,1)}, u32[]{:S(2)}, u32[]{:S(2)}) collective-permute-start(bf16[512,768]{1,0:T(8,128)(2,1)} %first_rows.1), channel_id=1, source_target_pairs={{0,1},{1,2},{2,3},{3,0},{4,5},{5,6},{6,7},{7,4},{8,9},{9,10},{10,1... | collective-permute-start | bytes 2359304 | tf_op jit(solution)/shard_map/ppermute | solution.py:52
  261.0 3.7 %collective-permute-start.26 = (bf16[2,1,96,1728]{3,2,1,0:T(8,128)(2,1)}, bf16[2,1,96,1728]{3,2,1,0:T(8,128)(2,1)}, u32[]{:S(2)}, u32[]{:S(2)}) collective-permute-start(bf16[2,1,96,1728]{3,2,1,0:T(8,128)(2,1)} %fusion.10), channel_id=1, source_target_pairs={{0,16},{4,20},{8,24},{12,28},{16,0},{20,4},{24,8},{28,12},{1,17},{... | collective-permute-start | bytes 1990664 | tf_op jit(solution)/shard_map/ppermute | solution.py:48
  278.8 4.8 %in_grad.1 = f32[768,768]{1,0:T(8,128)S(1)} custom-call(bf16[4,512,768]{2,1,0:T(8,128)(2,1)S(1)} %get-tuple-element.157.d_ref, bf16[512,768]{1,0:T(8,128)(2,1)S(1)} %copy-done.12, bf16[512,768]{1,0:T(8,128)(2,1)S(1)} %copy-done.20, bf16[512,768]{1,0:T(8,128)(2,1)} %collective-permute-done.4.refs_2_, bf16[512,768]{1,0:T(8,128)(2,1)} %collective-permute-done.7.refs_3_), custom_call_target="tpu_custom_call" | custom-call | flops 40000000000 | bytes 1024 | tf_op jit(solution)/shard_map/in_grad/pallas_call | solution.py:1007
  286.7 8.9 %collective-permute-done.25 = bf16[512,768]{1,0:T(8,128)(2,1)S(1)} collective-permute-done((bf16[512,768]{1,0:T(8,128)(2,1)S(1)}, bf16[512,768]{1,0:T(8,128)(2,1)S(1)}, u32[]{:S(2)}, u32[]{:S(2)}) %collective-permute-start.25) | collective-permute-done | bytes 786464 | tf_op jit(solution)/shard_map/ppermute | solution.py:52
  298.6 4.4 %collective-permute-done.30 = bf16[96,1728]{1,0:T(8,128)(2,1)S(1)} collective-permute-done((bf16[96,1728]{1,0:T(8,128)(2,1)S(1)}, bf16[96,1728]{1,0:T(8,128)(2,1)S(1)}, u32[]{:S(2)}, u32[]{:S(2)}) %collective-permute-start.30) | collective-permute-done | bytes 331808 | tf_op jit(solution)/shard_map/ppermute | solution.py:52
  311.0 4.1 %collective-permute-start.38 = (f32[2,768]{1,0:T(2,128)S(1)}, f32[2,768]{1,0:T(2,128)S(1)}, u32[]{:S(2)}, u32[]{:S(2)}) collective-permute-start(f32[2,768]{1,0:T(2,128)S(1)} %convert_add_fusion.4), channel_id=1, source_target_pairs={{0,2},{1,3},{2,0},{3,1},{4,6},{5,7},{6,4},{7,5},{8,10},{9,11},{10,... | collective-permute-start | bytes 18440 | tf_op jit(solution)/shard_map/ppermute | solution.py:52
  315.1 10.7 %collective-permute-done.33 = bf16[96,1728]{1,0:T(8,128)(2,1)} collective-permute-done((bf16[96,1728]{1,0:T(8,128)(2,1)}, bf16[96,1728]{1,0:T(8,128)(2,1)}, u32[]{:S(2)}, u32[]{:S(2)}) %collective-permute-start.33) | collective-permute-done | bytes 331808 | tf_op jit(solution)/shard_map/ppermute | solution.py:52
  332.0 5.8 %collective-permute-done.36 = bf16[96,1728]{1,0:T(8,128)(2,1)} collective-permute-done((bf16[96,1728]{1,0:T(8,128)(2,1)}, bf16[96,1728]{1,0:T(8,128)(2,1)}, u32[]{:S(2)}, u32[]{:S(2)}) %collective-permute-start.36) | collective-permute-done | bytes 331808 | tf_op jit(solution)/shard_map/ppermute | solution.py:52
  (237 shorter events, 78.8 us)
Async XLA Ops:
  7.2 132.0 %all-gather.5.cloned.1.call-start = ((), (), s32[]{:S(2)}) async-start(), calls=%async_computation | async-start | bytes 6193152 | tf_op jit(solution)/shard_map/all_gather | solution.py:1073
  7.2 30.2 %collective-permute-start.1 = (bf16[512,768]{1,0:T(8,128)(2,1)}, bf16[512,768]{1,0:T(8,128)(2,1)S(1)}, u32[]{:S(2)}, u32[]{:S(2)}) collective-permute-start(bf16[512,768]{1,0:T(8,128)(2,1)} %refs_0_.1), channel_id=1, source_target_pairs={{0,1},{1,2},{2,3},{3,0},{4,5},{5,6},{6,7},{7,4},{8,9},{9,10},{10,1... | collective-permute-start | bytes 2359304 | tf_op jit(solution)/shard_map/ppermute | solution.py:52
  13.5 24.0 %collective-permute-start.2 = (bf16[96,1728]{1,0:T(8,128)(2,1)S(1)}, bf16[96,1728]{1,0:T(8,128)(2,1)S(1)}, u32[]{:S(2)}, u32[]{:S(2)}) collective-permute-start(bf16[96,1728]{1,0:T(8,128)(2,1)S(1)} %get-tuple-element.231), channel_id=1, source_target_pairs={{0,1},{1,2},{2,3},{3,0},{4,5},{5,6},{6,7},{7,4},{8,9},{9,10},{10,1... | collective-permute-start | bytes 995336 | tf_op jit(solution)/shard_map/ppermute | solution.py:52
  15.2 22.3 %collective-permute-start.3 = (bf16[192,768]{1,0:T(8,128)(2,1)S(1)}, bf16[192,768]{1,0:T(8,128)(2,1)S(1)}, u32[]{:S(2)}, u32[]{:S(2)}) collective-permute-start(bf16[192,768]{1,0:T(8,128)(2,1)S(1)} %maximum_select_fusion.2), channel_id=1, source_target_pairs={{0,8},{4,12},{8,0},{12,4},{16,24},{20,28},{24,16},{28,20},{1,9},{5... | collective-permute-start | bytes 884744 | tf_op jit(solution)/shard_map/ppermute | solution.py:48
  38.5 100.7 %all-gather.7.cloned.1.call-start = ((), (), s32[]{:S(2)}) async-start(), calls=%async_computation.1 | async-start | bytes 6193152 | tf_op jit(solution)/shard_map/all_gather | solution.py:1073
  38.5 28.1 %collective-permute-start.4 = (bf16[512,768]{1,0:T(8,128)(2,1)S(1)}, bf16[512,768]{1,0:T(8,128)(2,1)}, u32[]{:S(2)}, u32[]{:S(2)}) collective-permute-start(bf16[512,768]{1,0:T(8,128)(2,1)S(1)} %collective-permute-done.1.refs_1_), channel_id=1, source_target_pairs={{0,1},{1,2},{2,3},{3,0},{4,5},{5,6},{6,7},{7,4},{8,9},{9,10},{10,1... | collective-permute-start | bytes 2359304 | tf_op jit(solution)/shard_map/ppermute | solution.py:52
  38.8 27.8 %collective-permute-start.6 = (bf16[384,768]{1,0:T(8,128)(2,1)S(1)}, bf16[384,768]{1,0:T(8,128)(2,1)S(1)}, u32[]{:S(2)}, u32[]{:S(2)}) collective-permute-start(bf16[384,768]{1,0:T(8,128)(2,1)S(1)} %maximum_select_fusion.1), channel_id=1, source_target_pairs={{0,16},{4,20},{8,24},{12,28},{16,0},{20,4},{24,8},{28,12},{1,17},{... | collective-permute-start | bytes 1769480 | tf_op jit(solution)/shard_map/ppermute | solution.py:48
  41.3 25.3 %collective-permute-start.5 = (bf16[96,1728]{1,0:T(8,128)(2,1)S(1)}, bf16[96,1728]{1,0:T(8,128)(2,1)}, u32[]{:S(2)}, u32[]{:S(2)}) collective-permute-start(bf16[96,1728]{1,0:T(8,128)(2,1)S(1)} %collective-permute-done.2), channel_id=1, source_target_pairs={{0,1},{1,2},{2,3},{3,0},{4,5},{5,6},{6,7},{7,4},{8,9},{9,10},{10,1... | collective-permute-start | bytes 995336 | tf_op jit(solution)/shard_map/ppermute | solution.py:52
  66.6 27.2 %collective-permute-start.7 = (bf16[512,768]{1,0:T(8,128)(2,1)}, bf16[512,768]{1,0:T(8,128)(2,1)}, u32[]{:S(2)}, u32[]{:S(2)}) collective-permute-start(bf16[512,768]{1,0:T(8,128)(2,1)} %collective-permute-done.4.refs_2_), channel_id=1, source_target_pairs={{0,1},{1,2},{2,3},{3,0},{4,5},{5,6},{6,7},{7,4},{8,9},{9,10},{10,1... | collective-permute-start | bytes 2359304 | tf_op jit(solution)/shard_map/ppermute | solution.py:52
  66.6 27.2 %collective-permute-start.8 = (bf16[96,1728]{1,0:T(8,128)(2,1)}, bf16[96,1728]{1,0:T(8,128)(2,1)S(1)}, u32[]{:S(2)}, u32[]{:S(2)}) collective-permute-start(bf16[96,1728]{1,0:T(8,128)(2,1)} %collective-permute-done.5), channel_id=1, source_target_pairs={{0,1},{1,2},{2,3},{3,0},{4,5},{5,6},{6,7},{7,4},{8,9},{9,10},{10,1... | collective-permute-start | bytes 995336 | tf_op jit(solution)/shard_map/ppermute | solution.py:52
  122.1 17.1 %collective-permute-start.10 = (bf16[512,192]{1,0:T(8,128)(2,1)S(1)}, bf16[512,192]{1,0:T(8,128)(2,1)S(1)}, u32[]{:S(2)}, u32[]{:S(2)}) collective-permute-start(bf16[512,192]{1,0:T(8,128)(2,1)S(1)} %get-tuple-element.225), channel_id=1, source_target_pairs={{0,2},{1,3},{2,0},{3,1},{4,6},{5,7},{6,4},{7,5},{8,10},{9,11},{10,... | collective-permute-start | bytes 589832 | tf_op jit(solution)/shard_map/ppermute | solution.py:52
  122.1 17.1 %collective-permute-start.11 = (bf16[512,192]{1,0:T(8,128)(2,1)S(1)}, bf16[512,192]{1,0:T(8,128)(2,1)S(1)}, u32[]{:S(2)}, u32[]{:S(2)}) collective-permute-start(bf16[512,192]{1,0:T(8,128)(2,1)S(1)} %get-tuple-element.224), channel_id=1, source_target_pairs={{0,3},{1,0},{2,1},{3,2},{4,7},{5,4},{6,5},{7,6},{8,11},{9,8},{10,9... | collective-permute-start | bytes 589832 | tf_op jit(solution)/shard_map/ppermute | solution.py:52
  122.9 16.3 %collective-permute-start.9 = (bf16[512,192]{1,0:T(8,128)(2,1)S(1)}, bf16[512,192]{1,0:T(8,128)(2,1)S(1)}, u32[]{:S(2)}, u32[]{:S(2)}) collective-permute-start(bf16[512,192]{1,0:T(8,128)(2,1)S(1)} %get-tuple-element.226), channel_id=1, source_target_pairs={{0,1},{1,2},{2,3},{3,0},{4,5},{5,6},{6,7},{7,4},{8,9},{9,10},{10,1... | collective-permute-start | bytes 589832 | tf_op jit(solution)/shard_map/ppermute | solution.py:52
  213.9 37.8 %collective-permute-start.21 = (bf16[2,2,96,1728]{3,2,0,1:T(8,128)(2,1)S(1)}, bf16[2,2,96,1728]{3,2,0,1:T(8,128)(2,1)S(1)}, u32[]{:S(2)}, u32[]{:S(2)}) collective-permute-start(bf16[2,2,96,1728]{3,2,0,1:T(8,128)(2,1)S(1)} %fusion.5), channel_id=1, source_target_pairs={{0,8},{4,12},{8,0},{12,4},{16,24},{20,28},{24,16},{28,20},{1,9},{5... | collective-permute-start | bytes 3981320 | tf_op jit(solution)/shard_map/ppermute | solution.py:48
  215.5 36.2 %collective-permute-start.22 = (bf16[2,2,96,1728]{3,2,0,1:T(8,128)(2,1)S(1)}, bf16[2,2,96,1728]{3,2,0,1:T(8,128)(2,1)S(1)}, u32[]{:S(2)}, u32[]{:S(2)}) collective-permute-start(bf16[2,2,96,1728]{3,2,0,1:T(8,128)(2,1)S(1)} %fusion.6), channel_id=1, source_target_pairs={{0,16},{4,20},{8,24},{12,28},{16,0},{20,4},{24,8},{28,12},{1,17},{... | collective-permute-start | bytes 3981320 | tf_op jit(solution)/shard_map/ppermute | solution.py:48
  216.3 35.5 %collective-permute-start.23 = (bf16[1092,128]{1,0:T(8,128)(2,1)S(1)}, bf16[1092,128]{1,0:T(8,128)(2,1)S(1)}, u32[]{:S(2)}, u32[]{:S(2)}) collective-permute-start(bf16[1092,128]{1,0:T(8,128)(2,1)S(1)} %add.210), channel_id=1, source_target_pairs={{0,2},{1,3},{2,0},{3,1},{4,6},{5,7},{6,4},{7,5},{8,10},{9,11},{10,... | collective-permute-start | bytes 838664 | tf_op jit(solution)/shard_map/ppermute | solution.py:48
  253.5 18.4 %collective-permute-start.24 = (bf16[512,768]{1,0:T(8,128)(2,1)}, bf16[512,768]{1,0:T(8,128)(2,1)}, u32[]{:S(2)}, u32[]{:S(2)}) collective-permute-start(bf16[512,768]{1,0:T(8,128)(2,1)} %first_rows.1), channel_id=1, source_target_pairs={{0,1},{1,2},{2,3},{3,0},{4,5},{5,6},{6,7},{7,4},{8,9},{9,10},{10,1... | collective-permute-start | bytes 2359304 | tf_op jit(solution)/shard_map/ppermute | solution.py:52
  266.3 17.5 %collective-permute-start.28 = (bf16[1092,128]{1,0:T(8,128)(2,1)S(1)}, bf16[1092,128]{1,0:T(8,128)(2,1)S(1)}, u32[]{:S(2)}, u32[]{:S(2)}) collective-permute-start(bf16[1092,128]{1,0:T(8,128)(2,1)S(1)} %add.217), channel_id=1, source_target_pairs={{0,4},{4,0},{8,12},{12,8},{16,20},{20,16},{24,28},{28,24},{1,5},{5... | collective-permute-start | bytes 838664 | tf_op jit(solution)/shard_map/ppermute | solution.py:48
  273.2 22.3 %collective-permute-start.25 = (bf16[512,768]{1,0:T(8,128)(2,1)S(1)}, bf16[512,768]{1,0:T(8,128)(2,1)S(1)}, u32[]{:S(2)}, u32[]{:S(2)}) collective-permute-start(bf16[512,768]{1,0:T(8,128)(2,1)S(1)} %fusion.2), channel_id=1, source_target_pairs={{0,1},{1,2},{2,3},{3,0},{4,5},{5,6},{6,7},{7,4},{8,9},{9,10},{10,1... | collective-permute-start | bytes 2359304 | tf_op jit(solution)/shard_map/ppermute | solution.py:52
  278.5 24.4 %collective-permute-start.30 = (bf16[96,1728]{1,0:T(8,128)(2,1)S(1)}, bf16[96,1728]{1,0:T(8,128)(2,1)S(1)}, u32[]{:S(2)}, u32[]{:S(2)}) collective-permute-start(bf16[96,1728]{1,0:T(8,128)(2,1)S(1)} %fusion.17), channel_id=1, source_target_pairs={{0,1},{1,2},{2,3},{3,0},{4,5},{5,6},{6,7},{7,4},{8,9},{9,10},{10,1... | collective-permute-start | bytes 995336 | tf_op jit(solution)/shard_map/ppermute | solution.py:52
  296.7 32.7 %collective-permute-start.29 = (bf16[512,768]{1,0:T(8,128)(2,1)}, bf16[512,768]{1,0:T(8,128)(2,1)S(1)}, u32[]{:S(2)}, u32[]{:S(2)}) collective-permute-start(bf16[512,768]{1,0:T(8,128)(2,1)} %fusion.3), channel_id=1, source_target_pairs={{0,1},{1,2},{2,3},{3,0},{4,5},{5,6},{6,7},{7,4},{8,9},{9,10},{10,1... | collective-permute-start | bytes 2359304 | tf_op jit(solution)/shard_map/ppermute | solution.py:52
  303.8 22.0 %collective-permute-start.33 = (bf16[96,1728]{1,0:T(8,128)(2,1)}, bf16[96,1728]{1,0:T(8,128)(2,1)}, u32[]{:S(2)}, u32[]{:S(2)}) collective-permute-start(bf16[96,1728]{1,0:T(8,128)(2,1)} %fusion.14), channel_id=1, source_target_pairs={{0,1},{1,2},{2,3},{3,0},{4,5},{5,6},{6,7},{7,4},{8,9},{9,10},{10,1... | collective-permute-start | bytes 995336 | tf_op jit(solution)/shard_map/ppermute | solution.py:52
  311.0 17.6 %collective-permute-start.37 = (f32[2,768]{1,0:T(2,128)S(1)}, f32[2,768]{1,0:T(2,128)S(1)}, u32[]{:S(2)}, u32[]{:S(2)}) collective-permute-start(f32[2,768]{1,0:T(2,128)S(1)} %convert_add_fusion.4), channel_id=1, source_target_pairs={{0,1},{1,2},{2,3},{3,0},{4,5},{5,6},{6,7},{7,4},{8,9},{9,10},{10,1... | collective-permute-start | bytes 18440 | tf_op jit(solution)/shard_map/ppermute | solution.py:52
  311.0 17.5 %collective-permute-start.38 = (f32[2,768]{1,0:T(2,128)S(1)}, f32[2,768]{1,0:T(2,128)S(1)}, u32[]{:S(2)}, u32[]{:S(2)}) collective-permute-start(f32[2,768]{1,0:T(2,128)S(1)} %convert_add_fusion.4), channel_id=1, source_target_pairs={{0,2},{1,3},{2,0},{3,1},{4,6},{5,7},{6,4},{7,5},{8,10},{9,11},{10,... | collective-permute-start | bytes 18440 | tf_op jit(solution)/shard_map/ppermute | solution.py:52
  (57 other events, 692.6 us)
Sparse Core Ops, SparseCore 0:
  38.6 47.0 all-gather.4
  95.8 39.9 all-gather.6
